TPU v7x, 256 devices: a whole 4x4x8 slice. The times are simulated.
256 devices in a mesh: axial: 16 (over z, core), circ: 16 (over x, y).
Axes of the slice: x: 4, y: 4, z: 8, core: 2. Of those that a mesh axis runs over, the one named last changes fastest.
Arguments:
- right_side: float32 [128, 256, 256], P('axial', 'circ'), may hold values from -6 to 6
- stiffness: float32 [128, 256, 256], P('axial', 'circ'), may hold values from 0.03 to 0.3
- material: int32 [128, 256, 256], P('axial', 'circ'), may hold values from 0 to 15
- groups: int32 [128, 256, 256], P('axial', 'circ'), may hold values from 0 to 7, as said below
Outputs:
- solution: float32 [128, 256, 256], P('axial', 'circ')
- residual: float32 [128, 256, 256], P('axial', 'circ')
Inputs may be any that keep to these rules, and one draw needn't show every extreme that they name: `groups`: in every column of cells along the third dimension every group number from 0 to 7 occurs.
All inputs are finite; a program needn't handle non-finite values.
Results may differ from a plain program's by a relative error of at most 0.0003.
Values sent between devices are 32-bit elements; how exact they have to be, the bound alone decides.
No kernel may reach another device: no remote copies, remote signals or barrier semaphores. Data moves between devices by JAX's collectives and lax.ppermute only.
A program may use at most 128 MiB of HBM per device.

v0:
```python
import functools
import math

import jax
import jax.numpy as jnp
import numpy as np
from jax import lax
from jax.sharding import Mesh
from jax.sharding import PartitionSpec as P

LABELS = 8
CLASSES = 16
ITERS = 2
CIRC = ("circ_0", "circ_1")
AXIAL = ("axial_0", "axial_1")
AXIAL_CIRC = ("axial_0", "axial_1", "circ_0", "circ_1")


MASS_SHIFT = 0.02
PRECISE = lax.Precision.HIGHEST
HALF_STEPS = (
    (0, 0, 1),
    (0, 1, -1),
    (0, 1, 0),
    (0, 1, 1),
    (1, -1, -1),
    (1, -1, 0),
    (1, -1, 1),
    (1, 0, -1),
    (1, 0, 0),
    (1, 0, 1),
    (1, 1, -1),
    (1, 1, 0),
    (1, 1, 1),
)


def with_halo(array, sides, width, wrap):
    for axis, dim in sides:
        peers, length = (lax.axis_size(axis), array.shape[dim])
        up = [(i, (i + 1) % peers) for i in range(peers if wrap else peers - 1)]
        down = [(j, i) for i, j in up]
        last = lax.slice_in_dim(array, length - width, length, axis=dim)
        first = lax.slice_in_dim(array, 0, width, axis=dim)
        before = lax.ppermute(last, axis, up)
        after = lax.ppermute(first, axis, down)
        array = jnp.concatenate([before, array, after], axis=dim)
    return array


def copy_for_each(array, axis):
    copies = jnp.broadcast_to(array, (lax.axis_size(axis), *array.shape))
    return lax.all_to_all(copies, axis, split_axis=0, concat_axis=0, tiled=True)


def in_order(parts, dim):
    shape = list(parts.shape[1:])
    shape[dim] *= parts.shape[0]
    return jnp.moveaxis(parts, 0, dim).reshape(shape)


def collect(array, axis, dim):
    parts = copy_for_each(array, axis)
    return in_order(parts, dim)


def gather_in_order(array, axes, turns):
    parts = array[None]
    for k in turns:
        parts = lax.all_gather(parts, axes[k], axis=0, tiled=True)
    held = [lax.axis_size(axes[k]) for k in reversed(turns)]
    parts = parts.reshape(*held, *array.shape)
    turned = sorted(range(len(turns)), key=lambda place: turns[len(turns) - 1 - place])
    return parts.transpose(*turned, *range(len(turns), parts.ndim)).reshape(-1, *array.shape)


def gather_axes(array, axes, turns, dim):
    return in_order(gather_in_order(array, axes, turns), dim)


def over_axes(array, axes):
    return functools.reduce(lax.psum, axes, array)


def coefficient_table():
    rows_out = []
    for material_id in range(CLASSES):
        fiber_angle = math.pi * (material_id % 8) / 8.0
        if material_id < 8:
            fiber_dir = (math.cos(fiber_angle), math.sin(fiber_angle), 0.0)
            strength, anisotropy = (1.0, 6.0)
        else:
            fiber_dir = (0.6 * math.cos(fiber_angle), 0.6 * math.sin(fiber_angle), 0.8)
            strength, anisotropy = (0.35, 2.0)
        line_values = []
        for offset in HALF_STEPS:
            length_sq = float(offset[0] * offset[0] + offset[1] * offset[1] + offset[2] * offset[2])
            along_fiber = (
                fiber_dir[0] * offset[0] + fiber_dir[1] * offset[1] + fiber_dir[2] * offset[2]
            )
            line_values.append(
                strength * (0.15 + anisotropy * along_fiber * along_fiber / length_sq) / length_sq
            )
        rows_out.append(line_values)
    return np.array(rows_out, dtype=np.float32)


def shift_radial(values_in, amount):
    if amount == 0:
        return values_in
    blank_edge = jnp.zeros(values_in.shape[:-1] + (1,), values_in.dtype)
    if amount > 0:
        return jnp.concatenate([values_in[..., 1:], blank_edge], axis=-1)
    return jnp.concatenate([blank_edge, values_in[..., :-1]], axis=-1)


def neighbour(padded, move_axial, move_circ, move_radial):
    rows_axial = padded.shape[-3] - 2
    rows_circ = padded.shape[-2] - 2
    window = padded[
        ...,
        1 + move_axial : 1 + move_axial + rows_axial,
        1 + move_circ : 1 + move_circ + rows_circ,
        :,
    ]
    return shift_radial(window, move_radial)


def extend_field(field):
    widened = with_halo(field, ((CIRC, 1),), 1, True)
    return with_halo(widened, ((AXIAL, 0),), 1, False)


def extend_labels(labels):
    widened = with_halo(labels, ((CIRC, 2),), 1, True)
    return with_halo(widened, ((AXIAL, 1),), 1, False)


def class_onehot(labels, class_count):
    levels = jnp.arange(class_count, dtype=jnp.int32).reshape((class_count,) + (1,) * labels.ndim)
    return (labels[None] == levels).astype(jnp.float32)


def edge_weights(stiff_pad, class_pad):
    looked_up = jnp.einsum(
        "mxyr,mj->jxyr",
        class_onehot(class_pad, CLASSES),
        jnp.asarray(coefficient_table()),
        precision=PRECISE,
    )
    coefficient = stiff_pad[None] * looked_up
    weights = []
    diagonal = None
    for position, offset in enumerate(HALF_STEPS):
        centre = coefficient[position, 1:-1, 1:-1]
        forward_weight = 0.5 * (
            centre + neighbour(coefficient[position], offset[0], offset[1], offset[2])
        )
        backward_weight = 0.5 * (
            centre + neighbour(coefficient[position], -offset[0], -offset[1], -offset[2])
        )
        weights.append((forward_weight, backward_weight))
        pair_sum = forward_weight + backward_weight
        diagonal = pair_sum if diagonal is None else diagonal + pair_sum
    return (weights, MASS_SHIFT + diagonal)


def stencil_apply(padded, weights, diagonal):
    result = diagonal * padded[1:-1, 1:-1]
    for position, offset in enumerate(HALF_STEPS):
        forward_weight, backward_weight = weights[position]
        result = result - forward_weight * neighbour(padded, offset[0], offset[1], offset[2])
        result = result - backward_weight * neighbour(padded, -offset[0], -offset[1], -offset[2])
    return result


def coarse_panels(weights, diagonal, own_onehot, halo_onehot):
    stencil_terms = [((0, 0, 0), diagonal)]
    for position, offset in enumerate(HALF_STEPS):
        forward_weight, backward_weight = weights[position]
        stencil_terms.append((offset, -forward_weight))
        stencil_terms.append(((-offset[0], -offset[1], -offset[2]), -backward_weight))
    reached = None
    for offset, entry_value in stencil_terms:
        portion = shift_radial(own_onehot * entry_value[None], -offset[2])
        placed = jnp.pad(
            portion,
            ((0, 0), (1 + offset[0], 1 - offset[0]), (1 + offset[1], 1 - offset[1]), (0, 0)),
        )
        reached = placed if reached is None else reached + placed
    rows_axial = own_onehot.shape[1]
    rows_circ = own_onehot.shape[2]
    axial_parts = ((1, rows_axial + 1), (rows_axial + 1, rows_axial + 2))
    circ_parts = ((0, 1), (1, rows_circ + 1), (rows_circ + 1, rows_circ + 2))
    panel_rows = []
    for axial_start, axial_stop in axial_parts:
        panel_line = []
        for circ_start, circ_stop in circ_parts:
            panel_line.append(
                jnp.einsum(
                    "kxyr,lxyr->kl",
                    reached[:, axial_start:axial_stop, circ_start:circ_stop],
                    halo_onehot[:, axial_start:axial_stop, circ_start:circ_stop],
                    precision=PRECISE,
                )
            )
        panel_rows.append(jnp.stack(panel_line))
    return jnp.transpose(jnp.stack(panel_rows), (2, 0, 1, 3))


def cycle_blocks(panels):
    cycle_size = panels.shape[0]
    positions = jnp.arange(cycle_size, dtype=jnp.int32)
    shifts = jnp.stack(
        [
            ((positions[:, None] + offset) % cycle_size == positions[None, :]).astype(jnp.float32)
            for offset in (-1, 0, 1)
        ]
    )
    blocks = jnp.einsum("sjm,jkrsl->rjkml", shifts, panels, precision=PRECISE)
    return blocks.reshape(2, cycle_size * LABELS, cycle_size * LABELS)


def block_factor(diagonal_blocks, upper_blocks):
    block_size = diagonal_blocks.shape[1]
    identity = jnp.eye(block_size, dtype=jnp.float32)

    def advance(carried, inputs):
        inverse_prev, upper_prev = carried
        diagonal_now, upper_now = inputs
        coupling = jnp.dot(inverse_prev, upper_prev, precision=PRECISE)
        schur_block = diagonal_now - jnp.dot(coupling.T, coupling, precision=PRECISE)
        factor_now = jnp.linalg.cholesky(schur_block)
        inverse_now = lax.linalg.triangular_solve(factor_now, identity, left_side=True, lower=True)
        return ((inverse_now, upper_now), (inverse_now, coupling))

    start = (identity, jnp.zeros((block_size, block_size), jnp.float32))
    unused, (inverses, couplings) = lax.scan(advance, start, (diagonal_blocks, upper_blocks))
    return (inverses, couplings)


def coarse_solve(inverses, couplings, coarse_rhs):
    cycle_count, block_size = (inverses.shape[0], inverses.shape[1])
    parts = coarse_rhs.reshape(cycle_count, block_size)

    def forward(previous, members):
        inverse_now, coupling, part_now = members
        target = part_now - jnp.dot(coupling.T, previous, precision=PRECISE)
        solved = jnp.dot(inverse_now, target, precision=PRECISE)
        return (solved, solved)

    unused, middle = lax.scan(
        forward, jnp.zeros((block_size,), jnp.float32), (inverses, couplings, parts)
    )
    couplings_next = jnp.concatenate(
        [couplings[1:], jnp.zeros((1, block_size, block_size), jnp.float32)], axis=0
    )

    def backward(solved_next, members):
        inverse_now, coupling_next, middle_now = members
        target = middle_now - jnp.dot(coupling_next, solved_next, precision=PRECISE)
        solved = jnp.dot(inverse_now.T, target, precision=PRECISE)
        return (solved, solved)

    unused_last, solution_parts = lax.scan(
        backward,
        jnp.zeros((block_size,), jnp.float32),
        (inverses, couplings_next, middle),
        reverse=True,
    )
    return solution_parts.reshape(-1)


def spread_coarse(coarse_values, halo_onehot, axial_index, circ_index, cycle_count, cycle_size):
    by_device = coarse_values.reshape(cycle_count, cycle_size, LABELS)
    grid_rows = []
    for move_axial in (-1, 0, 1):
        target = axial_index + move_axial
        present = jnp.logical_and(target >= 0, target < cycle_count)
        cycle_row = lax.dynamic_index_in_dim(
            by_device, jnp.clip(target, 0, cycle_count - 1), 0, keepdims=False
        )
        line_values = []
        for move_circ in (-1, 0, 1):
            beside = lax.dynamic_index_in_dim(
                cycle_row, (circ_index + move_circ) % cycle_size, 0, keepdims=False
            )
            line_values.append(jnp.where(present, beside, jnp.zeros_like(beside)))
        grid_rows.append(jnp.stack(line_values))
    regional = jnp.stack(grid_rows)
    rows_axial = halo_onehot.shape[1] - 2
    rows_circ = halo_onehot.shape[2] - 2
    regional = jnp.repeat(
        regional, np.array([1, rows_axial, 1]), axis=0, total_repeat_length=rows_axial + 2
    )
    regional = jnp.repeat(
        regional, np.array([1, rows_circ, 1]), axis=1, total_repeat_length=rows_circ + 2
    )
    return jnp.einsum("lxyr,xyl->xyr", halo_onehot, regional, precision=PRECISE)


def shards(right_side, stiffness, material, groups):
    cycle_count = lax.axis_size(AXIAL)
    cycle_size = lax.axis_size(CIRC)
    axial_index = lax.axis_index(AXIAL)
    circ_index = lax.axis_index(CIRC)
    labels_pad = extend_labels(jnp.stack([material, groups]))
    weights, diagonal = edge_weights(extend_field(stiffness), labels_pad[0])
    own_onehot = class_onehot(groups, LABELS)
    halo_onehot = class_onehot(labels_pad[1], LABELS)
    panels = coarse_panels(weights, diagonal, own_onehot, halo_onehot)
    cycle_panels = collect(panels[None], CIRC, 0)
    own_cycle = cycle_blocks(cycle_panels)
    all_cycles = lax.all_gather(own_cycle[None], AXIAL, axis=0, tiled=True)
    inverses, couplings = block_factor(all_cycles[:, 0], all_cycles[:, 1])

    def project(field):
        return jnp.einsum("kxyr,xyr->k", own_onehot, field, precision=PRECISE)

    def coarse_gather(field, partial_sum):
        gathered = gather_axes(
            jnp.concatenate([project(field), partial_sum[None]])[None], AXIAL_CIRC, (0, 2, 3, 1), 0
        )
        return (gathered[:, :LABELS].reshape(-1), jnp.sum(gathered[:, LABELS]))

    def spread(coarse_rhs):
        return spread_coarse(
            coarse_solve(inverses, couplings, coarse_rhs),
            halo_onehot,
            axial_index,
            circ_index,
            cycle_count,
            cycle_size,
        )

    def deflate(residual_now):
        residual_image = stencil_apply(extend_field(residual_now), weights, diagonal)
        partial_sum = jnp.sum(residual_now * residual_now)
        coarse_rhs, norm_value = coarse_gather(residual_image, partial_sum)
        return (residual_image, norm_value, spread(coarse_rhs))

    start_rhs, unused_norm = coarse_gather(right_side, jnp.zeros((), jnp.float32))
    start_pad = spread(start_rhs)
    solution = start_pad[1:-1, 1:-1]
    residual = right_side - stencil_apply(start_pad, weights, diagonal)
    residual_image, norm_now, spread_pad = deflate(residual)
    direction = residual - spread_pad[1:-1, 1:-1]
    direction_image = None
    direction_image = residual_image - stencil_apply(spread_pad, weights, diagonal)
    for iteration in range(ITERS):
        curvature = over_axes(jnp.sum(direction * direction_image), AXIAL_CIRC)
        step_length = norm_now / curvature
        solution = solution + step_length * direction
        residual = residual - step_length * direction_image
        if iteration + 1 < ITERS:
            residual_image, norm_next, spread_pad = deflate(residual)
            beta_ratio = norm_next / norm_now
            shifted = spread_pad[1:-1, 1:-1]
            direction_image = (
                beta_ratio * direction_image
                + residual_image
                - stencil_apply(spread_pad, weights, diagonal)
            )
            direction = beta_ratio * direction + residual - shifted
            norm_now = norm_next
    return (solution, residual)


def solution(mesh):
    split = Mesh(mesh.devices.reshape(8, 2, 4, 4), ("axial_0", "axial_1", "circ_0", "circ_1"))
    placed = (
        P(AXIAL, CIRC, None),
        P(AXIAL, CIRC, None),
        P(AXIAL, CIRC, None),
        P(AXIAL, CIRC, None),
    )
    return jax.shard_map(
        shards,
        mesh=split,
        in_specs=placed,
        out_specs=(P(AXIAL, CIRC, None), P(AXIAL, CIRC, None)),
        check_vma=False,
    )
```

profile of v0, /device:TPU:1, one launch (start us, length us, event | category | flops | bytes accessed | tf_op | source)
XLA Modules:
  0.0 991.9 jit_solution(13249270050933131890)
XLA Ops:
  101.8 17.4 %all-reduce.154 = f32[72]{0:T(128)S(1)} all-reduce(f32[72]{0:T(128)S(1)} %maximum_dynamic-update-slice_fusion), channel_id=2, replica_groups=mesh['axial_0'=8,'axial_1'=2,'circ_0'=4,'circ_1'=4] {'axial_0'}, use_global_device_ids=true, to_apply=%add.154 | all-reduce | flops 72 | bytes 576
  150.2 416.1 %while.113 = (s32[]{:T(128)}, f32[128,128]{1,0:T(8,128)S(1)}, f32[128,128]{1,0:T(8,128)S(1)}, f32[16,128,128]{2,1,0:T(8,128)}, f32[16,128,128]{2,1,0:T(8,128)}, ...) while((s32[]{:T(128)}, f32[128,128]{1,0:T(8,128)S(1)}, ...), condition=%wide.region_3.4_spmd.clone, body=%wide.region_0.3_spmd.clone.sunk | while | flops 75694208 | bytes 1575007 | solution.py:238
  152.9 11.7 %cholesky.75 = f32[128,128]{1,0:T(8,128)S(1)} custom-call(f32[128,128]{1,0:T(8,128)S(1)} %fusion.439), custom_call_target="Cholesky" | custom-call | tf_op jit(solution)/shard_map/while/body/eval_jaxpr/jit(cholesky)/cholesky | solution.py:233
  178.9 11.7 %cholesky.75 = f32[128,128]{1,0:T(8,128)S(1)} custom-call(f32[128,128]{1,0:T(8,128)S(1)} %fusion.439), custom_call_target="Cholesky" | custom-call | tf_op jit(solution)/shard_map/while/body/eval_jaxpr/jit(cholesky)/cholesky | solution.py:233
  204.8 11.7 %cholesky.75 = f32[128,128]{1,0:T(8,128)S(1)} custom-call(f32[128,128]{1,0:T(8,128)S(1)} %fusion.439), custom_call_target="Cholesky" | custom-call | tf_op jit(solution)/shard_map/while/body/eval_jaxpr/jit(cholesky)/cholesky | solution.py:233
  230.8 11.7 %cholesky.75 = f32[128,128]{1,0:T(8,128)S(1)} custom-call(f32[128,128]{1,0:T(8,128)S(1)} %fusion.439), custom_call_target="Cholesky" | custom-call | tf_op jit(solution)/shard_map/while/body/eval_jaxpr/jit(cholesky)/cholesky | solution.py:233
  256.8 11.7 %cholesky.75 = f32[128,128]{1,0:T(8,128)S(1)} custom-call(f32[128,128]{1,0:T(8,128)S(1)} %fusion.439), custom_call_target="Cholesky" | custom-call | tf_op jit(solution)/shard_map/while/body/eval_jaxpr/jit(cholesky)/cholesky | solution.py:233
  282.8 11.7 %cholesky.75 = f32[128,128]{1,0:T(8,128)S(1)} custom-call(f32[128,128]{1,0:T(8,128)S(1)} %fusion.439), custom_call_target="Cholesky" | custom-call | tf_op jit(solution)/shard_map/while/body/eval_jaxpr/jit(cholesky)/cholesky | solution.py:233
  308.8 11.7 %cholesky.75 = f32[128,128]{1,0:T(8,128)S(1)} custom-call(f32[128,128]{1,0:T(8,128)S(1)} %fusion.439), custom_call_target="Cholesky" | custom-call | tf_op jit(solution)/shard_map/while/body/eval_jaxpr/jit(cholesky)/cholesky | solution.py:233
  334.8 11.7 %cholesky.75 = f32[128,128]{1,0:T(8,128)S(1)} custom-call(f32[128,128]{1,0:T(8,128)S(1)} %fusion.439), custom_call_target="Cholesky" | custom-call | tf_op jit(solution)/shard_map/while/body/eval_jaxpr/jit(cholesky)/cholesky | solution.py:233
  360.7 11.7 %cholesky.75 = f32[128,128]{1,0:T(8,128)S(1)} custom-call(f32[128,128]{1,0:T(8,128)S(1)} %fusion.439), custom_call_target="Cholesky" | custom-call | tf_op jit(solution)/shard_map/while/body/eval_jaxpr/jit(cholesky)/cholesky | solution.py:233
  386.7 11.7 %cholesky.75 = f32[128,128]{1,0:T(8,128)S(1)} custom-call(f32[128,128]{1,0:T(8,128)S(1)} %fusion.439), custom_call_target="Cholesky" | custom-call | tf_op jit(solution)/shard_map/while/body/eval_jaxpr/jit(cholesky)/cholesky | solution.py:233
  567.7 33.8 %while.107 = (s32[]{:T(128)}, f32[128]{0:T(128)S(1)}, f32[16,128]{1,0:T(8,128)S(1)}, f32[16,128,128]{2,1,0:T(8,128)}, f32[16,128]{1,0:T(8,128)S(1)}, /*index=5*/f32[16,128,128]{2,1,0:T(8,128)}, s32[]{:T(128)}, s32[]{:T(128)}) while((s32[]{:T(128)}, f32[128]{0:T(128)S(1)}, f32[16,128]{1,0:T(8,128)S(1)}, f32[16,128,128]{2,1,0:T(8,128)}, ...), condition=%wide.region_5.6_spmd, body=%wide.region_4.5_spmd.sunk | while | flops 393346 | bytes 136281 | solution.py:252
  601.6 20.4 %while.108 = (s32[]{:T(128)}, f32[128]{0:T(128)S(1)}, f32[16,128]{1,0:T(8,128)S(1)}, f32[16,128,128]{2,1,0:T(8,128)}, f32[16,128]{1,0:T(8,128)S(1)}, /*index=5*/...) while((s32[]{:T(128)}, f32[128]{0:T(128)S(1)}, f32[16,128]{1,0:T(8,128)S(1)}, ...), condition=%wide.region_7.8_spmd, body=%wide.region_6.7_spmd.sunk | while | flops 393347 | bytes 135793 | solution.py:265
  646.6 12.2 %all-reduce.155 = f32[72]{0:T(128)S(1)} all-reduce(f32[72]{0:T(128)S(1)} %maximum_dynamic-update-slice_fusion.1), channel_id=3, replica_groups=mesh['axial_0'=8,'axial_1'=2,'circ_0'=4,'circ_1'=4] {'axial_0'}, use_global_device_ids=true, to_apply=%add.155 | all-reduce | flops 72 | bytes 576
  677.0 13.1 %all_gather.47 = f32[256,1,9]{2,0,1:T(8,128)S(1)} all-gather(f32[128,1,9]{2,0,1:T(8,128)S(1)} %all_gather.46), channel_id=1, replica_groups=mesh['axial_0'=8,'axial_1'=2,'circ_0'=4,'circ_1'=4] {'axial_1'}, dimensions={0}, use_global_device_ids=true | all-gather | bytes 13824 | tf_op jit(solution)/shard_map/all_gather | solution.py:70
  690.3 33.7 %while.109 = (s32[]{:T(128)}, f32[128]{0:T(128)S(1)}, f32[16,128]{1,0:T(8,128)S(1)}, f32[16,128,128]{2,1,0:T(8,128)}, f32[16,128]{1,0:T(8,128)S(1)}, /*index=5*/f32[16,128,128]{2,1,0:T(8,128)}, s32[]{:T(128)}, s32[]{:T(128)}) while((s32[]{:T(128)}, f32[128]{0:T(128)S(1)}, f32[16,128]{1,0:T(8,128)S(1)}, f32[16,128,128]{2,1,0:T(8,128)}, ...), condition=%wide.region_17.20_spmd, body=%wide.region_16.19_spmd.sunk | while | flops 393346 | bytes 136281 | solution.py:252
  724.1 33.8 %while.110 = (s32[]{:T(128)}, f32[128]{0:T(128)S(1)}, f32[16,128]{1,0:T(8,128)S(1)}, f32[16,128,128]{2,1,0:T(8,128)}, f32[16,128]{1,0:T(8,128)S(1)}, /*index=5*/...) while((s32[]{:T(128)}, f32[128]{0:T(128)S(1)}, f32[16,128]{1,0:T(8,128)S(1)}, ...), condition=%wide.region_19.22_spmd, body=%wide.region_18.21_spmd.sunk | while | flops 393347 | bytes 135793 | solution.py:265
  765.0 12.6 %psum.56 = f32[]{:T(128)} all-reduce(f32[]{:T(128)} %get-tuple-element.743), channel_id=1, replica_groups=mesh['axial_0'=8,'axial_1'=2,'circ_0'=4,'circ_1'=4] {'axial_0'}, use_global_device_ids=true, to_apply=%region_27.30 | all-reduce | flops 1 | bytes 8 | tf_op jit(solution)/shard_map/psum | solution.py:82
  825.9 12.1 %all-reduce.156 = f32[72]{0:T(128)S(1)} all-reduce(f32[72]{0:T(128)S(1)} %maximum_dynamic-update-slice_fusion.2), channel_id=4, replica_groups=mesh['axial_0'=8,'axial_1'=2,'circ_0'=4,'circ_1'=4] {'axial_0'}, use_global_device_ids=true, to_apply=%add.156 | all-reduce | flops 72 | bytes 576
  856.1 12.1 %all_gather.51 = f32[256,1,9]{2,0,1:T(8,128)S(1)} all-gather(f32[128,1,9]{2,0,1:T(8,128)S(1)} %all_gather.50), channel_id=1, replica_groups=mesh['axial_0'=8,'axial_1'=2,'circ_0'=4,'circ_1'=4] {'axial_1'}, dimensions={0}, use_global_device_ids=true | all-gather | bytes 13824 | tf_op jit(solution)/shard_map/all_gather | solution.py:70
  869.2 33.8 %while.111 = (s32[]{:T(128)}, f32[128]{0:T(128)S(1)}, f32[16,128]{1,0:T(8,128)S(1)}, f32[16,128,128]{2,1,0:T(8,128)}, f32[16,128]{1,0:T(8,128)S(1)}, /*index=5*/f32[16,128,128]{2,1,0:T(8,128)}, s32[]{:T(128)}, s32[]{:T(128)}) while((s32[]{:T(128)}, f32[128]{0:T(128)S(1)}, f32[16,128]{1,0:T(8,128)S(1)}, f32[16,128,128]{2,1,0:T(8,128)}, ...), condition=%wide.region_34.37_spmd, body=%wide.region_33.36_spmd.sunk | while | flops 393346 | bytes 136281 | solution.py:252
  903.0 33.8 %while.112 = (s32[]{:T(128)}, f32[128]{0:T(128)S(1)}, f32[16,128]{1,0:T(8,128)S(1)}, f32[16,128,128]{2,1,0:T(8,128)}, f32[16,128]{1,0:T(8,128)S(1)}, /*index=5*/...) while((s32[]{:T(128)}, f32[128]{0:T(128)S(1)}, f32[16,128]{1,0:T(8,128)S(1)}, ...), condition=%wide.region_36.39_spmd, body=%wide.region_35.38_spmd.sunk | while | flops 393347 | bytes 135793 | solution.py:265
  947.9 13.8 %psum.60 = f32[]{:T(128)} all-reduce(f32[]{:T(128)} %get-tuple-element.739), channel_id=1, replica_groups=mesh['axial_0'=8,'axial_1'=2,'circ_0'=4,'circ_1'=4] {'axial_0'}, use_global_device_ids=true, to_apply=%region_44.47 | all-reduce | flops 1 | bytes 8 | tf_op jit(solution)/shard_map/psum | solution.py:82
  (875 shorter events, 757.0 us)
Async XLA Ops:
  7.2 31.9 %copy-start.48 = (s32[8,16,256]{2,1,0:T(8,128)S(1)}, s32[8,16,256]{2,1,0:T(8,128)}, u32[]{:S(2)}) copy-start(s32[8,16,256]{2,1,0:T(8,128)} %param.43) | copy-start | bytes 393220
  7.2 31.9 %copy-start.47 = (s32[8,16,256]{2,1,0:T(8,128)S(1)}, s32[8,16,256]{2,1,0:T(8,128)}, u32[]{:S(2)}) copy-start(s32[8,16,256]{2,1,0:T(8,128)} %param.44) | copy-start | bytes 393220
  8.2 21.0 %collective-permute-start = (s32[2,8,1,256]{3,2,1,0:T(1,128)S(1)}, s32[2,8,1,256]{3,2,1,0:T(1,128)S(1)}, u32[]{:S(2)}, u32[]{:S(2)}) collective-permute-start(s32[2,8,1,256]{3,2,1,0:T(1,128)S(1)} %get-tuple-element.828), channel_id=1, source_target_pairs={{0,1},{1,2},{2,3},{3,4},{4,5},{5,6},{6,7},{7,8},{8,9},{9,10},{10,1... | collective-permute-start | bytes 49160 | tf_op jit(solution)/shard_map/ppermute | solution.py:45
  10.4 18.8 %collective-permute-start.1 = (s32[2,8,1,256]{3,2,1,0:T(1,128)S(1)}, s32[2,8,1,256]{3,2,1,0:T(1,128)S(1)}, u32[]{:S(2)}, u32[]{:S(2)}) collective-permute-start(s32[2,8,1,256]{3,2,1,0:T(1,128)S(1)} %get-tuple-element.829), channel_id=1, source_target_pairs={{1,0},{2,1},{3,2},{4,3},{5,4},{6,5},{7,6},{8,7},{9,8},{10,9},{11,1... | collective-permute-start | bytes 49160 | tf_op jit(solution)/shard_map/ppermute | solution.py:46
  15.0 6.2 collective-permute-start.4
  15.1 6.2 collective-permute-start.5
  21.1 34.8 %copy-start.44 = (pred[8,8,16,256]{3,0,1,2:T(8,128)(4,1)}, pred[8,8,16,256]{3,0,1,2:T(8,128)(4,1)S(1)}, u32[]{:S(2)}) copy-start(pred[8,8,16,256]{3,0,1,2:T(8,128)(4,1)S(1)} %iota_compare_fusion.6) | copy-start | bytes 786436
  22.0 13.8 %collective-permute-start.6 = (f32[1,18,256]{2,1,0:T(8,128)S(1)}, f32[1,18,256]{2,1,0:T(8,128)S(1)}, u32[]{:S(2)}, u32[]{:S(2)}) collective-permute-start(f32[1,18,256]{2,1,0:T(8,128)S(1)} %get-tuple-element.934), channel_id=1, source_target_pairs={{0,16},{16,32},{32,48},{48,64},{64,80},{80,96},{96,112},{112,128},... | collective-permute-start | bytes 55304 | tf_op jit(solution)/shard_map/ppermute | solution.py:45
  27.3 8.5 collective-permute-start.7
  30.0 5.9 collective-permute-start.2
  33.7 5.4 collective-permute-start.3
  78.2 12.9 %all-to-all-start = ((f32[16,1,384]{2,1,0:T(1,128)}), f32[16,1,384]{2,1,0:T(1,128)S(1)}, u32[]{:S(2)}, u32[]{:S(2)}) async-start(f32[16,1,384]{2,1,0:T(1,128)} %reshape.1223), calls=%async_computation | async-start | bytes 49152 | tf_op jit(solution)/shard_map/all_to_all | solution.py:53
  84.7 62.8 %all-gather.5.cloned.1.call-start = ((), (), s32[]{:S(2)}) async-start(), calls=%async_computation.1 | async-start | bytes 2228224 | tf_op jit(solution)/shard_map/all_gather | solution.py:314
  98.0 49.4 %copy-start.58 = (s32[10]{0:T(128)S(1)}, s32[10]{0:T(128)}, u32[]{:S(2)}) copy-start(s32[10]{0:T(128)} %constant.1462) | copy-start | bytes 124
  98.0 49.4 %copy-start.57 = (s32[18]{0:T(128)S(1)}, s32[18]{0:T(128)}, u32[]{:S(2)}) copy-start(s32[18]{0:T(128)} %constant.1463) | copy-start | bytes 220
  627.9 2.6 collective-permute-start.8
  629.4 5.8 collective-permute-start.9
  635.3 6.6 collective-permute-start.10
  639.0 3.5 collective-permute-start.11
  690.2 68.2 %copy-start.49 = (f32[2,4,4,8,1,9]{5,1,2,0,3,4:T(4,128)}, f32[2,4,4,8,1,9]{5,1,2,0,3,4:T(4,128)S(1)}, u32[]{:S(2)}) copy-start(f32[2,4,4,8,1,9]{5,1,2,0,3,4:T(4,128)S(1)} %copy.274) | copy-start | bytes 27652
  802.6 3.5 collective-permute-start.12
  805.3 5.8 collective-permute-start.13
  811.2 9.6 collective-permute-start.14
  818.6 3.1 collective-permute-start.15
  (54 other events, 142.2 us)
Sparse Core Ops, SparseCore 0:
  98.2 40.7 all-gather.4
where the time goes:
time: 1010 us; the launch traced here: 992 us
  other arithmetic  409 us (40%)
  matrix products  235 us (23%)
  blocking collectives  198 us (20%)
  local copies, waits for them, and re-layouts  51.7 us (5%)
  starting transfers between devices  50.3 us (5%)
  waiting for transfers between devices  22.7 us (2%)
  between operations  21 us (2%)
    another operation x48, other arithmetic, advance(): factor_now = jnp.linalg.cholesky(schur_block)  198 us
    another operation x32, other arithmetic, advance(): lax.linalg.triangular_solve(factor_now, identity, left_side=True, lower=T...  167 us
    all_gather x9, blocking collectives, gather_in_order(): parts = lax.all_gather(parts, axes[k], axis=0, tiled=True)  89.4 us
    psum x8, blocking collectives, over_axes(): return functools.reduce(lax.psum, axes, array)  66.9 us
    dot_general x48, matrix products, backward(): solved = jnp.dot(inverse_now.T, target, precision=PRECISE)  49.9 us
    dot_general x48, matrix products, forward(): solved = jnp.dot(inverse_now, target, precision=PRECISE)  49.3 us
    dot_general x48, matrix products, forward(): target = part_now - jnp.dot(coupling.T, previous, precision=PRECISE)  48.1 us
    unnamed x3, blocking collectives  41.6 us
  transfers between devices with their start and end apart: 18, of which 8 were waited for; matrix products, arithmetic and copies ran while one was open for 1% of the time, Pallas kernels for 0%

commit v1 on v0

v1 whole, which is shorter than its diff:
```python
import math

import jax
import jax.numpy as jnp
import numpy as np
from jax import lax
from jax.experimental import pallas as pl
from jax.experimental.pallas import tpu as pltpu
from jax.sharding import Mesh
from jax.sharding import PartitionSpec as P

LABELS = 8
CLASSES = 16
CIRC = ("circ_0", "circ_1")
AXIAL = ("axial_0", "axial_1")
AXIAL_CIRC = ("axial_0", "axial_1", "circ_0", "circ_1")
MASS_SHIFT = 0.02
HIGH = lax.Precision.HIGHEST
HALF_STEPS = (
    (0, 0, 1),
    (0, 1, -1),
    (0, 1, 0),
    (0, 1, 1),
    (1, -1, -1),
    (1, -1, 0),
    (1, -1, 1),
    (1, 0, -1),
    (1, 0, 0),
    (1, 0, 1),
    (1, 1, -1),
    (1, 1, 0),
    (1, 1, 1),
)
STEP_OF = {step: place for place, step in enumerate(HALF_STEPS)}
SHIFTS = [(sy, sz) for sy in (-1, 0, 1) for sz in (-1, 0, 1)]
ROWS = 24
EDGE = 4
DEPTH = 3
BLOCK = 128
F32 = jnp.float32
BF16 = jnp.bfloat16


def coefficient_table():
    rows_out = []
    for material_id in range(CLASSES):
        fiber_angle = math.pi * (material_id % 8) / 8.0
        if material_id < 8:
            fiber_dir = (math.cos(fiber_angle), math.sin(fiber_angle), 0.0)
            strength, anisotropy = (1.0, 6.0)
        else:
            fiber_dir = (0.6 * math.cos(fiber_angle), 0.6 * math.sin(fiber_angle), 0.8)
            strength, anisotropy = (0.35, 2.0)
        line_values = []
        for offset in HALF_STEPS:
            length_sq = float(offset[0] * offset[0] + offset[1] * offset[1] + offset[2] * offset[2])
            along_fiber = (
                fiber_dir[0] * offset[0] + fiber_dir[1] * offset[1] + fiber_dir[2] * offset[2]
            )
            line_values.append(
                strength * (0.15 + anisotropy * along_fiber * along_fiber / length_sq) / length_sq
            )
        rows_out.append(line_values)
    return np.array(rows_out, dtype=np.float32)


def inverse_scales():
    table = coefficient_table().astype(np.float64)
    widest = MASS_SHIFT + 0.3 * (table.sum(axis=1).max() + table.max(axis=0).sum())
    low = 0.5 * MASS_SHIFT / widest
    scales = []
    while 1.0 - low > 2e-7:
        scales.append(2.0 / (1.0 + low))
        low = 4.0 * low / (1.0 + low) ** 2
    return scales


SCALES = inverse_scales()


def lanes(shape):
    return lax.broadcasted_iota(jnp.int32, shape, len(shape) - 1)


def sublanes(shape):
    return lax.broadcasted_iota(jnp.int32, shape, len(shape) - 2)


def shift_z(values, move, fill):
    if move == 0:
        return values
    length = values.shape[-1]
    turned = pltpu.roll(values, (-move) % length, axis=1)
    edge = length - 1 if move > 0 else 0
    return jnp.where(lanes(values.shape) == edge, fill, turned)


def shift_y(values, move):
    if move == 0:
        return values
    return pltpu.roll(values, (-move) % values.shape[0], axis=0)


def shifted(values, fill):
    by_z = {sz: shift_z(values, sz, fill) for sz in (-1, 0, 1)}
    return {(sy, sz): shift_y(by_z[sz], sy) for sy, sz in SHIFTS}


def present_flags(place_ref, plane):
    if plane < 0:
        return place_ref[0] > 0
    if plane > 7:
        return place_ref[0] < 15
    return None


def masked(values, flag):
    if flag is None:
        return values
    return values * jnp.where(flag, 1.0, 0.0).astype(F32)


def stencil(v_at, k_ref, diag_ref, start, stop, emit):
    wide = {}
    made = {}

    def prepare(plane):
        values = v_at(plane)
        wide[plane] = shifted(values, 0.0)
        made[plane] = [k_ref[plane + DEPTH, j] * values for j in range(13)]

    prepare(start - 1)
    prepare(start)
    for plane in range(start, stop):
        prepare(plane + 1)
        total = None
        for j, (ox, oy, oz) in enumerate(HALF_STEPS):
            pair = wide[plane + ox][(oy, oz)] + wide[plane - ox][(-oy, -oz)]
            term = k_ref[plane + DEPTH, j] * pair
            total = term if total is None else total + term
        for sz in (-1, 0, 1):
            by_y = None
            for sy in (-1, 0, 1):
                part = made[plane + 1][STEP_OF[(1, sy, sz)]] + made[plane - 1][STEP_OF[(1, -sy, -sz)]]
                if (0, sy, sz) in STEP_OF:
                    part = part + made[plane][STEP_OF[(0, sy, sz)]]
                elif (0, -sy, -sz) in STEP_OF:
                    part = part + made[plane][STEP_OF[(0, -sy, -sz)]]
                part = shift_y(part, sy)
                by_y = part if by_y is None else by_y + part
            total = total + shift_z(by_y, sz, 0.0)
        emit(plane, diag_ref[plane + 2] * wide[plane][(0, 0)] - 0.5 * total)
        del wide[plane - 1], made[plane - 1]


def piece(low_ref, mid_ref, high_ref, field, plane):
    if plane < 0:
        return low_ref[field, plane + DEPTH]
    if plane > 7:
        return high_ref[field, plane - 8]
    return mid_ref[field, plane]


def split3(values):
    high = values.astype(BF16)
    rest = values - high.astype(F32)
    mid = rest.astype(BF16)
    low = (rest - mid.astype(F32)).astype(BF16)
    return high, mid, low


def dot(a, b, dims=((1,), (0,))):
    return lax.dot_general(a, b, (dims, ((), ())), preferred_element_type=F32)


def dot_high(a, b, dims=((1,), (0,))):
    return lax.dot_general(
        a, b, (dims, ((), ())), precision=HIGH, preferred_element_type=F32
    )


def pick(values, chooser):
    return sum(dot(part, chooser) for part in split3(values))


def setup_kernel(low_ref, mid_ref, high_ref, table_ref, place_ref, k_ref, diag_ref, slot_ref, label_ref):
    for plane in range(-DEPTH, 8 + DEPTH):
        stiff = piece(low_ref, mid_ref, high_ref, 1, plane)
        kind = piece(low_ref, mid_ref, high_ref, 2, plane).astype(jnp.int32)
        for j in range(13):
            row = jnp.broadcast_to(table_ref[j : j + 1, :], (8, 128))
            parts = []
            for top in range(0, ROWS, 8):
                line = []
                for left in (0, 128):
                    line.append(
                        jnp.take_along_axis(
                            row,
                            kind[top : top + 8, left : left + 128],
                            axis=1,
                            mode="promise_in_bounds",
                        )
                    )
                parts.append(jnp.concatenate(line, axis=1))
            k_ref[plane + DEPTH, j] = stiff * jnp.concatenate(parts, axis=0)
    for plane in range(-2, 10):
        own = None
        total = None
        for j in range(13):
            term = k_ref[plane + DEPTH, j]
            own = term if own is None else own + term
        for sz in (-1, 0, 1):
            by_y = None
            for sy in (-1, 0, 1):
                part = k_ref[plane + 1 + DEPTH, STEP_OF[(1, sy, sz)]]
                part = part + k_ref[plane - 1 + DEPTH, STEP_OF[(1, -sy, -sz)]]
                if (0, sy, sz) in STEP_OF:
                    part = part + k_ref[plane + DEPTH, STEP_OF[(0, sy, sz)]]
                elif (0, -sy, -sz) in STEP_OF:
                    part = part + k_ref[plane + DEPTH, STEP_OF[(0, -sy, -sz)]]
                part = shift_y(part, sy)
                by_y = part if by_y is None else by_y + part
            by_y = shift_z(by_y, sz, 0.0)
            total = by_y if total is None else total + by_y
        diag_ref[plane + 2] = MASS_SHIFT + own + 0.5 * total
    for plane in range(0, 9):
        spots = shifted(piece(low_ref, mid_ref, high_ref, 3, plane), -1.0)
        for place, shift in enumerate(SHIFTS):
            label_ref[plane, place] = spots[shift][:16]
    row16 = sublanes((16, 256))
    sums = {}
    for plane in range(8):
        pairs = {"own": [], "up": [], "down": [], "next": [], "nextup": [], "nextdown": []}
        for j, (ox, oy, oz) in enumerate(HALF_STEPS):
            across = shift_z(shift_y(k_ref[plane + ox + DEPTH, j], oy), oz, 0.0)[:16]
            weight = -0.5 * (k_ref[plane + DEPTH, j, 0:16] + across)
            target = label_ref[plane + ox, SHIFTS.index((oy, oz))]
            outside = ox == 1 and plane == 7
            if oy == 0:
                pairs["next" if outside else "own"].append((weight, target))
            elif oy == 1:
                pairs["next" if outside else "own"].append((jnp.where(row16 == 15, 0.0, weight), target))
                pairs["nextup" if outside else "up"].append(
                    (jnp.where(row16 == 15, weight, 0.0)[8:], target[8:])
                )
            else:
                pairs["next" if outside else "own"].append((jnp.where(row16 == 0, 0.0, weight), target))
                pairs["nextdown" if outside else "down"].append(
                    (jnp.where(row16 == 0, weight, 0.0)[:8], target[:8])
                )
        home = label_ref[plane, SHIFTS.index((0, 0))]
        pairs["own"].append((0.5 * diag_ref[plane + 2, 0:16], home))
        load = mid_ref[0, plane, 0:16]

        def by_label(region):
            out = []
            for label in range(LABELS):
                total = None
                for weight, target in pairs[region]:
                    term = jnp.where(target == float(label), weight, 0.0)
                    total = term if total is None else total + term
                if total is None:
                    total = jnp.zeros((8, 256), F32)
                out.append(total)
            return out

        own = by_label("own")
        sides = (by_label("down"), by_label("up"))
        for half in (0, 1):
            rows = slice(8 * half, 8 * half + 8)
            chosen = jnp.concatenate(
                [jnp.where(home[rows] == float(k), 1.0, 0.0) for k in range(LABELS)], axis=0
            ).astype(BF16)
            right = jnp.concatenate([o[rows] for o in own] + [load[rows]] + sides[half], axis=0)
            got = sum(dot(chosen, part, ((1,), (1,))) for part in split3(right))
            sums[half] = got if half not in sums else sums[half] + got
            if plane == 7:
                if half == 0:
                    nexts = by_label("next")
                    corners = (by_label("nextdown"), by_label("nextup"))
                right = jnp.concatenate([o[rows] for o in nexts] + corners[half], axis=0)
                sums[2 + half] = sum(dot(chosen, part, ((1,), (1,))) for part in split3(right))

    def place_of(col, half, ahead):
        group = col // 8
        if ahead:
            side = 24 + (16 if half else 0)
            return jnp.where(group < 8, 24 + 8 + group, side + group - 8)
        side = 16 if half else 0
        return jnp.where(group < 8, 8 + group, jnp.where(group == 8, 48, side + group - 9))

    collected = None
    for which in range(4):
        width = sums[which].shape[1]
        shape = (64, width)
        kept = jnp.where(sublanes(shape) % 8 == lanes(shape) % 8, sums[which], 0.0)
        shape = (width, 128)
        chooser = jnp.where(
            lanes(shape) % 64 == place_of(sublanes(shape), which % 2, which >= 2), 1.0, 0.0
        )
        part = pick(kept, chooser.astype(BF16))
        collected = part if collected is None else collected + part
    shape = (64, 128)
    kept = jnp.where((sublanes(shape) // 8) % 2 == lanes(shape) // 64, collected, 0.0)
    shape = (8, 64)
    joiner = jnp.where(lanes(shape) // 16 == sublanes(shape) % 4, 1.0, 0.0).astype(BF16)
    slot = sum(dot(joiner, part) for part in split3(kept))
    for device in range(128):
        slot_ref[8 * device : 8 * device + 8, :] = slot


def coarse_rows(values, chooser):
    spread = pick(values, chooser)
    shape = (256, BLOCK)
    kept = jnp.where(sublanes(shape) % 16 == lanes(shape) % 16, spread, 0.0)
    return jnp.sum(kept.reshape(16, 16, BLOCK), axis=1)


def as_columns(rows):
    count = len(rows)
    stacked = jnp.concatenate(rows + [jnp.zeros((1, BLOCK), F32)] * (8 - count), axis=0)
    turned = stacked.T
    return [turned[:, i : i + 1] for i in range(count)]


def coarse_solve(coarse_rhs, right_ref, left_ref, last_ref):
    now = [coarse_rhs[i : i + 1, :] for i in range(16)]
    begin = 0
    stages = []
    while len(now) > 1:
        count = len(now)
        odd = now[1::2]
        even = now[0::2]
        solved = []
        for q, column in enumerate(as_columns(odd)):
            product = jnp.sum(right_ref[begin + q] * column, axis=0, keepdims=True)
            solved.append(product[:, :BLOCK])
            even[q] = even[q] - product[:, BLOCK : 2 * BLOCK]
            if q + 1 < len(even):
                even[q + 1] = even[q + 1] - product[:, 2 * BLOCK :]
        stages.append((begin, solved))
        begin += count // 2
        now = even
    (column,) = as_columns(now)
    found = [jnp.sum(last_ref[...] * column, axis=0, keepdims=True)]
    for begin, solved in reversed(stages):
        columns = as_columns(found)
        merged = []
        for q, value in enumerate(solved):
            value = value - jnp.sum(left_ref[begin + q, :BLOCK] * columns[q], axis=0, keepdims=True)
            if q + 1 < len(found):
                value = value - jnp.sum(
                    left_ref[begin + q, BLOCK:] * columns[q + 1], axis=0, keepdims=True
                )
            merged += [found[q], value]
        found = merged
    return jnp.concatenate(found, axis=0)


def split2(values):
    high = values.astype(BF16)
    return high, (values - high.astype(F32)).astype(BF16)


def dot_split(a, b):
    return dot(a[0], b[0]) + (dot(a[0], b[1]) + dot(a[1], b[0]))


def invert(blocks, scale_ref, s_ref, x_ref):
    shape = (BLOCK, BLOCK)
    eye = jnp.where(lanes(shape) == sublanes(shape), 1.0, 0.0).astype(F32)
    for q, block in enumerate(blocks):
        kept = eye * block
        across = 1.0 / jnp.sum(kept, axis=0, keepdims=True)
        down = 1.0 / jnp.sum(kept, axis=1, keepdims=True)
        c = 0.5 * SCALES[0]
        x_ref[q] = (2.0 * c * eye - (c * c) * (block * down)) * across
        high, low = split2(block)
        s_ref[q, 0] = high
        s_ref[q, 1] = low

    def step(k, carry):
        c = scale_ref[k]
        for q in range(len(blocks)):
            x = split2(x_ref[q])
            product = dot_split((s_ref[q, 0], s_ref[q, 1]), x)
            x_ref[q] = dot_split(x, split2((2.0 * c) * eye - (c * c) * product))
        return carry

    lax.fori_loop(1, len(SCALES) - 1, step, 0)
    out = []
    for q, block in enumerate(blocks):
        x = x_ref[q]
        left = eye - dot_high(block, x)
        out.append(x + dot_split(split2(x), split2(left)))
    return out


def factor_kernel(
    slots_ref, scale_ref, right_ref, left_ref, last_ref, y_ref, d_ref, b_ref, bt_ref, s_ref, x_ref
):
    shape = (256, BLOCK)
    device = sublanes(shape) % 16
    ring = lanes(shape) % 16
    near = [(device + c + 15) % 16 == ring for c in range(3)]
    coarse_rhs = None
    for pair in range(4):
        values = split3(slots_ref[pl.ds(pair, 256, stride=4), :])
        for half in (0, 1):
            label = 2 * pair + half
            shape = (128, 7 * BLOCK)
            group = lanes(shape) // BLOCK
            column = jnp.where(group < 6, group * 8 + (lanes(shape) % BLOCK) // 16, 48) + 64 * half
            chooser = jnp.where(sublanes(shape) == column, 1.0, 0.0).astype(BF16)
            wide = sum(dot(part, chooser) for part in values)
            for r, target in enumerate((d_ref, b_ref)):
                total = None
                for c in range(3):
                    at = (3 * r + c) * BLOCK
                    term = jnp.where(near[c], wide[:, at : at + BLOCK], 0.0)
                    total = term if total is None else total + term
                target[:, 16 * label : 16 * label + 16, :] = total.reshape(16, 16, BLOCK)
            mine = jnp.logical_and(device == ring, lanes((256, BLOCK)) // 16 == label)
            term = jnp.where(mine, wide[:, 6 * BLOCK :], 0.0)
            coarse_rhs = term if coarse_rhs is None else coarse_rhs + term
    coarse_rhs = jnp.sum(coarse_rhs.reshape(16, 16, BLOCK), axis=1)
    b_ref[15] = jnp.zeros((BLOCK, BLOCK), F32)
    for i in range(16):
        d_ref[i] = d_ref[i] + d_ref[i].T
        bt_ref[i] = b_ref[i].T
    begin = 0
    stride = 1
    while stride < 16:
        count = 8 // stride
        odd = [(2 * q + 1) * stride for q in range(count)]
        inverses = invert([d_ref[i] for i in odd], scale_ref, s_ref, x_ref)
        for q, i in enumerate(odd):
            before = i - stride
            after = i + stride
            inverse = inverses[q]
            c_rows = jnp.concatenate([b_ref[before], bt_ref[i]], axis=0)
            c_cols = jnp.concatenate([bt_ref[before], b_ref[i]], axis=1)
            left_ref[begin + q] = dot_high(c_rows, inverse)
            products = dot_high(inverse, c_cols)
            right_ref[begin + q, :, :BLOCK] = inverse
            right_ref[begin + q, :, BLOCK:] = products
            gram = dot_high(c_rows, products)
            d_ref[before] = d_ref[before] - gram[:BLOCK, :BLOCK]
            b_ref[before] = -gram[:BLOCK, BLOCK:]
            bt_ref[before] = -gram[BLOCK:, :BLOCK]
            if after < 16:
                d_ref[after] = d_ref[after] - gram[BLOCK:, BLOCK:]
        begin += count
        stride *= 2
    (last,) = invert([d_ref[0]], scale_ref, s_ref, x_ref)
    last_ref[...] = last
    y_ref[...] = coarse_solve(coarse_rhs, right_ref, left_ref, last_ref)


def spread_field(y_ref, place_ref, label_of, plane):
    axial = place_ref[0]
    if plane < 0:
        axial = jnp.maximum(axial - 1, 0)
    elif plane > 7:
        axial = jnp.minimum(axial + 1, 15)
    line = jnp.broadcast_to(y_ref[pl.ds(axial, 1), :], (8, BLOCK))
    ring = sublanes((ROWS, 256))
    move = jnp.where(ring < 16, 0, jnp.where(ring < 16 + EDGE, 1, 15))
    spot = label_of(plane).astype(jnp.int32) * 16 + (place_ref[1] + move) % 16
    parts = []
    for top in range(0, ROWS, 8):
        parts.append(
            jnp.concatenate(
                [
                    jnp.take_along_axis(
                        line,
                        spot[top : top + 8, left : left + 128],
                        axis=1,
                        mode="promise_in_bounds",
                    )
                    for left in (0, 128)
                ],
                axis=1,
            )
        )
    return masked(jnp.concatenate(parts, axis=0), present_flags(place_ref, plane))


def fold(values):
    half = values[:8] + values[8:]
    return half[:, :128] + half[:, 128:]


def slot_row(totals):
    count = len(totals)
    stacked = jnp.concatenate(totals, axis=0)
    shape = (8 * count, 128)
    sums = jnp.sum(stacked, axis=1, keepdims=True)
    kept = jnp.where(sublanes(shape) // 8 == lanes(shape), sums, 0.0)
    return jnp.sum(kept, axis=0, keepdims=True)


class Totals:
    def __init__(self, count):
        self.values = [None] * count

    def add(self, at, term):
        self.values[at] = term if self.values[at] is None else self.values[at] + term

    def by_label(self, labels, field):
        for k in range(LABELS):
            self.add(k, fold(jnp.where(labels == float(k), field, 0.0)))


def start_kernel(
    low_ref, mid_ref, high_ref, k_ref, diag_ref, y_ref, place_ref,
    x_out, r_out, image_ref, slot_ref, v_ref, w_ref,
):
    def label_of(plane):
        return piece(low_ref, mid_ref, high_ref, 3, plane)

    for plane in range(-3, 11):
        v_ref[plane + 3] = spread_field(y_ref, place_ref, label_of, plane)

    def put_residual(plane, image):
        load = piece(low_ref, mid_ref, high_ref, 0, plane)
        w_ref[plane + 2] = masked(load - image, present_flags(place_ref, plane))

    stencil(lambda plane: v_ref[plane + 3], k_ref, diag_ref, -2, 10, put_residual)
    totals = Totals(9)

    def put_image(plane, image):
        image_ref[plane + 1] = image
        if 0 <= plane < 8:
            totals.by_label(mid_ref[3, plane, 0:16], image[:16])
            own = w_ref[plane + 2, 0:16]
            totals.add(8, fold(own * own))

    stencil(lambda plane: w_ref[plane + 2], k_ref, diag_ref, -1, 9, put_image)
    for plane in range(8):
        x_out[plane] = v_ref[plane + 3, 0:16]
        r_out[plane] = w_ref[plane + 2, 0:16]
    slot_ref[...] = jnp.broadcast_to(slot_row(totals.values), (256, 128))


def label_chooser():
    shape = (128, BLOCK)
    return jnp.where(sublanes(shape) == lanes(shape) // 16, 1.0, 0.0).astype(BF16)


def first_kernel(
    got_ref, right_ref, left_ref, last_ref, low_ref, mid_ref, high_ref, k_ref, diag_ref, image_ref,
    r_ref, place_ref, w_out, d_out, aw_out, slot_ref, y_ref, v_ref, w_ref,
):
    got = got_ref[...]
    coarse_rhs = coarse_rows(got, label_chooser())
    y_ref[...] = coarse_solve(coarse_rhs, right_ref, left_ref, last_ref)

    def label_of(plane):
        return piece(low_ref, mid_ref, high_ref, 3, plane)

    for plane in range(-2, 10):
        v_ref[plane + 2] = spread_field(y_ref, place_ref, label_of, plane)
    totals = Totals(12)

    def put_direction_image(plane, image):
        w_ref[plane + 1] = masked(image_ref[plane + 1] - image, present_flags(place_ref, plane))

    stencil(lambda plane: v_ref[plane + 2], k_ref, diag_ref, -1, 9, put_direction_image)

    def put_second(plane, image):
        own = w_ref[plane + 1, 0:16]
        image = image[:16]
        residual = r_ref[plane]
        direction = residual - v_ref[plane + 2, 0:16]
        w_out[plane] = own
        d_out[plane] = direction
        aw_out[plane] = image
        totals.by_label(mid_ref[3, plane, 0:16], image)
        totals.add(8, fold(direction * own))
        totals.add(9, fold(own * own))
        totals.add(10, fold(residual * own))
        totals.add(11, fold(own * image))

    stencil(lambda plane: w_ref[plane + 1], k_ref, diag_ref, 0, 8, put_second)
    square = jnp.sum(got, axis=0, keepdims=True) * (1.0 / 256.0)
    shape = (1, 128)
    square = jnp.sum(jnp.where(lanes(shape) == 8, square, 0.0), axis=1, keepdims=True)
    row = slot_row(totals.values) + jnp.where(lanes(shape) == 12, square, 0.0)
    slot_ref[...] = jnp.broadcast_to(row, (256, 128))


def last_kernel(
    got_ref, right_ref, left_ref, last_ref, low_ref, mid_ref, high_ref, k_ref, diag_ref,
    x_ref, r_ref, w_ref, d_ref, aw_ref, place_ref, x_out, r_out, y_ref, v_ref,
):
    got = got_ref[...]
    coarse_rhs = coarse_rows(got, label_chooser())
    solved = coarse_solve(coarse_rhs, right_ref, left_ref, last_ref)
    y_ref[...] = solved
    row = jnp.sum(got, axis=0, keepdims=True)

    def scalar(at):
        return jnp.sum(jnp.where(lanes((1, 128)) == at, row, 0.0), axis=1, keepdims=True)

    dw, ww, rw, waw, rr = (scalar(at) for at in (8, 9, 10, 11, 12))
    hq = jnp.sum(jnp.sum(coarse_rhs * solved, axis=1, keepdims=True), axis=0, keepdims=True)
    alpha = rr / dw
    rr_next = rr - 2.0 * alpha * rw + alpha * alpha * ww
    beta = rr_next / rr
    gain = 1.0 + beta
    curvature = gain * gain * dw - 2.0 * gain * alpha * ww + alpha * alpha * (waw - hq)
    alpha_next = rr_next / curvature

    def label_of(plane):
        return piece(low_ref, mid_ref, high_ref, 3, plane)

    for plane in range(-1, 9):
        v_ref[plane + 1] = spread_field(y_ref, place_ref, label_of, plane)

    def put(plane, image):
        w = w_ref[plane]
        d = d_ref[plane]
        u = aw_ref[plane] - image[:16]
        d_next = gain * d - alpha * (w - v_ref[plane + 1, 0:16])
        w_next = gain * w - alpha * u
        x_out[plane] = x_ref[plane] + alpha * d + alpha_next * d_next
        r_out[plane] = r_ref[plane] - alpha * w - alpha_next * w_next

    stencil(lambda plane: v_ref[plane + 1], k_ref, diag_ref, 0, 8, put)


VMEM = pl.BlockSpec(memory_space=pltpu.VMEM)
SMEM = pl.BlockSpec(memory_space=pltpu.SMEM)
BIG = pltpu.CompilerParams(vmem_limit_bytes=56 * 1024 * 1024)


def shape_of(*dims):
    return jax.ShapeDtypeStruct(dims, F32)


def call(kernel, name, outs, scratch, in_specs):
    return pl.pallas_call(
        kernel,
        name=name,
        out_shape=outs,
        in_specs=in_specs,
        out_specs=tuple(VMEM for _ in outs),
        scratch_shapes=scratch,
        compiler_params=BIG,
    )


def ring_pairs(peers, wrap):
    up = [(i, (i + 1) % peers) for i in range(peers if wrap else peers - 1)]
    return up, [(j, i) for i, j in up]


def exchange(slots, count):
    return lax.all_to_all(slots.reshape(256, count, 128), AXIAL_CIRC, 0, 0, tiled=True).reshape(
        256 * count, 128
    )


def shards(right_side, stiffness, material, groups):
    place = jnp.stack([lax.axis_index(AXIAL), lax.axis_index(CIRC)]).astype(jnp.int32)
    fields = jnp.stack([right_side, stiffness, material.astype(F32), groups.astype(F32)])
    up, down = ring_pairs(16, True)
    before = lax.ppermute(fields[:, :, 16 - EDGE :], CIRC, up)
    after = lax.ppermute(fields[:, :, :EDGE], CIRC, down)
    middle = jnp.concatenate([fields, after, before], axis=2)
    up, down = ring_pairs(16, False)
    low = lax.ppermute(middle[:, 8 - DEPTH :], AXIAL, up)
    high = lax.ppermute(middle[:, :DEPTH], AXIAL, down)
    table = np.zeros((16, 128), np.float32)
    table[:13, :CLASSES] = coefficient_table().T
    ext = (ROWS, 256)
    k, diag, slots = call(
        setup_kernel,
        "setup",
        (shape_of(14, 13, *ext), shape_of(12, *ext), shape_of(1024, 128)),
        [pltpu.VMEM((9, 9, 16, 256), F32)],
        [VMEM, VMEM, VMEM, VMEM, SMEM],
    )(low, middle, high, jnp.asarray(table), place)
    gathered = exchange(slots, 4)
    square = (BLOCK, BLOCK)
    right, left, last, y = call(
        factor_kernel,
        "factor",
        (shape_of(15, BLOCK, 3 * BLOCK), shape_of(15, 2 * BLOCK, BLOCK), shape_of(*square), shape_of(16, BLOCK)),
        [
            pltpu.VMEM((16, *square), F32),
            pltpu.VMEM((16, *square), F32),
            pltpu.VMEM((16, *square), F32),
            pltpu.VMEM((8, 2, *square), BF16),
            pltpu.VMEM((8, *square), F32),
        ],
        [VMEM, SMEM],
    )(gathered, jnp.asarray(np.array(SCALES, np.float32)))
    own = (8, 16, 256)
    x0, r0, image, slots = call(
        start_kernel,
        "start",
        (shape_of(*own), shape_of(*own), shape_of(10, *ext), shape_of(256, 128)),
        [pltpu.VMEM((14, *ext), F32), pltpu.VMEM((12, *ext), F32)],
        [VMEM] * 6 + [SMEM],
    )(low, middle, high, k, diag, y, place)
    gathered = exchange(slots, 1)
    w0, d0, aw0, slots = call(
        first_kernel,
        "first",
        (shape_of(*own), shape_of(*own), shape_of(*own), shape_of(256, 128)),
        [pltpu.VMEM((16, BLOCK), F32), pltpu.VMEM((12, *ext), F32), pltpu.VMEM((10, *ext), F32)],
        [VMEM] * 11 + [SMEM],
    )(gathered, right, left, last, low, middle, high, k, diag, image, r0, place)
    gathered = exchange(slots, 1)
    return call(
        last_kernel,
        "last",
        (shape_of(*own), shape_of(*own)),
        [pltpu.VMEM((16, BLOCK), F32), pltpu.VMEM((10, *ext), F32)],
        [VMEM] * 14 + [SMEM],
    )(gathered, right, left, last, low, middle, high, k, diag, x0, r0, w0, d0, aw0, place)


def solution(mesh):
    split = Mesh(mesh.devices.reshape(8, 2, 4, 4), ("axial_0", "axial_1", "circ_0", "circ_1"))
    placed = P(AXIAL, CIRC, None)
    return jax.shard_map(
        shards,
        mesh=split,
        in_specs=(placed,) * 4,
        out_specs=(placed, placed),
        check_vma=False,
    )
```

time: 1010 us -> 171 us (0.17); the launches traced: 992 us -> 170 us
  other arithmetic: 409 us -> 3.64 us
  matrix products: 235 us -> 0 us
  blocking collectives: 198 us -> 71.2 us
  Pallas kernels: 0 us -> 70.7 us
  local copies, waits for them, and re-layouts: 51.7 us -> 0.78 us
  starting transfers between devices: 50.3 us -> 13.3 us
  between operations: 21 us -> 0.7 us
  waiting for transfers between devices: 22.7 us -> 10.2 us
    another operation x96 -> x2, other arithmetic: 366 us -> 1.6 us  [the longest x1 0.99 us: shards(): jnp.stack([right_side, stiffness, material.astype(F32), groups.astype(F32)])]
    dot_general x238 -> x0, matrix products: 221 us -> none  [the longest x48 49.9 us: backward(): solved = jnp.dot(inverse_now.T, target, precision=PRECISE)]
    all_gather x9 -> x0, blocking collectives: 89.4 us -> none  [gather_in_order(): parts = lax.all_gather(parts, axes[k], axis=0, tiled=True)]
    all_to_all x0 -> x3, blocking collectives: none -> 71.2 us  [exchange(): lax.all_to_all(slots.reshape(256, count, 128), AXIAL_CIRC, 0, 0, tiled=True)]
    pallas_call x0 -> x5, Pallas kernels: none -> 70.7 us  [the longest x1 37.7 us: shards(): call(factor_kernel, 'factor', (shape_of(15, BLOCK, 3 * BLOCK), shape_of(1...]
    psum x8 -> x0, blocking collectives: 66.9 us -> none  [over_axes(): return functools.reduce(lax.psum, axes, array)]
    unnamed x3 -> x0, blocking collectives: 41.6 us -> none
    ppermute x16 -> x4, starting transfers between devices: 43.8 us -> 13.3 us  [the longest x1 5.82 us: shards(): after = lax.ppermute(fields[:, :, :EDGE], CIRC, down)]
  transfers between devices with their start and end apart: 18 -> 4, of which waited for: 8 -> 4; matrix products, arithmetic and copies ran while one was open for 1% -> 0% of each run, Pallas kernels for 0% -> 0%
where the time goes in v1:
time: 171 us; the launch traced here: 170 us
  blocking collectives  71.2 us (42%)
  Pallas kernels  70.7 us (41%)
  starting transfers between devices  13.3 us (8%)
  waiting for transfers between devices  10.2 us (6%)
  other arithmetic  3.64 us (2%)
    all_to_all x3, blocking collectives, exchange(): lax.all_to_all(slots.reshape(256, count, 128), AXIAL_CIRC, 0, 0, tiled=True)  71.2 us
    pallas_call x1, Pallas kernels, shards(): call(factor_kernel, 'factor', (shape_of(15, BLOCK, 3 * BLOCK), shape_of(1...  37.7 us
    pallas_call x1, Pallas kernels, shards(): call(setup_kernel, 'setup', (shape_of(14, 13, *ext), shape_of(12, *ext),...  9.5 us
    pallas_call x1, Pallas kernels, shards(): call(first_kernel, 'first', (shape_of(*own), shape_of(*own), shape_of(*ow...  9.37 us
    pallas_call x1, Pallas kernels, shards(): call(last_kernel, 'last', (shape_of(*own), shape_of(*own)), [pltpu.VMEM((...  8.23 us
    pallas_call x1, Pallas kernels, shards(): call(start_kernel, 'start', (shape_of(*own), shape_of(*own), shape_of(10,...  5.94 us
    ppermute x1, starting transfers between devices, shards(): after = lax.ppermute(fields[:, :, :EDGE], CIRC, down)  5.82 us
    ppermute x1, waiting for transfers between devices, shards(): before = lax.ppermute(fields[:, :, 16 - EDGE:], CIRC, up)  4.96 us
  transfers between devices with their start and end apart: 4, of which 4 were waited for; matrix products, arithmetic and copies ran while one was open for 0% of the time, Pallas kernels for 0%

profile of v1, /device:TPU:1, one launch (start us, length us, event | category | flops | bytes accessed | tf_op | source)
XLA Modules:
  0.0 170.5 jit_solution(15822337699239449797)
XLA Ops:
  0.6 1.0 convert_bitcast_fusion
  1.6 1.0 pad_maximum_fusion.4
  2.6 5.8 %collective-permute-start = (f32[4,8,4,256]{3,2,1,0:T(4,128)S(1)}, f32[4,8,4,256]{3,2,1,0:T(4,128)S(1)}, u32[]{:S(2)}, u32[]{:S(2)}) collective-permute-start(f32[4,8,4,256]{3,2,1,0:T(4,128)S(1)} %get-tuple-element.34), channel_id=1, source_target_pairs={{1,0},{2,1},{3,2},{4,3},{5,4},{6,5},{7,6},{8,7},{9,8},{10,9},{11,1... | collective-permute-start | bytes 393224 | tf_op jit(solution)/shard_map/ppermute | solution.py:670
  8.4 0.0 collective-permute-start.1
  8.4 2.2 %collective-permute-done = f32[4,8,4,256]{3,2,1,0:T(4,128)S(1)} collective-permute-done((f32[4,8,4,256]{3,2,1,0:T(4,128)S(1)}, f32[4,8,4,256]{3,2,1,0:T(4,128)S(1)}, u32[]{:S(2)}, u32[]{:S(2)}) %collective-permute-start) | collective-permute-done | bytes 131104 | tf_op jit(solution)/shard_map/ppermute | solution.py:670
  10.6 5.0 %collective-permute-done.1 = f32[4,8,4,256]{3,2,1,0:T(4,128)S(1)} collective-permute-done((f32[4,8,4,256]{3,2,1,0:T(4,128)S(1)}, f32[4,8,4,256]{3,2,1,0:T(4,128)S(1)}, u32[]{:S(2)}, u32[]{:S(2)}) %collective-permute-start.1) | collective-permute-done | bytes 131104 | tf_op jit(solution)/shard_map/ppermute | solution.py:669
  15.6 1.1 pad_maximum_fusion.mid_ref
  16.6 0.0 copy-start
  16.7 4.0 %collective-permute-start.3 = (f32[4,3,24,256]{3,2,1,0:T(8,128)S(1)}, f32[4,3,24,256]{3,2,1,0:T(8,128)S(1)}, u32[]{:S(2)}, u32[]{:S(2)}) collective-permute-start(f32[4,3,24,256]{3,2,1,0:T(8,128)S(1)} %get-tuple-element.32), channel_id=1, source_target_pairs={{16,0},{32,16},{48,32},{64,48},{80,64},{96,80},{112,96},{128,112},... | collective-permute-start | bytes 884744 | tf_op jit(solution)/shard_map/ppermute | solution.py:674
  20.7 3.4 %collective-permute-start.2 = (f32[4,3,24,256]{3,2,1,0:T(8,128)S(1)}, f32[4,3,24,256]{3,2,1,0:T(8,128)S(1)}, u32[]{:S(2)}, u32[]{:S(2)}) collective-permute-start(f32[4,3,24,256]{3,2,1,0:T(8,128)S(1)} %get-tuple-element.33), channel_id=1, source_target_pairs={{0,16},{16,32},{32,48},{48,64},{64,80},{80,96},{96,112},{112,128},... | collective-permute-start | bytes 884744 | tf_op jit(solution)/shard_map/ppermute | solution.py:673
  24.2 0.6 pad_add_fusion.place_ref
  24.8 1.8 %collective-permute-done.3.high_ref = f32[4,3,24,256]{3,2,1,0:T(8,128)S(1)} collective-permute-done((f32[4,3,24,256]{3,2,1,0:T(8,128)S(1)}, f32[4,3,24,256]{3,2,1,0:T(8,128)S(1)}, u32[]{:S(2)}, u32[]{:S(2)}) %collective-permute-start.3) | collective-permute-done | bytes 294944 | tf_op jit(solution)/shard_map/ppermute | solution.py:674
  26.6 1.2 collective-permute-done.2.low_ref
  27.8 0.0 copy-done
  27.8 0.0 copy-done.1
  27.8 0.7 copy-done.2
  28.6 9.5 %setup.1 = (f32[14,13,24,256]{3,2,1,0:T(8,128)}, f32[12,24,256]{2,1,0:T(8,128)}, f32[1024,128]{1,0:T(8,128)}) custom-call(f32[4,3,24,256]{3,2,1,0:T(8,128)} %copy-done.2, f32[4,8,24,256]{3,2,1,0:T(8,128)} %copy-done, f32[4,3,24,256]{3,2,1,0:T(8,128)} %copy-done.1, f32[16,128]{1,0:T(8,128)} %constant.27.clone.table_ref, s32[2]{0:T(128)} %pad_add_fusion.place_ref), custom_call_target="tpu_custom_call" | custom-call | tf_op jit(solution)/shard_map/setup/pallas_call | solution.py:678
  38.1 32.2 %all_to_all.15 = f32[256,4,128]{2,1,0:T(4,128)} all-to-all(f32[256,4,128]{2,1,0:T(4,128)} %bitcast.21), channel_id=1, replica_groups=mesh['axial_0'=8,'axial_1'=2,'circ_0'=4,'circ_1'=4] {'axial_0','axial_1'..., dimensions={0} | all-to-all | bytes 1048576 | tf_op jit(solution)/shard_map/all_to_all | solution.py:660
  70.2 37.7 %factor.1 = (f32[15,128,384]{2,1,0:T(8,128)}, f32[15,256,128]{2,1,0:T(8,128)}, f32[128,128]{1,0:T(8,128)}, f32[16,128]{1,0:T(8,128)}) custom-call(f32[1024,128]{1,0:T(8,128)} %bitcast.18, f32[9]{0:T(128)} %constant.28.clone.scale_ref), custom_call_target="tpu_custom_call" | custom-call | tf_op jit(solution)/shard_map/factor/pallas_call | solution.py:687
  107.9 5.9 %start.1 = (f32[8,16,256]{2,1,0:T(8,128)}, f32[8,16,256]{2,1,0:T(8,128)}, f32[10,24,256]{2,1,0:T(8,128)}, f32[256,128]{1,0:T(8,128)}) custom-call(f32[4,3,24,256]{3,2,1,0:T(8,128)} %copy-done.2, f32[4,8,24,256]{3,2,1,0:T(8,128)} %copy-done, f32[4,3,24,256]{3,2,1,0:T(8,128)} %copy-done.1, f32[14,13,24,256]{3,2,1,0:T(8,128)} %get-tuple-element.17.k_ref, ...), custom_call_target="tpu_custom_call" | custom-call | tf_op jit(solution)/shard_map/start/pallas_call | solution.py:701
  113.8 19.3 %all_to_all.16 = f32[256,1,128]{2,1,0:T(1,128)} all-to-all(f32[256,1,128]{2,1,0:T(1,128)} %bitcast.27), channel_id=1, replica_groups=mesh['axial_0'=8,'axial_1'=2,'circ_0'=4,'circ_1'=4] {'axial_0','axial_1'..., dimensions={0} | all-to-all | bytes 262144 | tf_op jit(solution)/shard_map/all_to_all | solution.py:660
  133.1 9.4 %first.1 = (f32[8,16,256]{2,1,0:T(8,128)}, f32[8,16,256]{2,1,0:T(8,128)}, f32[8,16,256]{2,1,0:T(8,128)}, f32[256,128]{1,0:T(8,128)}) custom-call(f32[256,128]{1,0:T(8,128)} %bitcast.20, f32[15,128,384]{2,1,0:T(8,128)} %get-tuple-element.22.right_ref, f32[15,256,128]{2,1,0:T(8,128)} %get-tuple-element.23.left_ref, f32[128,128]{1,0:T(8,128)} %get-tuple-element.24.last_ref, ...), custom_call_target="tpu_custom_call" | custom-call | tf_op jit(solution)/shard_map/first/pallas_call | solution.py:709
  142.5 19.8 %all_to_all.17 = f32[256,1,128]{2,1,0:T(1,128)} all-to-all(f32[256,1,128]{2,1,0:T(1,128)} %bitcast.26), channel_id=1, replica_groups=mesh['axial_0'=8,'axial_1'=2,'circ_0'=4,'circ_1'=4] {'axial_0','axial_1'..., dimensions={0} | all-to-all | bytes 262144 | tf_op jit(solution)/shard_map/all_to_all | solution.py:660
  162.2 8.2 %last.1 = (f32[8,16,256]{2,1,0:T(8,128)}, f32[8,16,256]{2,1,0:T(8,128)}) custom-call(f32[256,128]{1,0:T(8,128)} %bitcast.19, f32[15,128,384]{2,1,0:T(8,128)} %get-tuple-element.22.right_ref, f32[15,256,128]{2,1,0:T(8,128)} %get-tuple-element.23.left_ref, f32[128,128]{1,0:T(8,128)} %get-tuple-element.24.last_ref, f32[4,3,24,256]{3,2,1,0:T(8,128)} %copy-done.2, ...), custom_call_target="tpu_custom_call" | custom-call | tf_op jit(solution)/shard_map/last/pallas_call | solution.py:717
  (3 shorter events, 0.0 us)
Async XLA Ops:
  2.6 8.0 %collective-permute-start = (f32[4,8,4,256]{3,2,1,0:T(4,128)S(1)}, f32[4,8,4,256]{3,2,1,0:T(4,128)S(1)}, u32[]{:S(2)}, u32[]{:S(2)}) collective-permute-start(f32[4,8,4,256]{3,2,1,0:T(4,128)S(1)} %get-tuple-element.34), channel_id=1, source_target_pairs={{1,0},{2,1},{3,2},{4,3},{5,4},{6,5},{7,6},{8,7},{9,8},{10,9},{11,1... | collective-permute-start | bytes 393224 | tf_op jit(solution)/shard_map/ppermute | solution.py:670
  8.4 7.1 %collective-permute-start.1 = (f32[4,8,4,256]{3,2,1,0:T(4,128)S(1)}, f32[4,8,4,256]{3,2,1,0:T(4,128)S(1)}, u32[]{:S(2)}, u32[]{:S(2)}) collective-permute-start(f32[4,8,4,256]{3,2,1,0:T(4,128)S(1)} %get-tuple-element.35), channel_id=1, source_target_pairs={{0,1},{1,2},{2,3},{3,4},{4,5},{5,6},{6,7},{7,8},{8,9},{9,10},{10,1... | collective-permute-start | bytes 393224 | tf_op jit(solution)/shard_map/ppermute | solution.py:669
  16.6 11.2 %copy-start = (f32[4,8,24,256]{3,2,1,0:T(8,128)}, f32[4,8,24,256]{3,2,1,0:T(8,128)S(1)}, u32[]{:S(2)}) copy-start(f32[4,8,24,256]{3,2,1,0:T(8,128)S(1)} %pad_maximum_fusion.mid_ref) | copy-start | bytes 2359300
  16.7 9.9 %collective-permute-start.3 = (f32[4,3,24,256]{3,2,1,0:T(8,128)S(1)}, f32[4,3,24,256]{3,2,1,0:T(8,128)S(1)}, u32[]{:S(2)}, u32[]{:S(2)}) collective-permute-start(f32[4,3,24,256]{3,2,1,0:T(8,128)S(1)} %get-tuple-element.32), channel_id=1, source_target_pairs={{16,0},{32,16},{48,32},{64,48},{80,64},{96,80},{112,96},{128,112},... | collective-permute-start | bytes 884744 | tf_op jit(solution)/shard_map/ppermute | solution.py:674
  20.7 7.1 %collective-permute-start.2 = (f32[4,3,24,256]{3,2,1,0:T(8,128)S(1)}, f32[4,3,24,256]{3,2,1,0:T(8,128)S(1)}, u32[]{:S(2)}, u32[]{:S(2)}) collective-permute-start(f32[4,3,24,256]{3,2,1,0:T(8,128)S(1)} %get-tuple-element.33), channel_id=1, source_target_pairs={{0,16},{16,32},{32,48},{48,64},{64,80},{80,96},{96,112},{112,128},... | collective-permute-start | bytes 884744 | tf_op jit(solution)/shard_map/ppermute | solution.py:673
  26.6 1.2 copy-start.1
  27.8 0.7 copy-start.2

commit v2 on v1

--- a/solution.py
+++ b/solution.py
@@ -185,7 +185,7 @@
 
 def setup_kernel(low_ref, mid_ref, high_ref, table_ref, place_ref, k_ref, diag_ref, slot_ref, label_ref):
     for plane in range(-DEPTH, 8 + DEPTH):
-        stiff = piece(low_ref, mid_ref, high_ref, 1, plane)
+        stiff = masked(piece(low_ref, mid_ref, high_ref, 1, plane), present_flags(place_ref, plane))
         kind = piece(low_ref, mid_ref, high_ref, 2, plane).astype(jnp.int32)
         for j in range(13):
             row = jnp.broadcast_to(table_ref[j : j + 1, :], (8, 128))
@@ -305,7 +305,7 @@
     shape = (8, 64)
     joiner = jnp.where(lanes(shape) // 16 == sublanes(shape) % 4, 1.0, 0.0).astype(BF16)
     slot = sum(dot(joiner, part) for part in split3(kept))
-    for device in range(128):
+    for device in range(8):
         slot_ref[8 * device : 8 * device + 8, :] = slot
 
 
@@ -362,11 +362,17 @@
     return high, (values - high.astype(F32)).astype(BF16)
 
 
-def dot_split(a, b):
-    return dot(a[0], b[0]) + (dot(a[0], b[1]) + dot(a[1], b[0]))
-
-
-def invert(blocks, scale_ref, s_ref, x_ref):
+def left_stack(values):
+    high, low = split2(values)
+    return jnp.concatenate([high, high, low], axis=1)
+
+
+def right_stack(values):
+    high, low = split2(values)
+    return jnp.concatenate([high, low, high], axis=0)
+
+
+def invert(blocks, scale_ref, x_ref, p_ref):
     shape = (BLOCK, BLOCK)
     eye = jnp.where(lanes(shape) == sublanes(shape), 1.0, 0.0).astype(F32)
     for q, block in enumerate(blocks):
@@ -375,86 +381,110 @@
         down = 1.0 / jnp.sum(kept, axis=1, keepdims=True)
         c = 0.5 * SCALES[0]
         x_ref[q] = (2.0 * c * eye - (c * c) * (block * down)) * across
-        high, low = split2(block)
-        s_ref[q, 0] = high
-        s_ref[q, 1] = low
+    for q, block in enumerate(blocks):
+        p_ref[q] = dot(left_stack(block), right_stack(x_ref[q]))
 
     def step(k, carry):
         c = scale_ref[k]
         for q in range(len(blocks)):
-            x = split2(x_ref[q])
-            product = dot_split((s_ref[q, 0], s_ref[q, 1]), x)
-            x_ref[q] = dot_split(x, split2((2.0 * c) * eye - (c * c) * product))
+            x = x_ref[q]
+            p = p_ref[q]
+            both = jnp.concatenate([left_stack(p), left_stack(x)], axis=0)
+            product = dot(both, right_stack(p))
+            p_ref[q] = (2.0 * c) * p - (c * c) * product[:BLOCK]
+            x_ref[q] = (2.0 * c) * x - (c * c) * product[BLOCK:]
         return carry
 
-    lax.fori_loop(1, len(SCALES) - 1, step, 0)
-    out = []
-    for q, block in enumerate(blocks):
-        x = x_ref[q]
-        left = eye - dot_high(block, x)
-        out.append(x + dot_split(split2(x), split2(left)))
-    return out
+    lax.fori_loop(1, len(SCALES) - 2, step, 0)
+    values = [x_ref[q] for q in range(len(blocks))]
+    rests = [eye - dot(left_stack(s), right_stack(x)) for s, x in zip(blocks, values)]
+    values = [x + dot(x.astype(BF16), r.astype(BF16)) for x, r in zip(values, rests)]
+    rests = [eye - dot_high(s, x) for s, x in zip(blocks, values)]
+    return [x + dot(x.astype(BF16), r.astype(BF16)) for x, r in zip(values, rests)]
+
+
+def turned(values):
+    shape = (BLOCK, BLOCK)
+    eye = jnp.where(lanes(shape) == sublanes(shape), 1.0, 0.0).astype(BF16)
+    return sum(dot(eye, part, ((1,), (1,))) for part in split3(values))
+
+
+def gather_lanes(values, spot):
+    return jnp.take_along_axis(values, spot, axis=1, mode="promise_in_bounds")
+
+
+def unpack_coarse(slots_ref, d_ref, b_ref, f_ref):
+    for top in (0, 8):
+        shape = (8, BLOCK)
+        device = sublanes(shape) + top
+        ring = lanes(shape) % 16
+        column = lanes(shape) // 16
+        side = (ring - device + 17) % 16
+        near = side < 3
+        spot = jnp.minimum(side, 2) * 8 + column
+        for s in range(16):
+            load = None
+            for pair in range(4):
+                values = slots_ref[pl.ds(64 * top + 4 * s + pair, 8, stride=64), :]
+                for half in (0, 1):
+                    row = 16 * (2 * pair + half) + top
+                    for r, target in enumerate((d_ref, b_ref)):
+                        if r == 1 and s == 15:
+                            continue
+                        got = gather_lanes(values, spot + (64 * half + 24 * r))
+                        target[s, row : row + 8, :] = jnp.where(near, got, 0.0)
+                got = gather_lanes(values, 48 + 64 * (column % 2))
+                mine = jnp.logical_and(ring == device, column // 2 == pair)
+                term = jnp.where(mine, got, 0.0)
+                load = term if load is None else load + term
+            load = jnp.sum(load, axis=0, keepdims=True)
+            if top == 0:
+                f_ref[s : s + 1, :] = load
+            else:
+                f_ref[s : s + 1, :] = f_ref[s : s + 1, :] + load
 
 
 def factor_kernel(
-    slots_ref, scale_ref, right_ref, left_ref, last_ref, y_ref, d_ref, b_ref, bt_ref, s_ref, x_ref
+    slots_ref, scale_ref, right_ref, left_ref, last_ref, y_ref, d_ref, b_ref, x_ref, p_ref, f_ref
 ):
-    shape = (256, BLOCK)
-    device = sublanes(shape) % 16
-    ring = lanes(shape) % 16
-    near = [(device + c + 15) % 16 == ring for c in range(3)]
-    coarse_rhs = None
-    for pair in range(4):
-        values = split3(slots_ref[pl.ds(pair, 256, stride=4), :])
-        for half in (0, 1):
-            label = 2 * pair + half
-            shape = (128, 7 * BLOCK)
-            group = lanes(shape) // BLOCK
-            column = jnp.where(group < 6, group * 8 + (lanes(shape) % BLOCK) // 16, 48) + 64 * half
-            chooser = jnp.where(sublanes(shape) == column, 1.0, 0.0).astype(BF16)
-            wide = sum(dot(part, chooser) for part in values)
-            for r, target in enumerate((d_ref, b_ref)):
-                total = None
-                for c in range(3):
-                    at = (3 * r + c) * BLOCK
-                    term = jnp.where(near[c], wide[:, at : at + BLOCK], 0.0)
-                    total = term if total is None else total + term
-                target[:, 16 * label : 16 * label + 16, :] = total.reshape(16, 16, BLOCK)
-            mine = jnp.logical_and(device == ring, lanes((256, BLOCK)) // 16 == label)
-            term = jnp.where(mine, wide[:, 6 * BLOCK :], 0.0)
-            coarse_rhs = term if coarse_rhs is None else coarse_rhs + term
-    coarse_rhs = jnp.sum(coarse_rhs.reshape(16, 16, BLOCK), axis=1)
+    unpack_coarse(slots_ref, d_ref, b_ref, f_ref)
     b_ref[15] = jnp.zeros((BLOCK, BLOCK), F32)
     for i in range(16):
-        d_ref[i] = d_ref[i] + d_ref[i].T
-        bt_ref[i] = b_ref[i].T
+        d_ref[i] = d_ref[i] + turned(d_ref[i])
     begin = 0
     stride = 1
     while stride < 16:
         count = 8 // stride
         odd = [(2 * q + 1) * stride for q in range(count)]
-        inverses = invert([d_ref[i] for i in odd], scale_ref, s_ref, x_ref)
+        inverses = invert([d_ref[i] for i in odd], scale_ref, x_ref, p_ref)
+        ups = [
+            dot_high(inverse, b_ref[i - stride], ((1,), (1,))) for i, inverse in zip(odd, inverses)
+        ]
+        downs = [dot_high(inverse, b_ref[i]) for i, inverse in zip(odd, inverses)]
+        products = [jnp.concatenate(pair, axis=1) for pair in zip(ups, downs)]
+        for q in range(count):
+            right_ref[begin + q, :, :BLOCK] = inverses[q]
+            right_ref[begin + q, :, BLOCK:] = products[q]
+        grams = [dot_high(b_ref[i - stride], product) for i, product in zip(odd, products)]
+        for q in range(count):
+            left_ref[begin + q, :BLOCK, :] = turned(ups[q])
+            left_ref[begin + q, BLOCK:, :] = turned(downs[q])
+        afters = [
+            dot_high(left_ref[begin + q, BLOCK:, :], b_ref[i])
+            for q, i in enumerate(odd)
+            if i + stride < 16
+        ]
         for q, i in enumerate(odd):
-            before = i - stride
-            after = i + stride
-            inverse = inverses[q]
-            c_rows = jnp.concatenate([b_ref[before], bt_ref[i]], axis=0)
-            c_cols = jnp.concatenate([bt_ref[before], b_ref[i]], axis=1)
-            left_ref[begin + q] = dot_high(c_rows, inverse)
-            products = dot_high(inverse, c_cols)
-            right_ref[begin + q, :, :BLOCK] = inverse
-            right_ref[begin + q, :, BLOCK:] = products
-            gram = dot_high(c_rows, products)
-            d_ref[before] = d_ref[before] - gram[:BLOCK, :BLOCK]
-            b_ref[before] = -gram[:BLOCK, BLOCK:]
-            bt_ref[before] = -gram[BLOCK:, :BLOCK]
-            if after < 16:
-                d_ref[after] = d_ref[after] - gram[BLOCK:, BLOCK:]
+            change = grams[q][:, :BLOCK]
+            if q > 0:
+                change = change + afters[q - 1]
+            d_ref[i - stride] = d_ref[i - stride] - change
+            b_ref[i - stride] = -grams[q][:, BLOCK:]
         begin += count
         stride *= 2
-    (last,) = invert([d_ref[0]], scale_ref, s_ref, x_ref)
+    (last,) = invert([d_ref[0]], scale_ref, x_ref, p_ref)
     last_ref[...] = last
-    y_ref[...] = coarse_solve(coarse_rhs, right_ref, left_ref, last_ref)
+    y_ref[...] = coarse_solve(f_ref[...], right_ref, left_ref, last_ref)
 
 
 def spread_field(y_ref, place_ref, label_of, plane):
@@ -632,14 +662,13 @@
 
 VMEM = pl.BlockSpec(memory_space=pltpu.VMEM)
 SMEM = pl.BlockSpec(memory_space=pltpu.SMEM)
-BIG = pltpu.CompilerParams(vmem_limit_bytes=56 * 1024 * 1024)
 
 
 def shape_of(*dims):
     return jax.ShapeDtypeStruct(dims, F32)
 
 
-def call(kernel, name, outs, scratch, in_specs):
+def call(kernel, name, outs, scratch, in_specs, mib):
     return pl.pallas_call(
         kernel,
         name=name,
@@ -647,13 +676,20 @@
         in_specs=in_specs,
         out_specs=tuple(VMEM for _ in outs),
         scratch_shapes=scratch,
-        compiler_params=BIG,
+        compiler_params=pltpu.CompilerParams(vmem_limit_bytes=mib * 1024 * 1024),
     )
 
 
-def ring_pairs(peers, wrap):
-    up = [(i, (i + 1) % peers) for i in range(peers if wrap else peers - 1)]
+def ring_pairs(peers):
+    up = [(i, (i + 1) % peers) for i in range(peers)]
     return up, [(j, i) for i, j in up]
+
+
+def exchange_all(slots, count):
+    width = slots.shape[0] // 16
+    held = lax.all_to_all(slots.reshape(16, width, 128), AXIAL, 0, 0, tiled=True)
+    held = jnp.broadcast_to(held.reshape(1, 16 * width, 128), (16, 16 * width, 128))
+    return lax.all_to_all(held, CIRC, 0, 0, tiled=True).reshape(256 * width, 128)
 
 
 def exchange(slots, count):
@@ -665,11 +701,10 @@
 def shards(right_side, stiffness, material, groups):
     place = jnp.stack([lax.axis_index(AXIAL), lax.axis_index(CIRC)]).astype(jnp.int32)
     fields = jnp.stack([right_side, stiffness, material.astype(F32), groups.astype(F32)])
-    up, down = ring_pairs(16, True)
+    up, down = ring_pairs(16)
     before = lax.ppermute(fields[:, :, 16 - EDGE :], CIRC, up)
     after = lax.ppermute(fields[:, :, :EDGE], CIRC, down)
     middle = jnp.concatenate([fields, after, before], axis=2)
-    up, down = ring_pairs(16, False)
     low = lax.ppermute(middle[:, 8 - DEPTH :], AXIAL, up)
     high = lax.ppermute(middle[:, :DEPTH], AXIAL, down)
     table = np.zeros((16, 128), np.float32)
@@ -678,11 +713,12 @@
     k, diag, slots = call(
         setup_kernel,
         "setup",
-        (shape_of(14, 13, *ext), shape_of(12, *ext), shape_of(1024, 128)),
+        (shape_of(14, 13, *ext), shape_of(12, *ext), shape_of(64, 128)),
         [pltpu.VMEM((9, 9, 16, 256), F32)],
         [VMEM, VMEM, VMEM, VMEM, SMEM],
+        24,
     )(low, middle, high, jnp.asarray(table), place)
-    gathered = exchange(slots, 4)
+    gathered = exchange_all(slots, 4)
     square = (BLOCK, BLOCK)
     right, left, last, y = call(
         factor_kernel,
@@ -691,11 +727,12 @@
         [
             pltpu.VMEM((16, *square), F32),
             pltpu.VMEM((16, *square), F32),
-            pltpu.VMEM((16, *square), F32),
-            pltpu.VMEM((8, 2, *square), BF16),
             pltpu.VMEM((8, *square), F32),
+            pltpu.VMEM((8, *square), F32),
+            pltpu.VMEM((16, BLOCK), F32),
         ],
         [VMEM, SMEM],
+        24,
     )(gathered, jnp.asarray(np.array(SCALES, np.float32)))
     own = (8, 16, 256)
     x0, r0, image, slots = call(
@@ -704,6 +741,7 @@
         (shape_of(*own), shape_of(*own), shape_of(10, *ext), shape_of(256, 128)),
         [pltpu.VMEM((14, *ext), F32), pltpu.VMEM((12, *ext), F32)],
         [VMEM] * 6 + [SMEM],
+        24,
     )(low, middle, high, k, diag, y, place)
     gathered = exchange(slots, 1)
     w0, d0, aw0, slots = call(
@@ -712,6 +750,7 @@
         (shape_of(*own), shape_of(*own), shape_of(*own), shape_of(256, 128)),
         [pltpu.VMEM((16, BLOCK), F32), pltpu.VMEM((12, *ext), F32), pltpu.VMEM((10, *ext), F32)],
         [VMEM] * 11 + [SMEM],
+        24,
     )(gathered, right, left, last, low, middle, high, k, diag, image, r0, place)
     gathered = exchange(slots, 1)
     return call(
@@ -720,6 +759,7 @@
         (shape_of(*own), shape_of(*own)),
         [pltpu.VMEM((16, BLOCK), F32), pltpu.VMEM((10, *ext), F32)],
         [VMEM] * 14 + [SMEM],
+        24,
     )(gathered, right, left, last, low, middle, high, k, diag, x0, r0, w0, d0, aw0, place)
 
 

time: 171 us -> 141 us (0.82)
  Pallas kernels: 70.7 us -> 46.9 us
  starting transfers between devices: 13.3 us -> 9.49 us
  blocking collectives: 71.2 us -> 68.5 us
    all_to_all x3 -> x2, blocking collectives: 71.2 us -> 38.6 us  [exchange(): lax.all_to_all(slots.reshape(256, count, 128), AXIAL_CIRC, 0, 0, tiled=True)]
    all_to_all x0 -> x2, blocking collectives: none -> 30 us  [the longest x1 17.1 us: exchange_all(): lax.all_to_all(slots.reshape(16, width, 128), AXIAL, 0, 0, tiled=True)]
    pallas_call x1, Pallas kernels: 37.7 us -> 26.6 us  [shards(): call(factor_kernel, 'factor', (shape_of(15, BLOCK, 3 * BLOCK), shape_of(1...]
    pallas_call x1, Pallas kernels: 9.37 us -> 5.4 us  [shards(): call(first_kernel, 'first', (shape_of(*own), shape_of(*own), shape_of(*ow...]
    pallas_call x1, Pallas kernels: 8.23 us -> 4.63 us  [shards(): call(last_kernel, 'last', (shape_of(*own), shape_of(*own)), [pltpu.VMEM((...]
    pallas_call x1, Pallas kernels: 9.5 us -> 6.69 us  [shards(): call(setup_kernel, 'setup', (shape_of(14, 13, *ext), shape_of(12, *ext),...]
    ppermute x1, waiting for transfers between devices: 1.85 us -> 4.31 us  [shards(): high = lax.ppermute(middle[:, :DEPTH], AXIAL, down)]
    pallas_call x1, Pallas kernels: 5.94 us -> 3.62 us  [shards(): call(start_kernel, 'start', (shape_of(*own), shape_of(*own), shape_of(10,...]
  transfers between devices with their start and end apart: 4 -> 4, of which waited for: 4 -> 3; matrix products, arithmetic and copies ran while one was open for 0% -> 0% of each run, Pallas kernels for 0% -> 0%
where the time goes in v2:
time: 141 us; the launch traced here: 140 us
  blocking collectives  68.5 us (49%)
  Pallas kernels  46.9 us (33%)
  waiting for transfers between devices  11.4 us (8%)
  starting transfers between devices  9.49 us (7%)
  other arithmetic  3.1 us (2%)
    all_to_all x2, blocking collectives, exchange(): lax.all_to_all(slots.reshape(256, count, 128), AXIAL_CIRC, 0, 0, tiled=True)  38.6 us
    pallas_call x1, Pallas kernels, shards(): call(factor_kernel, 'factor', (shape_of(15, BLOCK, 3 * BLOCK), shape_of(1...  26.6 us
    all_to_all x1, blocking collectives, exchange_all(): lax.all_to_all(slots.reshape(16, width, 128), AXIAL, 0, 0, tiled=True)  17.1 us
    all_to_all x1, blocking collectives, exchange_all(): lax.all_to_all(held, CIRC, 0, 0, tiled=True).reshape(256 * width, 128)  12.9 us
    pallas_call x1, Pallas kernels, shards(): call(setup_kernel, 'setup', (shape_of(14, 13, *ext), shape_of(12, *ext),...  6.69 us
    ppermute x1, starting transfers between devices, shards(): after = lax.ppermute(fields[:, :, :EDGE], CIRC, down)  5.82 us
    pallas_call x1, Pallas kernels, shards(): call(first_kernel, 'first', (shape_of(*own), shape_of(*own), shape_of(*ow...  5.4 us
    ppermute x1, waiting for transfers between devices, shards(): before = lax.ppermute(fields[:, :, 16 - EDGE:], CIRC, up)  4.96 us
  transfers between devices with their start and end apart: 4, of which 3 were waited for; matrix products, arithmetic and copies ran while one was open for 0% of the time, Pallas kernels for 0%

profile of v2, /device:TPU:1, one launch (start us, length us, event | category | flops | bytes accessed | tf_op | source)
XLA Modules:
  0.0 140.3 jit_solution(2269870755591586295)
XLA Ops:
  0.6 0.0 copy-start
  0.6 1.0 convert_bitcast_fusion
  1.6 1.0 pad_maximum_fusion.4
  2.6 0.0 copy-start.1
  2.6 5.8 %collective-permute-start = (f32[4,8,4,256]{3,2,1,0:T(4,128)S(1)}, f32[4,8,4,256]{3,2,1,0:T(4,128)S(1)}, u32[]{:S(2)}, u32[]{:S(2)}) collective-permute-start(f32[4,8,4,256]{3,2,1,0:T(4,128)S(1)} %get-tuple-element.34), channel_id=1, source_target_pairs={{1,0},{2,1},{3,2},{4,3},{5,4},{6,5},{7,6},{8,7},{9,8},{10,9},{11,1... | collective-permute-start | bytes 393224 | tf_op jit(solution)/shard_map/ppermute | solution.py:706
  8.5 0.0 collective-permute-start.1
  8.5 2.2 %collective-permute-done = f32[4,8,4,256]{3,2,1,0:T(4,128)S(1)} collective-permute-done((f32[4,8,4,256]{3,2,1,0:T(4,128)S(1)}, f32[4,8,4,256]{3,2,1,0:T(4,128)S(1)}, u32[]{:S(2)}, u32[]{:S(2)}) %collective-permute-start) | collective-permute-done | bytes 131104 | tf_op jit(solution)/shard_map/ppermute | solution.py:706
  10.6 5.0 %collective-permute-done.1 = f32[4,8,4,256]{3,2,1,0:T(4,128)S(1)} collective-permute-done((f32[4,8,4,256]{3,2,1,0:T(4,128)S(1)}, f32[4,8,4,256]{3,2,1,0:T(4,128)S(1)}, u32[]{:S(2)}, u32[]{:S(2)}) %collective-permute-start.1) | collective-permute-done | bytes 131104 | tf_op jit(solution)/shard_map/ppermute | solution.py:705
  15.6 1.1 pad_maximum_fusion.mid_ref
  16.7 2.1 %collective-permute-start.3 = (f32[4,3,24,256]{3,2,1,0:T(8,128)S(1)}, f32[4,3,24,256]{3,2,1,0:T(8,128)S(1)}, u32[]{:S(2)}, u32[]{:S(2)}) collective-permute-start(f32[4,3,24,256]{3,2,1,0:T(8,128)S(1)} %get-tuple-element.32), channel_id=1, source_target_pairs={{16,0},{32,16},{48,32},{64,48},{80,64},{96,80},{112,96},{128,112},... | collective-permute-start | bytes 884744 | tf_op jit(solution)/shard_map/ppermute | solution.py:709
  18.8 1.5 %collective-permute-start.2 = (f32[4,3,24,256]{3,2,1,0:T(8,128)S(1)}, f32[4,3,24,256]{3,2,1,0:T(8,128)S(1)}, u32[]{:S(2)}, u32[]{:S(2)}) collective-permute-start(f32[4,3,24,256]{3,2,1,0:T(8,128)S(1)} %get-tuple-element.33), channel_id=1, source_target_pairs={{0,16},{16,32},{32,48},{48,64},{64,80},{80,96},{96,112},{112,128},... | collective-permute-start | bytes 884744 | tf_op jit(solution)/shard_map/ppermute | solution.py:708
  20.4 0.1 pad_add_fusion.place_ref
  20.5 4.3 %collective-permute-done.3.high_ref = f32[4,3,24,256]{3,2,1,0:T(8,128)S(1)} collective-permute-done((f32[4,3,24,256]{3,2,1,0:T(8,128)S(1)}, f32[4,3,24,256]{3,2,1,0:T(8,128)S(1)}, u32[]{:S(2)}, u32[]{:S(2)}) %collective-permute-start.3) | collective-permute-done | bytes 294944 | tf_op jit(solution)/shard_map/ppermute | solution.py:709
  24.8 0.0 collective-permute-done.2.low_ref
  24.8 0.0 copy-done
  24.8 6.7 %setup.1 = (f32[14,13,24,256]{3,2,1,0:T(8,128)S(1)}, f32[12,24,256]{2,1,0:T(8,128)S(1)}, f32[64,128]{1,0:T(8,128)S(1)}) custom-call(f32[4,3,24,256]{3,2,1,0:T(8,128)S(1)} %collective-permute-done.2.low_ref, f32[4,8,24,256]{3,2,1,0:T(8,128)S(1)} %pad_maximum_fusion.mid_ref, f32[4,3,24,256]{3,2,1,0:T(8,128)S(1)} %collective-permute-done.3.high_ref, ...), custom_call_target="tpu_custom_call" | custom-call | tf_op jit(solution)/shard_map/setup/pallas_call | solution.py:713
  31.5 17.1 %all_to_all.20 = f32[16,4,128]{2,1,0:T(4,128)S(1)} all-to-all(f32[16,4,128]{2,1,0:T(4,128)S(1)} %bitcast.24), channel_id=1, replica_groups=mesh['axial_0'=8,'axial_1'=2,'circ_0'=4,'circ_1'=4] {'axial_0','axial_1'}, dimensions={0} | all-to-all | bytes 65536 | tf_op jit(solution)/shard_map/all_to_all | solution.py:690
  48.6 12.9 %all_to_all.21 = f32[16,64,128]{2,1,0:T(8,128)S(1)} all-to-all(f32[16,64,128]{2,1,0:T(8,128)S(1)} %broadcast_in_dim.8), channel_id=1, replica_groups=mesh['axial_0'=8,'axial_1'=2,'circ_0'=4,'circ_1'=4] {'circ_0','circ_1'}, dimensions={0} | all-to-all | bytes 1048576 | tf_op jit(solution)/shard_map/all_to_all | solution.py:692
  61.5 26.6 %factor.1 = (f32[15,128,384]{2,1,0:T(8,128)S(1)}, f32[15,256,128]{2,1,0:T(8,128)S(1)}, f32[128,128]{1,0:T(8,128)S(1)}, f32[16,128]{1,0:T(8,128)S(1)}) custom-call(f32[1024,128]{1,0:T(8,128)S(1)} %bitcast.19, f32[9]{0:T(128)S(1)} %copy-done.1), custom_call_target="tpu_custom_call" | custom-call | tf_op jit(solution)/shard_map/factor/pallas_call | solution.py:723
  88.1 3.6 %start.1 = (f32[8,16,256]{2,1,0:T(8,128)S(1)}, f32[8,16,256]{2,1,0:T(8,128)S(1)}, f32[10,24,256]{2,1,0:T(8,128)S(1)}, f32[256,128]{1,0:T(8,128)S(1)}) custom-call(f32[4,3,24,256]{3,2,1,0:T(8,128)S(1)} %collective-permute-done.2.low_ref, f32[4,8,24,256]{3,2,1,0:T(8,128)S(1)} %pad_maximum_fusion.mid_ref, ...), custom_call_target="tpu_custom_call" | custom-call | tf_op jit(solution)/shard_map/start/pallas_call | solution.py:738
  91.7 20.1 %all_to_all.22 = f32[256,1,128]{2,1,0:T(1,128)S(1)} all-to-all(f32[256,1,128]{2,1,0:T(1,128)S(1)} %bitcast.23), channel_id=1, replica_groups=mesh['axial_0'=8,'axial_1'=2,'circ_0'=4,'circ_1'=4] {'axial_0','axial_1'..., dimensions={0} | all-to-all | bytes 262144 | tf_op jit(solution)/shard_map/all_to_all | solution.py:696
  111.8 5.4 %first.1 = (f32[8,16,256]{2,1,0:T(8,128)S(1)}, f32[8,16,256]{2,1,0:T(8,128)S(1)}, f32[8,16,256]{2,1,0:T(8,128)S(1)}, f32[256,128]{1,0:T(8,128)S(1)}) custom-call(f32[256,128]{1,0:T(8,128)S(1)} %bitcast.21, f32[15,128,384]{2,1,0:T(8,128)S(1)} %get-tuple-element.22.right_ref, f32[15,256,128]{2,1,0:T(8,128)S(1)} %get-tuple-element.23.left_ref, ...), custom_call_target="tpu_custom_call" | custom-call | tf_op jit(solution)/shard_map/first/pallas_call | solution.py:747
  117.2 18.4 %all_to_all.23 = f32[256,1,128]{2,1,0:T(1,128)S(1)} all-to-all(f32[256,1,128]{2,1,0:T(1,128)S(1)} %bitcast.22), channel_id=1, replica_groups=mesh['axial_0'=8,'axial_1'=2,'circ_0'=4,'circ_1'=4] {'axial_0','axial_1'..., dimensions={0} | all-to-all | bytes 262144 | tf_op jit(solution)/shard_map/all_to_all | solution.py:696
  135.7 4.6 %last.1 = (f32[8,16,256]{2,1,0:T(8,128)}, f32[8,16,256]{2,1,0:T(8,128)}) custom-call(f32[256,128]{1,0:T(8,128)S(1)} %bitcast.20, f32[15,128,384]{2,1,0:T(8,128)S(1)} %get-tuple-element.22.right_ref, f32[15,256,128]{2,1,0:T(8,128)S(1)} %get-tuple-element.23.left_ref, f32[128,128]{1,0:T(8,128)S(1)} %get-tuple-element.24.last_ref, ...), custom_call_target="tpu_custom_call" | custom-call | tf_op jit(solution)/shard_map/last/pallas_call | solution.py:756
  (3 shorter events, 0.1 us)
Async XLA Ops:
  0.6 24.1 %copy-start = (f32[16,128]{1,0:T(8,128)S(1)}, f32[16,128]{1,0:T(8,128)}, u32[]{:S(2)}) copy-start(f32[16,128]{1,0:T(8,128)} %constant.27.clone.table_ref) | copy-start | bytes 24580
  2.6 58.9 %copy-start.1 = (f32[9]{0:T(128)S(1)}, f32[9]{0:T(128)}, u32[]{:S(2)}) copy-start(f32[9]{0:T(128)} %constant.28.clone.scale_ref) | copy-start | bytes 112
  2.6 8.0 %collective-permute-start = (f32[4,8,4,256]{3,2,1,0:T(4,128)S(1)}, f32[4,8,4,256]{3,2,1,0:T(4,128)S(1)}, u32[]{:S(2)}, u32[]{:S(2)}) collective-permute-start(f32[4,8,4,256]{3,2,1,0:T(4,128)S(1)} %get-tuple-element.34), channel_id=1, source_target_pairs={{1,0},{2,1},{3,2},{4,3},{5,4},{6,5},{7,6},{8,7},{9,8},{10,9},{11,1... | collective-permute-start | bytes 393224 | tf_op jit(solution)/shard_map/ppermute | solution.py:706
  8.5 7.1 %collective-permute-start.1 = (f32[4,8,4,256]{3,2,1,0:T(4,128)S(1)}, f32[4,8,4,256]{3,2,1,0:T(4,128)S(1)}, u32[]{:S(2)}, u32[]{:S(2)}) collective-permute-start(f32[4,8,4,256]{3,2,1,0:T(4,128)S(1)} %get-tuple-element.35), channel_id=1, source_target_pairs={{0,1},{1,2},{2,3},{3,4},{4,5},{5,6},{6,7},{7,8},{8,9},{9,10},{10,1... | collective-permute-start | bytes 393224 | tf_op jit(solution)/shard_map/ppermute | solution.py:705
  16.7 8.0 %collective-permute-start.3 = (f32[4,3,24,256]{3,2,1,0:T(8,128)S(1)}, f32[4,3,24,256]{3,2,1,0:T(8,128)S(1)}, u32[]{:S(2)}, u32[]{:S(2)}) collective-permute-start(f32[4,3,24,256]{3,2,1,0:T(8,128)S(1)} %get-tuple-element.32), channel_id=1, source_target_pairs={{16,0},{32,16},{48,32},{64,48},{80,64},{96,80},{112,96},{128,112},... | collective-permute-start | bytes 884744 | tf_op jit(solution)/shard_map/ppermute | solution.py:709
  18.8 5.9 %collective-permute-start.2 = (f32[4,3,24,256]{3,2,1,0:T(8,128)S(1)}, f32[4,3,24,256]{3,2,1,0:T(8,128)S(1)}, u32[]{:S(2)}, u32[]{:S(2)}) collective-permute-start(f32[4,3,24,256]{3,2,1,0:T(8,128)S(1)} %get-tuple-element.33), channel_id=1, source_target_pairs={{0,16},{16,32},{32,48},{48,64},{64,80},{80,96},{96,112},{112,128},... | collective-permute-start | bytes 884744 | tf_op jit(solution)/shard_map/ppermute | solution.py:708

commit v3 on v2

--- a/solution.py
+++ b/solution.py
@@ -68,14 +68,15 @@
     table = coefficient_table().astype(np.float64)
     widest = MASS_SHIFT + 0.3 * (table.sum(axis=1).max() + table.max(axis=0).sum())
     low = 0.5 * MASS_SHIFT / widest
-    scales = []
+    scales, lows = [], []
     while 1.0 - low > 2e-7:
         scales.append(2.0 / (1.0 + low))
+        lows.append(low)
         low = 4.0 * low / (1.0 + low) ** 2
-    return scales
-
-
-SCALES = inverse_scales()
+    return scales, lows
+
+
+SCALES, LOWS = inverse_scales()
 
 
 def lanes(shape):
@@ -230,7 +231,7 @@
     row16 = sublanes((16, 256))
     sums = {}
     for plane in range(8):
-        pairs = {"own": [], "up": [], "down": [], "next": [], "nextup": [], "nextdown": []}
+        pairs = {"own": [], "up": [], "next": [], "nextup": [], "nextdown": []}
         for j, (ox, oy, oz) in enumerate(HALF_STEPS):
             across = shift_z(shift_y(k_ref[plane + ox + DEPTH, j], oy), oz, 0.0)[:16]
             weight = -0.5 * (k_ref[plane + DEPTH, j, 0:16] + across)
@@ -245,9 +246,13 @@
                 )
             else:
                 pairs["next" if outside else "own"].append((jnp.where(row16 == 0, 0.0, weight), target))
-                pairs["nextdown" if outside else "down"].append(
-                    (jnp.where(row16 == 0, weight, 0.0)[:8], target[:8])
-                )
+                if outside:
+                    pairs["nextdown"].append((jnp.where(row16 == 0, weight, 0.0)[:8], target[:8]))
+                if plane > 0:
+                    back = shift_z(shift_y(k_ref[plane - 1 + DEPTH, j], -oy), -oz, 0.0)[8:16]
+                    back = -0.5 * (k_ref[plane + DEPTH, j, 8:16] + back)
+                    source = label_ref[plane - 1, SHIFTS.index((-oy, -oz)), 8:16]
+                    pairs["up"].append((jnp.where(row16[8:] == 15, back, 0.0), source))
         home = label_ref[plane, SHIFTS.index((0, 0))]
         pairs["own"].append((0.5 * diag_ref[plane + 2, 0:16], home))
         load = mid_ref[0, plane, 0:16]
@@ -265,13 +270,14 @@
             return out
 
         own = by_label("own")
-        sides = (by_label("down"), by_label("up"))
+        sides = ([], by_label("up"))
+        ones = jnp.ones((8, 256), F32)
         for half in (0, 1):
             rows = slice(8 * half, 8 * half + 8)
             chosen = jnp.concatenate(
                 [jnp.where(home[rows] == float(k), 1.0, 0.0) for k in range(LABELS)], axis=0
             ).astype(BF16)
-            right = jnp.concatenate([o[rows] for o in own] + [load[rows]] + sides[half], axis=0)
+            right = jnp.concatenate([o[rows] for o in own] + [load[rows], ones] + sides[half], axis=0)
             got = sum(dot(chosen, part, ((1,), (1,))) for part in split3(right))
             sums[half] = got if half not in sums else sums[half] + got
             if plane == 7:
@@ -281,32 +287,27 @@
                 right = jnp.concatenate([o[rows] for o in nexts] + corners[half], axis=0)
                 sums[2 + half] = sum(dot(chosen, part, ((1,), (1,))) for part in split3(right))
 
-    def place_of(col, half, ahead):
-        group = col // 8
-        if ahead:
-            side = 24 + (16 if half else 0)
-            return jnp.where(group < 8, 24 + 8 + group, side + group - 8)
-        side = 16 if half else 0
-        return jnp.where(group < 8, 8 + group, jnp.where(group == 8, 48, side + group - 9))
-
-    collected = None
+    total = None
     for which in range(4):
         width = sums[which].shape[1]
         shape = (64, width)
         kept = jnp.where(sublanes(shape) % 8 == lanes(shape) % 8, sums[which], 0.0)
-        shape = (width, 128)
-        chooser = jnp.where(
-            lanes(shape) % 64 == place_of(sublanes(shape), which % 2, which >= 2), 1.0, 0.0
-        )
-        part = pick(kept, chooser.astype(BF16))
-        collected = part if collected is None else collected + part
-    shape = (64, 128)
-    kept = jnp.where((sublanes(shape) // 8) % 2 == lanes(shape) // 64, collected, 0.0)
-    shape = (8, 64)
-    joiner = jnp.where(lanes(shape) // 16 == sublanes(shape) % 4, 1.0, 0.0).astype(BF16)
-    slot = sum(dot(joiner, part) for part in split3(kept))
-    for device in range(8):
-        slot_ref[8 * device : 8 * device + 8, :] = slot
+        shape = (width, 3 * 128)
+        group = sublanes(shape) // 8
+        if which < 2:
+            spot = jnp.where(group < 8, group, jnp.where(group < 10, 32 + group, group - 2))
+        else:
+            spot = jnp.where(group < 8, 24 + group, (8 if which == 2 else 24) + group)
+        here = (lanes(shape) // 128) * 16 + lanes(shape) % 16
+        part = pick(kept, jnp.where(here == spot, 1.0, 0.0).astype(BF16))
+        total = part if total is None else total + part
+    shape = (64, 3 * 128)
+    total = jnp.where(sublanes(shape) // 8 == (lanes(shape) % 128) // 16, total, 0.0)
+    total = jnp.sum(total, axis=0, keepdims=True)
+    rows = [total[:, 128 * r : 128 * r + 128] for r in range(3)]
+    slots = jnp.concatenate(rows * 8, axis=0)
+    slot_ref[0:24, :] = slots
+    slot_ref[24:48, :] = slots
 
 
 def coarse_rows(values, chooser):
@@ -362,42 +363,45 @@
     return high, (values - high.astype(F32)).astype(BF16)
 
 
-def left_stack(values):
-    high, low = split2(values)
+def left_stack(halves):
+    high, low = halves
     return jnp.concatenate([high, high, low], axis=1)
 
 
-def right_stack(values):
-    high, low = split2(values)
+def right_stack(halves):
+    high, low = halves
     return jnp.concatenate([high, low, high], axis=0)
 
 
-def invert(blocks, scale_ref, x_ref, p_ref):
+def invert(blocks, begin, scale_ref, x_ref, p_ref):
     shape = (BLOCK, BLOCK)
     eye = jnp.where(lanes(shape) == sublanes(shape), 1.0, 0.0).astype(F32)
     for q, block in enumerate(blocks):
         kept = eye * block
         across = 1.0 / jnp.sum(kept, axis=0, keepdims=True)
         down = 1.0 / jnp.sum(kept, axis=1, keepdims=True)
-        c = 0.5 * SCALES[0]
+        c = 0.5 * scale_ref[begin]
         x_ref[q] = (2.0 * c * eye - (c * c) * (block * down)) * across
     for q, block in enumerate(blocks):
-        p_ref[q] = dot(left_stack(block), right_stack(x_ref[q]))
+        p_ref[q] = dot(left_stack(split2(block)), right_stack(split2(x_ref[q])))
 
     def step(k, carry):
         c = scale_ref[k]
         for q in range(len(blocks)):
             x = x_ref[q]
             p = p_ref[q]
-            both = jnp.concatenate([left_stack(p), left_stack(x)], axis=0)
-            product = dot(both, right_stack(p))
+            halves = split2(p)
+            both = jnp.concatenate([left_stack(halves), left_stack(split2(x))], axis=0)
+            product = dot(both, right_stack(halves))
             p_ref[q] = (2.0 * c) * p - (c * c) * product[:BLOCK]
             x_ref[q] = (2.0 * c) * x - (c * c) * product[BLOCK:]
         return carry
 
-    lax.fori_loop(1, len(SCALES) - 2, step, 0)
+    lax.fori_loop(begin + 1, len(SCALES) - 2, step, 0)
     values = [x_ref[q] for q in range(len(blocks))]
-    rests = [eye - dot(left_stack(s), right_stack(x)) for s, x in zip(blocks, values)]
+    rests = [
+        eye - dot(left_stack(split2(s)), right_stack(split2(x))) for s, x in zip(blocks, values)
+    ]
     values = [x + dot(x.astype(BF16), r.astype(BF16)) for x, r in zip(values, rests)]
     rests = [eye - dot_high(s, x) for s, x in zip(blocks, values)]
     return [x + dot(x.astype(BF16), r.astype(BF16)) for x, r in zip(values, rests)]
@@ -413,50 +417,62 @@
     return jnp.take_along_axis(values, spot, axis=1, mode="promise_in_bounds")
 
 
-def unpack_coarse(slots_ref, d_ref, b_ref, f_ref):
+def unpack_coarse(slots_ref, d_ref, b_ref, f_ref, n_ref):
     for top in (0, 8):
         shape = (8, BLOCK)
         device = sublanes(shape) + top
         ring = lanes(shape) % 16
         column = lanes(shape) // 16
-        side = (ring - device + 17) % 16
-        near = side < 3
-        spot = jnp.minimum(side, 2) * 8 + column
+        ahead = (ring - device + 16) % 16
+        side = (ahead + 1) % 16
+        home = jnp.minimum(ahead, 1) * 8 + column
+        cross = jnp.minimum(side, 1) * 8 + column
         for s in range(16):
-            load = None
-            for pair in range(4):
-                values = slots_ref[pl.ds(64 * top + 4 * s + pair, 8, stride=64), :]
-                for half in (0, 1):
-                    row = 16 * (2 * pair + half) + top
-                    for r, target in enumerate((d_ref, b_ref)):
-                        if r == 1 and s == 15:
-                            continue
-                        got = gather_lanes(values, spot + (64 * half + 24 * r))
-                        target[s, row : row + 8, :] = jnp.where(near, got, 0.0)
-                got = gather_lanes(values, 48 + 64 * (column % 2))
-                mine = jnp.logical_and(ring == device, column // 2 == pair)
-                term = jnp.where(mine, got, 0.0)
-                load = term if load is None else load + term
-            load = jnp.sum(load, axis=0, keepdims=True)
-            if top == 0:
-                f_ref[s : s + 1, :] = load
-            else:
-                f_ref[s : s + 1, :] = f_ref[s : s + 1, :] + load
+            at = 48 * top + 3 * s
+            rows = [slots_ref[pl.ds(at + r, 8, stride=48), :] for r in range(3)]
+            for label in range(LABELS):
+                row = 16 * label + top
+                got = gather_lanes(rows[0], home + 16 * label)
+                d_ref[s, row : row + 8, :] = jnp.where(ahead < 2, got, 0.0)
+                if s < 15:
+                    got = jnp.where(
+                        side < 2,
+                        gather_lanes(rows[1], cross + 16 * label),
+                        gather_lanes(rows[2], column + 16 * label),
+                    )
+                    b_ref[s, row : row + 8, :] = jnp.where(side < 3, got, 0.0)
+            for place, target in ((8, f_ref), (9, n_ref)):
+                got = jnp.where(ring == device, gather_lanes(rows[2], 16 * column + place), 0.0)
+                total = jnp.sum(got, axis=0, keepdims=True)
+                if top > 0:
+                    total = target[s : s + 1, :] + total
+                target[s : s + 1, :] = total
+
+
+def first_step(d_ref, n_ref):
+    shape = (BLOCK, BLOCK)
+    eye = lanes(shape) == sublanes(shape)
+    diagonal = jnp.concatenate(
+        [jnp.sum(jnp.where(eye, d_ref[s], 0.0), axis=0, keepdims=True) for s in range(16)], axis=0
+    )
+    low = jnp.min((0.5 * MASS_SHIFT) * n_ref[...] / diagonal)
+    return sum(jnp.where(low >= bound, 1, 0).astype(jnp.int32) for bound in LOWS[1:-2])
 
 
 def factor_kernel(
-    slots_ref, scale_ref, right_ref, left_ref, last_ref, y_ref, d_ref, b_ref, x_ref, p_ref, f_ref
+    slots_ref, scale_ref, right_ref, left_ref, last_ref, y_ref, d_ref, b_ref, x_ref, p_ref, f_ref, n_ref
 ):
-    unpack_coarse(slots_ref, d_ref, b_ref, f_ref)
+    unpack_coarse(slots_ref, d_ref, b_ref, f_ref, n_ref)
     b_ref[15] = jnp.zeros((BLOCK, BLOCK), F32)
     for i in range(16):
         d_ref[i] = d_ref[i] + turned(d_ref[i])
+    first = first_step(d_ref, n_ref)
     begin = 0
     stride = 1
     while stride < 16:
         count = 8 // stride
         odd = [(2 * q + 1) * stride for q in range(count)]
-        inverses = invert([d_ref[i] for i in odd], scale_ref, x_ref, p_ref)
+        inverses = invert([d_ref[i] for i in odd], first, scale_ref, x_ref, p_ref)
         ups = [
             dot_high(inverse, b_ref[i - stride], ((1,), (1,))) for i, inverse in zip(odd, inverses)
         ]
@@ -482,7 +498,7 @@
             b_ref[i - stride] = -grams[q][:, BLOCK:]
         begin += count
         stride *= 2
-    (last,) = invert([d_ref[0]], scale_ref, x_ref, p_ref)
+    (last,) = invert([d_ref[0]], first, scale_ref, x_ref, p_ref)
     last_ref[...] = last
     y_ref[...] = coarse_solve(f_ref[...], right_ref, left_ref, last_ref)
 
@@ -685,9 +701,9 @@
     return up, [(j, i) for i, j in up]
 
 
-def exchange_all(slots, count):
+def exchange_all(slots):
     width = slots.shape[0] // 16
-    held = lax.all_to_all(slots.reshape(16, width, 128), AXIAL, 0, 0, tiled=True)
+    held = lax.all_to_all(slots.reshape(16, width * 128), AXIAL, 0, 0, tiled=True)
     held = jnp.broadcast_to(held.reshape(1, 16 * width, 128), (16, 16 * width, 128))
     return lax.all_to_all(held, CIRC, 0, 0, tiled=True).reshape(256 * width, 128)
 
@@ -700,11 +716,15 @@
 
 def shards(right_side, stiffness, material, groups):
     place = jnp.stack([lax.axis_index(AXIAL), lax.axis_index(CIRC)]).astype(jnp.int32)
-    fields = jnp.stack([right_side, stiffness, material.astype(F32), groups.astype(F32)])
+
+    def fields(rows):
+        parts = (right_side, stiffness, material, groups)
+        return jnp.stack([part[:, rows].astype(F32) for part in parts])
+
     up, down = ring_pairs(16)
-    before = lax.ppermute(fields[:, :, 16 - EDGE :], CIRC, up)
-    after = lax.ppermute(fields[:, :, :EDGE], CIRC, down)
-    middle = jnp.concatenate([fields, after, before], axis=2)
+    before = lax.ppermute(fields(slice(16 - EDGE, 16)), CIRC, up)
+    after = lax.ppermute(fields(slice(0, EDGE)), CIRC, down)
+    middle = jnp.concatenate([fields(slice(0, 16)), after, before], axis=2)
     low = lax.ppermute(middle[:, 8 - DEPTH :], AXIAL, up)
     high = lax.ppermute(middle[:, :DEPTH], AXIAL, down)
     table = np.zeros((16, 128), np.float32)
@@ -713,12 +733,12 @@
     k, diag, slots = call(
         setup_kernel,
         "setup",
-        (shape_of(14, 13, *ext), shape_of(12, *ext), shape_of(64, 128)),
+        (shape_of(14, 13, *ext), shape_of(12, *ext), shape_of(48, 128)),
         [pltpu.VMEM((9, 9, 16, 256), F32)],
         [VMEM, VMEM, VMEM, VMEM, SMEM],
         24,
     )(low, middle, high, jnp.asarray(table), place)
-    gathered = exchange_all(slots, 4)
+    gathered = exchange_all(slots)
     square = (BLOCK, BLOCK)
     right, left, last, y = call(
         factor_kernel,
@@ -729,6 +749,7 @@
             pltpu.VMEM((16, *square), F32),
             pltpu.VMEM((8, *square), F32),
             pltpu.VMEM((8, *square), F32),
+            pltpu.VMEM((16, BLOCK), F32),
             pltpu.VMEM((16, BLOCK), F32),
         ],
         [VMEM, SMEM],

time: 141 us -> 137 us (0.972)
  waiting for transfers between devices: 11.4 us -> 5.53 us
  blocking collectives: 68.5 us -> 70.3 us
    ppermute x2, waiting for transfers between devices: 7.13 us -> 1.23 us  [the longest x1 1.22 us: shards(): before = lax.ppermute(fields(slice(16 - EDGE, 16)), CIRC, up)]
    all_to_all x1, blocking collectives: 12.9 us -> 15.3 us  [exchange_all(): lax.all_to_all(held, CIRC, 0, 0, tiled=True).reshape(256 * width, 128)]
  transfers between devices with their start and end apart: 4 -> 4, of which waited for: 3 -> 2; matrix products, arithmetic and copies ran while one was open for 0% -> 1% of each run, Pallas kernels for 0% -> 0%
where the time goes in v3:
time: 137 us
  blocking collectives  70.3 us (51%)
  Pallas kernels  46.2 us (34%)
  starting transfers between devices  9.58 us (7%)
  waiting for transfers between devices  5.53 us (4%)
  other arithmetic  3.15 us (2%)
    all_to_all x2, blocking collectives, exchange(): lax.all_to_all(slots.reshape(256, count, 128), AXIAL_CIRC, 0, 0, tiled=True)  37.9 us
    pallas_call x1, Pallas kernels, shards(): call(factor_kernel, 'factor', (shape_of(15, BLOCK, 3 * BLOCK), shape_of(1...  25.9 us
    all_to_all x1, blocking collectives, exchange_all(): lax.all_to_all(slots.reshape(16, width * 128), AXIAL, 0, 0, tiled=True)  17.1 us
    all_to_all x1, blocking collectives, exchange_all(): lax.all_to_all(held, CIRC, 0, 0, tiled=True).reshape(256 * width, 128)  15.3 us
    pallas_call x1, Pallas kernels, shards(): call(setup_kernel, 'setup', (shape_of(14, 13, *ext), shape_of(12, *ext),...  6.74 us
    pallas_call x1, Pallas kernels, shards(): call(first_kernel, 'first', (shape_of(*own), shape_of(*own), shape_of(*ow...  5.4 us
    pallas_call x1, Pallas kernels, shards(): call(last_kernel, 'last', (shape_of(*own), shape_of(*own)), [pltpu.VMEM((...  4.63 us
    ppermute x1, waiting for transfers between devices, shards(): high = lax.ppermute(middle[:, :DEPTH], AXIAL, down)  4.31 us
  transfers between devices with their start and end apart: 4, of which 2 were waited for; matrix products, arithmetic and copies ran while one was open for 1% of the time, Pallas kernels for 0%

profile of v3, /device:TPU:1, one launch (start us, length us, event | category | flops | bytes accessed | tf_op | source)
XLA Modules:
  0.0 136.6 jit_solution(9783373767825529652)
XLA Ops:
  0.6 0.0 copy-start
  0.6 1.0 slice_bitcast_fusion.2
  1.6 1.0 convert_bitcast_fusion.4
  2.6 2.2 %collective-permute-start.1 = (f32[4,8,4,256]{3,2,1,0:T(4,128)S(1)}, f32[4,8,4,256]{3,2,1,0:T(4,128)S(1)}, u32[]{:S(2)}, u32[]{:S(2)}) collective-permute-start(f32[4,8,4,256]{3,2,1,0:T(4,128)S(1)} %pad_maximum_fusion.2), channel_id=1, source_target_pairs={{0,1},{1,2},{2,3},{3,4},{4,5},{5,6},{6,7},{7,8},{8,9},{9,10},{10,1... | collective-permute-start | bytes 393224 | tf_op jit(solution)/shard_map/ppermute | solution.py:725
  4.8 0.0 copy-start.1
  4.9 3.7 %collective-permute-start = (f32[4,8,4,256]{3,2,1,0:T(4,128)S(1)}, f32[4,8,4,256]{3,2,1,0:T(4,128)S(1)}, u32[]{:S(2)}, u32[]{:S(2)}) collective-permute-start(f32[4,8,4,256]{3,2,1,0:T(4,128)S(1)} %pad_maximum_fusion.1), channel_id=1, source_target_pairs={{1,0},{2,1},{3,2},{4,3},{5,4},{6,5},{7,6},{8,7},{9,8},{10,9},{11,1... | collective-permute-start | bytes 393224 | tf_op jit(solution)/shard_map/ppermute | solution.py:726
  8.6 1.0 convert_bitcast_fusion
  9.6 1.2 collective-permute-done.1
  10.8 0.0 collective-permute-done
  10.8 1.1 pad_maximum_fusion.mid_ref
  11.9 3.4 %collective-permute-start.3 = (f32[4,3,24,256]{3,2,1,0:T(8,128)S(1)}, f32[4,3,24,256]{3,2,1,0:T(8,128)S(1)}, u32[]{:S(2)}, u32[]{:S(2)}) collective-permute-start(f32[4,3,24,256]{3,2,1,0:T(8,128)S(1)} %get-tuple-element.32), channel_id=1, source_target_pairs={{16,0},{32,16},{48,32},{64,48},{80,64},{96,80},{112,96},{128,112},... | collective-permute-start | bytes 884744 | tf_op jit(solution)/shard_map/ppermute | solution.py:729
  15.3 0.3 collective-permute-start.2
  15.6 0.1 pad_add_fusion.place_ref
  15.6 4.3 %collective-permute-done.3.high_ref = f32[4,3,24,256]{3,2,1,0:T(8,128)S(1)} collective-permute-done((f32[4,3,24,256]{3,2,1,0:T(8,128)S(1)}, f32[4,3,24,256]{3,2,1,0:T(8,128)S(1)}, u32[]{:S(2)}, u32[]{:S(2)}) %collective-permute-start.3) | collective-permute-done | bytes 294944 | tf_op jit(solution)/shard_map/ppermute | solution.py:729
  19.9 0.0 collective-permute-done.2.low_ref
  20.0 6.7 %setup.1 = (f32[14,13,24,256]{3,2,1,0:T(8,128)S(1)}, f32[12,24,256]{2,1,0:T(8,128)S(1)}, f32[48,128]{1,0:T(8,128)S(1)}) custom-call(f32[4,3,24,256]{3,2,1,0:T(8,128)S(1)} %collective-permute-done.2.low_ref, f32[4,8,24,256]{3,2,1,0:T(8,128)S(1)} %pad_maximum_fusion.mid_ref, f32[4,3,24,256]{3,2,1,0:T(8,128)S(1)} %collective-permute-done.3.high_ref, ...), custom_call_target="tpu_custom_call" | custom-call | tf_op jit(solution)/shard_map/setup/pallas_call | solution.py:733
  26.7 17.1 %all_to_all.24 = f32[16,1,384]{2,1,0:T(1,128)S(1)} all-to-all(f32[16,1,384]{2,1,0:T(1,128)S(1)} %bitcast.40), channel_id=1, replica_groups=mesh['axial_0'=8,'axial_1'=2,'circ_0'=4,'circ_1'=4] {'axial_0','axial_1'}, dimensions={0} | all-to-all | bytes 49152 | tf_op jit(solution)/shard_map/all_to_all | solution.py:706
  43.8 15.3 %all_to_all.25 = f32[16,48,128]{2,1,0:T(8,128)S(1)} all-to-all(f32[16,48,128]{2,1,0:T(8,128)S(1)} %broadcast_in_dim.8), channel_id=1, replica_groups=mesh['axial_0'=8,'axial_1'=2,'circ_0'=4,'circ_1'=4] {'circ_0','circ_1'}, dimensions={0} | all-to-all | bytes 786432 | tf_op jit(solution)/shard_map/all_to_all | solution.py:708
  59.2 25.9 %factor.1 = (f32[15,128,384]{2,1,0:T(8,128)S(1)}, f32[15,256,128]{2,1,0:T(8,128)S(1)}, f32[128,128]{1,0:T(8,128)S(1)}, f32[16,128]{1,0:T(8,128)S(1)}) custom-call(f32[768,128]{1,0:T(8,128)S(1)} %bitcast.35, f32[9]{0:T(128)S(1)} %copy-done.1), custom_call_target="tpu_custom_call" | custom-call | tf_op jit(solution)/shard_map/factor/pallas_call | solution.py:743
  85.0 3.6 %start.1 = (f32[8,16,256]{2,1,0:T(8,128)S(1)}, f32[8,16,256]{2,1,0:T(8,128)S(1)}, f32[10,24,256]{2,1,0:T(8,128)S(1)}, f32[256,128]{1,0:T(8,128)S(1)}) custom-call(f32[4,3,24,256]{3,2,1,0:T(8,128)S(1)} %collective-permute-done.2.low_ref, f32[4,8,24,256]{3,2,1,0:T(8,128)S(1)} %pad_maximum_fusion.mid_ref, ...), custom_call_target="tpu_custom_call" | custom-call | tf_op jit(solution)/shard_map/start/pallas_call | solution.py:759
  88.6 19.5 %all_to_all.26 = f32[256,1,128]{2,1,0:T(1,128)S(1)} all-to-all(f32[256,1,128]{2,1,0:T(1,128)S(1)} %bitcast.39), channel_id=1, replica_groups=mesh['axial_0'=8,'axial_1'=2,'circ_0'=4,'circ_1'=4] {'axial_0','axial_1'..., dimensions={0} | all-to-all | bytes 262144 | tf_op jit(solution)/shard_map/all_to_all | solution.py:712
  108.1 5.4 %first.1 = (f32[8,16,256]{2,1,0:T(8,128)S(1)}, f32[8,16,256]{2,1,0:T(8,128)S(1)}, f32[8,16,256]{2,1,0:T(8,128)S(1)}, f32[256,128]{1,0:T(8,128)S(1)}) custom-call(f32[256,128]{1,0:T(8,128)S(1)} %bitcast.37, f32[15,128,384]{2,1,0:T(8,128)S(1)} %get-tuple-element.22.right_ref, f32[15,256,128]{2,1,0:T(8,128)S(1)} %get-tuple-element.23.left_ref, ...), custom_call_target="tpu_custom_call" | custom-call | tf_op jit(solution)/shard_map/first/pallas_call | solution.py:768
  113.5 18.4 %all_to_all.27 = f32[256,1,128]{2,1,0:T(1,128)S(1)} all-to-all(f32[256,1,128]{2,1,0:T(1,128)S(1)} %bitcast.38), channel_id=1, replica_groups=mesh['axial_0'=8,'axial_1'=2,'circ_0'=4,'circ_1'=4] {'axial_0','axial_1'..., dimensions={0} | all-to-all | bytes 262144 | tf_op jit(solution)/shard_map/all_to_all | solution.py:712
  132.0 4.6 %last.1 = (f32[8,16,256]{2,1,0:T(8,128)}, f32[8,16,256]{2,1,0:T(8,128)}) custom-call(f32[256,128]{1,0:T(8,128)S(1)} %bitcast.36, f32[15,128,384]{2,1,0:T(8,128)S(1)} %get-tuple-element.22.right_ref, f32[15,256,128]{2,1,0:T(8,128)S(1)} %get-tuple-element.23.left_ref, f32[128,128]{1,0:T(8,128)S(1)} %get-tuple-element.24.last_ref, ...), custom_call_target="tpu_custom_call" | custom-call | tf_op jit(solution)/shard_map/last/pallas_call | solution.py:777
  (6 shorter events, 0.1 us)
Async XLA Ops:
  0.6 19.3 %copy-start = (f32[16,128]{1,0:T(8,128)S(1)}, f32[16,128]{1,0:T(8,128)}, u32[]{:S(2)}) copy-start(f32[16,128]{1,0:T(8,128)} %constant.27.clone.table_ref) | copy-start | bytes 24580
  2.6 8.2 %collective-permute-start.1 = (f32[4,8,4,256]{3,2,1,0:T(4,128)S(1)}, f32[4,8,4,256]{3,2,1,0:T(4,128)S(1)}, u32[]{:S(2)}, u32[]{:S(2)}) collective-permute-start(f32[4,8,4,256]{3,2,1,0:T(4,128)S(1)} %pad_maximum_fusion.2), channel_id=1, source_target_pairs={{0,1},{1,2},{2,3},{3,4},{4,5},{5,6},{6,7},{7,8},{8,9},{9,10},{10,1... | collective-permute-start | bytes 393224 | tf_op jit(solution)/shard_map/ppermute | solution.py:725
  4.8 54.3 %copy-start.1 = (f32[9]{0:T(128)S(1)}, f32[9]{0:T(128)}, u32[]{:S(2)}) copy-start(f32[9]{0:T(128)} %constant.28.clone.scale_ref) | copy-start | bytes 112
  4.9 5.9 %collective-permute-start = (f32[4,8,4,256]{3,2,1,0:T(4,128)S(1)}, f32[4,8,4,256]{3,2,1,0:T(4,128)S(1)}, u32[]{:S(2)}, u32[]{:S(2)}) collective-permute-start(f32[4,8,4,256]{3,2,1,0:T(4,128)S(1)} %pad_maximum_fusion.1), channel_id=1, source_target_pairs={{1,0},{2,1},{3,2},{4,3},{5,4},{6,5},{7,6},{8,7},{9,8},{10,9},{11,1... | collective-permute-start | bytes 393224 | tf_op jit(solution)/shard_map/ppermute | solution.py:726
  11.9 8.0 %collective-permute-start.3 = (f32[4,3,24,256]{3,2,1,0:T(8,128)S(1)}, f32[4,3,24,256]{3,2,1,0:T(8,128)S(1)}, u32[]{:S(2)}, u32[]{:S(2)}) collective-permute-start(f32[4,3,24,256]{3,2,1,0:T(8,128)S(1)} %get-tuple-element.32), channel_id=1, source_target_pairs={{16,0},{32,16},{48,32},{64,48},{80,64},{96,80},{112,96},{128,112},... | collective-permute-start | bytes 884744 | tf_op jit(solution)/shard_map/ppermute | solution.py:729
  15.3 4.6 %collective-permute-start.2 = (f32[4,3,24,256]{3,2,1,0:T(8,128)S(1)}, f32[4,3,24,256]{3,2,1,0:T(8,128)S(1)}, u32[]{:S(2)}, u32[]{:S(2)}) collective-permute-start(f32[4,3,24,256]{3,2,1,0:T(8,128)S(1)} %get-tuple-element.33), channel_id=1, source_target_pairs={{0,16},{16,32},{32,48},{48,64},{64,80},{80,96},{96,112},{112,128},... | collective-permute-start | bytes 884744 | tf_op jit(solution)/shard_map/ppermute | solution.py:728

commit v4 on v3

--- a/solution.py
+++ b/solution.py
@@ -184,26 +184,111 @@
     return sum(dot(part, chooser) for part in split3(values))
 
 
-def setup_kernel(low_ref, mid_ref, high_ref, table_ref, place_ref, k_ref, diag_ref, slot_ref, label_ref):
-    for plane in range(-DEPTH, 8 + DEPTH):
+class Planes:
+    def __init__(self, mid_ref, end_ref):
+        self.mid_ref = mid_ref
+        self.end_ref = end_ref
+
+    def place(self, key):
+        plane = key[0] - DEPTH
+        if 0 <= plane < 8:
+            return self.mid_ref, (plane, *key[1:])
+        return self.end_ref, ((plane + DEPTH if plane < 0 else plane - 5), *key[1:])
+
+    def __getitem__(self, key):
+        ref, at = self.place(key)
+        return ref[at]
+
+    def __setitem__(self, key, values):
+        ref, at = self.place(key)
+        ref[at] = values
+
+
+def fill_stiffness(k_ref, table_ref, plane, stiff, kind):
+    kind = kind.astype(jnp.int32)
+    for j in range(13):
+        row = jnp.broadcast_to(table_ref[j : j + 1, :], (8, 128))
+        parts = []
+        for top in range(0, ROWS, 8):
+            line = [
+                gather_lanes(row, kind[top : top + 8, left : left + 128]) for left in (0, 128)
+            ]
+            parts.append(jnp.concatenate(line, axis=1))
+        k_ref[plane + DEPTH, j] = stiff * jnp.concatenate(parts, axis=0)
+
+
+def by_label(pairs):
+    out = []
+    for label in range(LABELS):
+        total = None
+        for weight, target in pairs:
+            term = jnp.where(target == float(label), weight, 0.0)
+            total = term if total is None else total + term
+        out.append(total)
+    return out
+
+
+def chosen_rows(home):
+    return jnp.concatenate(
+        [jnp.where(home == float(k), 1.0, 0.0) for k in range(LABELS)], axis=0
+    ).astype(BF16)
+
+
+def cell_sums(chosen, right):
+    return sum(dot(chosen, part, ((1,), (1,))) for part in split3(right))
+
+
+def inner_kernel(mid_ref, table_ref, km_ref, even_ref, odd_ref, label_ref):
+    k_ref = Planes(km_ref, None)
+    for plane in range(8):
+        fill_stiffness(k_ref, table_ref, plane, mid_ref[1, plane], mid_ref[2, plane])
+        spots = shifted(mid_ref[3, plane], -1.0)
+        for place, shift in enumerate(SHIFTS):
+            label_ref[plane, place] = spots[shift][:16]
+    row16 = sublanes((16, 256))
+    ones = jnp.ones((8, 256), F32)
+    sums = {}
+    for plane in range(8):
+        own, up = [], []
+        for j, (ox, oy, oz) in enumerate(HALF_STEPS):
+            if ox == 0 or plane < 7:
+                across = shift_z(shift_y(k_ref[plane + ox + DEPTH, j], oy), oz, 0.0)[:16]
+                weight = -0.5 * (k_ref[plane + DEPTH, j, 0:16] + across)
+                target = label_ref[plane + ox, SHIFTS.index((oy, oz))]
+                if oy == 0:
+                    own.append((weight, target))
+                else:
+                    edge = 15 if oy == 1 else 0
+                    own.append((jnp.where(row16 == edge, 0.0, weight), target))
+                    if oy == 1:
+                        up.append((jnp.where(row16 == 15, weight, 0.0)[8:], target[8:]))
+            if oy == -1 and plane > 0:
+                back = shift_z(shift_y(k_ref[plane - 1 + DEPTH, j], -oy), -oz, 0.0)[8:16]
+                back = -0.5 * (k_ref[plane + DEPTH, j, 8:16] + back)
+                source = label_ref[plane - 1, SHIFTS.index((-oy, -oz)), 8:16]
+                up.append((jnp.where(row16[8:] == 15, back, 0.0), source))
+        own = by_label(own)
+        sides = ([], by_label(up))
+        load = mid_ref[0, plane, 0:16]
+        home = label_ref[plane, SHIFTS.index((0, 0))]
+        for half in (0, 1):
+            rows = slice(8 * half, 8 * half + 8)
+            right = jnp.concatenate([o[rows] for o in own] + [load[rows], ones] + sides[half], axis=0)
+            got = cell_sums(chosen_rows(home[rows]), right)
+            sums[half] = got if half not in sums else sums[half] + got
+    even_ref[...] = sums[0]
+    odd_ref[...] = sums[1]
+
+
+def setup_kernel(
+    low_ref, mid_ref, high_ref, table_ref, place_ref, km_ref, even_ref, odd_ref,
+    ke_ref, diag_ref, slot_ref,
+):
+    k_ref = Planes(km_ref, ke_ref)
+    for plane in (-3, -2, -1, 8, 9, 10):
         stiff = masked(piece(low_ref, mid_ref, high_ref, 1, plane), present_flags(place_ref, plane))
-        kind = piece(low_ref, mid_ref, high_ref, 2, plane).astype(jnp.int32)
-        for j in range(13):
-            row = jnp.broadcast_to(table_ref[j : j + 1, :], (8, 128))
-            parts = []
-            for top in range(0, ROWS, 8):
-                line = []
-                for left in (0, 128):
-                    line.append(
-                        jnp.take_along_axis(
-                            row,
-                            kind[top : top + 8, left : left + 128],
-                            axis=1,
-                            mode="promise_in_bounds",
-                        )
-                    )
-                parts.append(jnp.concatenate(line, axis=1))
-            k_ref[plane + DEPTH, j] = stiff * jnp.concatenate(parts, axis=0)
+        kind = piece(low_ref, mid_ref, high_ref, 2, plane)
+        fill_stiffness(k_ref, table_ref, plane, stiff, kind)
     for plane in range(-2, 10):
         own = None
         total = None
@@ -224,70 +309,45 @@
             by_y = shift_z(by_y, sz, 0.0)
             total = by_y if total is None else total + by_y
         diag_ref[plane + 2] = MASS_SHIFT + own + 0.5 * total
-    for plane in range(0, 9):
-        spots = shifted(piece(low_ref, mid_ref, high_ref, 3, plane), -1.0)
-        for place, shift in enumerate(SHIFTS):
-            label_ref[plane, place] = spots[shift][:16]
+    middle = None
+    for plane in range(8):
+        for top in (0, 8):
+            rows = slice(top, top + 8)
+            got = cell_sums(
+                chosen_rows(mid_ref[3, plane, rows]), 0.5 * diag_ref[plane + 2, rows]
+            )
+            middle = got if middle is None else middle + got
+    spots = {shift: value[:16] for shift, value in shifted(high_ref[3, 0], -1.0).items()}
     row16 = sublanes((16, 256))
-    sums = {}
-    for plane in range(8):
-        pairs = {"own": [], "up": [], "next": [], "nextup": [], "nextdown": []}
-        for j, (ox, oy, oz) in enumerate(HALF_STEPS):
-            across = shift_z(shift_y(k_ref[plane + ox + DEPTH, j], oy), oz, 0.0)[:16]
-            weight = -0.5 * (k_ref[plane + DEPTH, j, 0:16] + across)
-            target = label_ref[plane + ox, SHIFTS.index((oy, oz))]
-            outside = ox == 1 and plane == 7
+    nexts, up, down = [], [], []
+    for j, (ox, oy, oz) in enumerate(HALF_STEPS):
+        if ox == 1:
+            across = shift_z(shift_y(k_ref[8 + DEPTH, j], oy), oz, 0.0)[:16]
+            weight = -0.5 * (k_ref[7 + DEPTH, j, 0:16] + across)
+            target = spots[(oy, oz)]
             if oy == 0:
-                pairs["next" if outside else "own"].append((weight, target))
+                nexts.append((weight, target))
             elif oy == 1:
-                pairs["next" if outside else "own"].append((jnp.where(row16 == 15, 0.0, weight), target))
-                pairs["nextup" if outside else "up"].append(
-                    (jnp.where(row16 == 15, weight, 0.0)[8:], target[8:])
-                )
+                nexts.append((jnp.where(row16 == 15, 0.0, weight), target))
+                up.append((jnp.where(row16 == 15, weight, 0.0)[8:], target[8:]))
             else:
-                pairs["next" if outside else "own"].append((jnp.where(row16 == 0, 0.0, weight), target))
-                if outside:
-                    pairs["nextdown"].append((jnp.where(row16 == 0, weight, 0.0)[:8], target[:8]))
-                if plane > 0:
-                    back = shift_z(shift_y(k_ref[plane - 1 + DEPTH, j], -oy), -oz, 0.0)[8:16]
-                    back = -0.5 * (k_ref[plane + DEPTH, j, 8:16] + back)
-                    source = label_ref[plane - 1, SHIFTS.index((-oy, -oz)), 8:16]
-                    pairs["up"].append((jnp.where(row16[8:] == 15, back, 0.0), source))
-        home = label_ref[plane, SHIFTS.index((0, 0))]
-        pairs["own"].append((0.5 * diag_ref[plane + 2, 0:16], home))
-        load = mid_ref[0, plane, 0:16]
-
-        def by_label(region):
-            out = []
-            for label in range(LABELS):
-                total = None
-                for weight, target in pairs[region]:
-                    term = jnp.where(target == float(label), weight, 0.0)
-                    total = term if total is None else total + term
-                if total is None:
-                    total = jnp.zeros((8, 256), F32)
-                out.append(total)
-            return out
-
-        own = by_label("own")
-        sides = ([], by_label("up"))
-        ones = jnp.ones((8, 256), F32)
-        for half in (0, 1):
-            rows = slice(8 * half, 8 * half + 8)
-            chosen = jnp.concatenate(
-                [jnp.where(home[rows] == float(k), 1.0, 0.0) for k in range(LABELS)], axis=0
-            ).astype(BF16)
-            right = jnp.concatenate([o[rows] for o in own] + [load[rows], ones] + sides[half], axis=0)
-            got = sum(dot(chosen, part, ((1,), (1,))) for part in split3(right))
-            sums[half] = got if half not in sums else sums[half] + got
-            if plane == 7:
-                if half == 0:
-                    nexts = by_label("next")
-                    corners = (by_label("nextdown"), by_label("nextup"))
-                right = jnp.concatenate([o[rows] for o in nexts] + corners[half], axis=0)
-                sums[2 + half] = sum(dot(chosen, part, ((1,), (1,))) for part in split3(right))
-
-    total = None
+                nexts.append((jnp.where(row16 == 0, 0.0, weight), target))
+                down.append((jnp.where(row16 == 0, weight, 0.0)[:8], target[:8]))
+    nexts, up, down = by_label(nexts), by_label(up), by_label(down)
+    sums = [even_ref[...], odd_ref[...]]
+    for half in (0, 1):
+        rows = slice(8 * half, 8 * half + 8)
+        right = jnp.concatenate([o[rows] for o in nexts] + (down, up)[half], axis=0)
+        sums.append(cell_sums(chosen_rows(mid_ref[3, 7, rows]), right))
+
+    shape = (64, 8)
+    total = jnp.sum(
+        jnp.where(sublanes(shape) % 8 == lanes(shape), middle, 0.0), axis=1, keepdims=True
+    )
+    shape = (64, 3 * 128)
+    total = jnp.where(
+        jnp.logical_and(lanes(shape) < 128, lanes(shape) % 16 == sublanes(shape) // 8), total, 0.0
+    )
     for which in range(4):
         width = sums[which].shape[1]
         shape = (64, width)
@@ -299,15 +359,14 @@
         else:
             spot = jnp.where(group < 8, 24 + group, (8 if which == 2 else 24) + group)
         here = (lanes(shape) // 128) * 16 + lanes(shape) % 16
-        part = pick(kept, jnp.where(here == spot, 1.0, 0.0).astype(BF16))
-        total = part if total is None else total + part
+        total = total + pick(kept, jnp.where(here == spot, 1.0, 0.0).astype(BF16))
     shape = (64, 3 * 128)
     total = jnp.where(sublanes(shape) // 8 == (lanes(shape) % 128) // 16, total, 0.0)
     total = jnp.sum(total, axis=0, keepdims=True)
     rows = [total[:, 128 * r : 128 * r + 128] for r in range(3)]
     slots = jnp.concatenate(rows * 8, axis=0)
-    slot_ref[0:24, :] = slots
-    slot_ref[24:48, :] = slots
+    for at in range(0, 768, 24):
+        slot_ref[at : at + 24, :] = slots
 
 
 def coarse_rows(values, chooser):
@@ -328,7 +387,7 @@
     now = [coarse_rhs[i : i + 1, :] for i in range(16)]
     begin = 0
     stages = []
-    while len(now) > 1:
+    while len(now) > 2:
         count = len(now)
         odd = now[1::2]
         even = now[0::2]
@@ -342,8 +401,9 @@
         stages.append((begin, solved))
         begin += count // 2
         now = even
-    (column,) = as_columns(now)
-    found = [jnp.sum(last_ref[...] * column, axis=0, keepdims=True)]
+    column = jnp.concatenate(as_columns(now), axis=0)
+    both = jnp.sum(last_ref[...] * column, axis=0, keepdims=True)
+    found = [both[:, :BLOCK], both[:, BLOCK:]]
     for begin, solved in reversed(stages):
         columns = as_columns(found)
         merged = []
@@ -374,7 +434,8 @@
 
 
 def invert(blocks, begin, scale_ref, x_ref, p_ref):
-    shape = (BLOCK, BLOCK)
+    shape = blocks[0].shape
+    size = shape[0]
     eye = jnp.where(lanes(shape) == sublanes(shape), 1.0, 0.0).astype(F32)
     for q, block in enumerate(blocks):
         kept = eye * block
@@ -393,8 +454,8 @@
             halves = split2(p)
             both = jnp.concatenate([left_stack(halves), left_stack(split2(x))], axis=0)
             product = dot(both, right_stack(halves))
-            p_ref[q] = (2.0 * c) * p - (c * c) * product[:BLOCK]
-            x_ref[q] = (2.0 * c) * x - (c * c) * product[BLOCK:]
+            p_ref[q] = (2.0 * c) * p - (c * c) * product[:size]
+            x_ref[q] = (2.0 * c) * x - (c * c) * product[size:]
         return carry
 
     lax.fori_loop(begin + 1, len(SCALES) - 2, step, 0)
@@ -428,8 +489,8 @@
         home = jnp.minimum(ahead, 1) * 8 + column
         cross = jnp.minimum(side, 1) * 8 + column
         for s in range(16):
-            at = 48 * top + 3 * s
-            rows = [slots_ref[pl.ds(at + r, 8, stride=48), :] for r in range(3)]
+            at = 48 * s + 3 * top
+            rows = [slots_ref[pl.ds(at + r, 8, stride=3), :] for r in range(3)]
             for label in range(LABELS):
                 row = 16 * label + top
                 got = gather_lanes(rows[0], home + 16 * label)
@@ -460,7 +521,8 @@
 
 
 def factor_kernel(
-    slots_ref, scale_ref, right_ref, left_ref, last_ref, y_ref, d_ref, b_ref, x_ref, p_ref, f_ref, n_ref
+    slots_ref, scale_ref, right_ref, left_ref, last_ref, y_ref, d_ref, b_ref, x_ref, p_ref,
+    xl_ref, pl_ref, f_ref, n_ref,
 ):
     unpack_coarse(slots_ref, d_ref, b_ref, f_ref, n_ref)
     b_ref[15] = jnp.zeros((BLOCK, BLOCK), F32)
@@ -469,7 +531,7 @@
     first = first_step(d_ref, n_ref)
     begin = 0
     stride = 1
-    while stride < 16:
+    while stride < 8:
         count = 8 // stride
         odd = [(2 * q + 1) * stride for q in range(count)]
         inverses = invert([d_ref[i] for i in odd], first, scale_ref, x_ref, p_ref)
@@ -498,7 +560,14 @@
             b_ref[i - stride] = -grams[q][:, BLOCK:]
         begin += count
         stride *= 2
-    (last,) = invert([d_ref[0]], first, scale_ref, x_ref, p_ref)
+    pair = jnp.concatenate(
+        [
+            jnp.concatenate([d_ref[0], b_ref[0]], axis=1),
+            jnp.concatenate([turned(b_ref[0]), d_ref[8]], axis=1),
+        ],
+        axis=0,
+    )
+    (last,) = invert([pair], first, scale_ref, xl_ref, pl_ref)
     last_ref[...] = last
     y_ref[...] = coarse_solve(f_ref[...], right_ref, left_ref, last_ref)
 
@@ -559,9 +628,10 @@
 
 
 def start_kernel(
-    low_ref, mid_ref, high_ref, k_ref, diag_ref, y_ref, place_ref,
+    low_ref, mid_ref, high_ref, km_ref, ke_ref, diag_ref, y_ref, place_ref,
     x_out, r_out, image_ref, slot_ref, v_ref, w_ref,
 ):
+    k_ref = Planes(km_ref, ke_ref)
     def label_of(plane):
         return piece(low_ref, mid_ref, high_ref, 3, plane)
 
@@ -595,9 +665,10 @@
 
 
 def first_kernel(
-    got_ref, right_ref, left_ref, last_ref, low_ref, mid_ref, high_ref, k_ref, diag_ref, image_ref,
+    got_ref, right_ref, left_ref, last_ref, low_ref, mid_ref, high_ref, km_ref, ke_ref, diag_ref, image_ref,
     r_ref, place_ref, w_out, d_out, aw_out, slot_ref, y_ref, v_ref, w_ref,
 ):
+    k_ref = Planes(km_ref, ke_ref)
     got = got_ref[...]
     coarse_rhs = coarse_rows(got, label_chooser())
     y_ref[...] = coarse_solve(coarse_rhs, right_ref, left_ref, last_ref)
@@ -637,9 +708,10 @@
 
 
 def last_kernel(
-    got_ref, right_ref, left_ref, last_ref, low_ref, mid_ref, high_ref, k_ref, diag_ref,
+    got_ref, right_ref, left_ref, last_ref, low_ref, mid_ref, high_ref, km_ref, ke_ref, diag_ref,
     x_ref, r_ref, w_ref, d_ref, aw_ref, place_ref, x_out, r_out, y_ref, v_ref,
 ):
+    k_ref = Planes(km_ref, ke_ref)
     got = got_ref[...]
     coarse_rhs = coarse_rows(got, label_chooser())
     solved = coarse_solve(coarse_rhs, right_ref, left_ref, last_ref)
@@ -684,7 +756,7 @@
     return jax.ShapeDtypeStruct(dims, F32)
 
 
-def call(kernel, name, outs, scratch, in_specs, mib):
+def call(kernel, name, outs, scratch, in_specs, mib, cost=None):
     return pl.pallas_call(
         kernel,
         name=name,
@@ -692,6 +764,7 @@
         in_specs=in_specs,
         out_specs=tuple(VMEM for _ in outs),
         scratch_shapes=scratch,
+        cost_estimate=cost,
         compiler_params=pltpu.CompilerParams(vmem_limit_bytes=mib * 1024 * 1024),
     )
 
@@ -702,10 +775,10 @@
 
 
 def exchange_all(slots):
-    width = slots.shape[0] // 16
-    held = lax.all_to_all(slots.reshape(16, width * 128), AXIAL, 0, 0, tiled=True)
-    held = jnp.broadcast_to(held.reshape(1, 16 * width, 128), (16, 16 * width, 128))
-    return lax.all_to_all(held, CIRC, 0, 0, tiled=True).reshape(256 * width, 128)
+    width = slots.shape[0] // 256
+    return lax.all_to_all(slots.reshape(256, width * 128), AXIAL_CIRC, 0, 0, tiled=True).reshape(
+        256 * width, 128
+    )
 
 
 def exchange(slots, count):
@@ -730,25 +803,38 @@
     table = np.zeros((16, 128), np.float32)
     table[:13, :CLASSES] = coefficient_table().T
     ext = (ROWS, 256)
-    k, diag, slots = call(
+    table = jnp.asarray(table)
+    k_mid, even, odd = call(
+        inner_kernel,
+        "inner",
+        (shape_of(8, 13, *ext), shape_of(64, 80), shape_of(64, 144)),
+        [pltpu.VMEM((8, 9, 16, 256), F32)],
+        [VMEM, VMEM],
+        20,
+        pl.CostEstimate(flops=40_000_000, transcendentals=0, bytes_accessed=4_000_000),
+    )(middle, table)
+    k_end, diag, slots = call(
         setup_kernel,
         "setup",
-        (shape_of(14, 13, *ext), shape_of(12, *ext), shape_of(48, 128)),
-        [pltpu.VMEM((9, 9, 16, 256), F32)],
-        [VMEM, VMEM, VMEM, VMEM, SMEM],
-        24,
-    )(low, middle, high, jnp.asarray(table), place)
+        (shape_of(6, 13, *ext), shape_of(12, *ext), shape_of(768, 128)),
+        [],
+        [VMEM, VMEM, VMEM, VMEM, SMEM, VMEM, VMEM, VMEM],
+        20,
+    )(low, middle, high, table, place, k_mid, even, odd)
     gathered = exchange_all(slots)
     square = (BLOCK, BLOCK)
+    double = (2 * BLOCK, 2 * BLOCK)
     right, left, last, y = call(
         factor_kernel,
         "factor",
-        (shape_of(15, BLOCK, 3 * BLOCK), shape_of(15, 2 * BLOCK, BLOCK), shape_of(*square), shape_of(16, BLOCK)),
+        (shape_of(14, BLOCK, 3 * BLOCK), shape_of(14, 2 * BLOCK, BLOCK), shape_of(*double), shape_of(16, BLOCK)),
         [
             pltpu.VMEM((16, *square), F32),
             pltpu.VMEM((16, *square), F32),
             pltpu.VMEM((8, *square), F32),
             pltpu.VMEM((8, *square), F32),
+            pltpu.VMEM((1, *double), F32),
+            pltpu.VMEM((1, *double), F32),
             pltpu.VMEM((16, BLOCK), F32),
             pltpu.VMEM((16, BLOCK), F32),
         ],
@@ -761,27 +847,27 @@
         "start",
         (shape_of(*own), shape_of(*own), shape_of(10, *ext), shape_of(256, 128)),
         [pltpu.VMEM((14, *ext), F32), pltpu.VMEM((12, *ext), F32)],
-        [VMEM] * 6 + [SMEM],
+        [VMEM] * 7 + [SMEM],
         24,
-    )(low, middle, high, k, diag, y, place)
+    )(low, middle, high, k_mid, k_end, diag, y, place)
     gathered = exchange(slots, 1)
     w0, d0, aw0, slots = call(
         first_kernel,
         "first",
         (shape_of(*own), shape_of(*own), shape_of(*own), shape_of(256, 128)),
         [pltpu.VMEM((16, BLOCK), F32), pltpu.VMEM((12, *ext), F32), pltpu.VMEM((10, *ext), F32)],
-        [VMEM] * 11 + [SMEM],
+        [VMEM] * 12 + [SMEM],
         24,
-    )(gathered, right, left, last, low, middle, high, k, diag, image, r0, place)
+    )(gathered, right, left, last, low, middle, high, k_mid, k_end, diag, image, r0, place)
     gathered = exchange(slots, 1)
     return call(
         last_kernel,
         "last",
         (shape_of(*own), shape_of(*own)),
         [pltpu.VMEM((16, BLOCK), F32), pltpu.VMEM((10, *ext), F32)],
-        [VMEM] * 14 + [SMEM],
+        [VMEM] * 15 + [SMEM],
         24,
-    )(gathered, right, left, last, low, middle, high, k, diag, x0, r0, w0, d0, aw0, place)
+    )(gathered, right, left, last, low, middle, high, k_mid, k_end, diag, x0, r0, w0, d0, aw0, place)
 
 
 def solution(mesh):

time: 137 us -> 130 us (0.949)
  waiting for transfers between devices: 5.53 us -> 1.48 us
  Pallas kernels: 46.2 us -> 44.1 us
    ppermute x1, waiting for transfers between devices: 4.31 us -> 0.24 us  [shards(): high = lax.ppermute(middle[:, :DEPTH], AXIAL, down)]
    all_to_all x2, blocking collectives: 37.9 us -> 36.3 us  [exchange(): lax.all_to_all(slots.reshape(256, count, 128), AXIAL_CIRC, 0, 0, tiled=True)]
    pallas_call x2 -> x3, Pallas kernels: 32.6 us -> 31 us  [the longest x1 24.2 us: shards(): call(factor_kernel, 'factor', (shape_of(14, BLOCK, 3 * BLOCK), shape_of(1...]
    all_to_all x2 -> x1, blocking collectives: 32.4 us -> 33.4 us  [exchange_all(): lax.all_to_all(slots.reshape(256, width * 128), AXIAL_CIRC, 0, 0, tiled=T...]
  transfers between devices with their start and end apart: 4 -> 4, of which waited for: 2 -> 2; matrix products, arithmetic and copies ran while one was open for 1% -> 1% of each run, Pallas kernels for 0% -> 3%
where the time goes in v4:
time: 130 us
  blocking collectives  69.6 us (54%)
  Pallas kernels  44.1 us (34%)
  starting transfers between devices  9.58 us (7%)
  other arithmetic  3.15 us (2%)
  waiting for transfers between devices  1.48 us (1%)
    all_to_all x2, blocking collectives, exchange(): lax.all_to_all(slots.reshape(256, count, 128), AXIAL_CIRC, 0, 0, tiled=True)  36.3 us
    all_to_all x1, blocking collectives, exchange_all(): lax.all_to_all(slots.reshape(256, width * 128), AXIAL_CIRC, 0, 0, tiled=T...  33.4 us
    pallas_call x1, Pallas kernels, shards(): call(factor_kernel, 'factor', (shape_of(14, BLOCK, 3 * BLOCK), shape_of(1...  24.2 us
    pallas_call x1, Pallas kernels, shards(): call(first_kernel, 'first', (shape_of(*own), shape_of(*own), shape_of(*ow...  5.14 us
    pallas_call x1, Pallas kernels, shards(): call(last_kernel, 'last', (shape_of(*own), shape_of(*own)), [pltpu.VMEM((...  4.38 us
    pallas_call x1, Pallas kernels, shards(): call(inner_kernel, 'inner', (shape_of(8, 13, *ext), shape_of(64, 80), sha...  4.04 us
    ppermute x1, starting transfers between devices, shards(): after = lax.ppermute(fields(slice(0, EDGE)), CIRC, down)  3.73 us
    pallas_call x1, Pallas kernels, shards(): call(start_kernel, 'start', (shape_of(*own), shape_of(*own), shape_of(10,...  3.64 us
  transfers between devices with their start and end apart: 4, of which 2 were waited for; matrix products, arithmetic and copies ran while one was open for 1% of the time, Pallas kernels for 3%

profile of v4, /device:TPU:1, one launch (start us, length us, event | category | flops | bytes accessed | tf_op | source)
XLA Modules:
  0.0 129.7 jit_solution(2257011783156713081)
XLA Ops:
  0.6 0.0 copy-start
  0.6 1.0 slice_bitcast_fusion.2
  1.6 1.0 convert_bitcast_fusion.4
  2.6 2.2 %collective-permute-start.1 = (f32[4,8,4,256]{3,2,1,0:T(4,128)S(1)}, f32[4,8,4,256]{3,2,1,0:T(4,128)S(1)}, u32[]{:S(2)}, u32[]{:S(2)}) collective-permute-start(f32[4,8,4,256]{3,2,1,0:T(4,128)S(1)} %pad_maximum_fusion.2), channel_id=1, source_target_pairs={{0,1},{1,2},{2,3},{3,4},{4,5},{5,6},{6,7},{7,8},{8,9},{9,10},{10,1... | collective-permute-start | bytes 393224 | tf_op jit(solution)/shard_map/ppermute | solution.py:798
  4.8 3.7 %collective-permute-start = (f32[4,8,4,256]{3,2,1,0:T(4,128)S(1)}, f32[4,8,4,256]{3,2,1,0:T(4,128)S(1)}, u32[]{:S(2)}, u32[]{:S(2)}) collective-permute-start(f32[4,8,4,256]{3,2,1,0:T(4,128)S(1)} %pad_maximum_fusion.1), channel_id=1, source_target_pairs={{1,0},{2,1},{3,2},{4,3},{5,4},{6,5},{7,6},{8,7},{9,8},{10,9},{11,1... | collective-permute-start | bytes 393224 | tf_op jit(solution)/shard_map/ppermute | solution.py:799
  8.6 1.0 convert_bitcast_fusion
  9.6 1.2 collective-permute-done.1
  10.8 0.0 collective-permute-done
  10.8 1.1 pad_maximum_fusion.mid_ref
  11.9 0.1 fusion
  11.9 3.4 %collective-permute-start.3 = (f32[4,3,24,256]{3,2,1,0:T(8,128)S(1)}, f32[4,3,24,256]{3,2,1,0:T(8,128)S(1)}, u32[]{:S(2)}, u32[]{:S(2)}) collective-permute-start(f32[4,3,24,256]{3,2,1,0:T(8,128)S(1)} %get-tuple-element.38), channel_id=1, source_target_pairs={{16,0},{32,16},{48,32},{64,48},{80,64},{96,80},{112,96},{128,112},... | collective-permute-start | bytes 884744 | tf_op jit(solution)/shard_map/ppermute | solution.py:802
  15.3 0.3 collective-permute-start.2
  15.6 0.1 pad_add_fusion.place_ref
  15.7 4.0 %inner.1 = (f32[8,13,24,256]{3,2,1,0:T(8,128)S(1)}, f32[64,80]{1,0:T(8,128)S(1)}, f32[64,144]{1,0:T(8,128)S(1)}) custom-call(f32[4,8,24,256]{3,2,1,0:T(8,128)S(1)} %pad_maximum_fusion.mid_ref, f32[16,128]{1,0:T(8,128)S(1)} %copy-done), custom_call_target="tpu_custom_call" | custom-call | flops 40000000 | bytes 4000000 | tf_op jit(solution)/shard_map/inner/pallas_call | solution.py:807
  19.7 0.0 copy-start.1
  19.7 0.2 collective-permute-done.3.high_ref
  20.0 2.7 %setup.1 = (f32[6,13,24,256]{3,2,1,0:T(8,128)S(1)}, f32[12,24,256]{2,1,0:T(8,128)S(1)}, f32[768,128]{1,0:T(8,128)S(1)}) custom-call(f32[4,3,24,256]{3,2,1,0:T(8,128)S(1)} %collective-permute-done.2.low_ref, f32[4,8,24,256]{3,2,1,0:T(8,128)S(1)} %pad_maximum_fusion.mid_ref, f32[4,3,24,256]{3,2,1,0:T(8,128)S(1)} %collective-permute-done.3.high_ref, ...), custom_call_target="tpu_custom_call" | custom-call | tf_op jit(solution)/shard_map/setup/pallas_call | solution.py:816
  22.7 33.4 %all_to_all.19 = f32[256,1,384]{2,1,0:T(1,128)S(1)} all-to-all(f32[256,1,384]{2,1,0:T(1,128)S(1)} %bitcast.37), channel_id=1, replica_groups=mesh['axial_0'=8,'axial_1'=2,'circ_0'=4,'circ_1'=4] {'axial_0','axial_1'..., dimensions={0} | all-to-all | bytes 786432 | tf_op jit(solution)/shard_map/all_to_all | solution.py:779
  56.0 24.2 %factor.1 = (f32[14,128,384]{2,1,0:T(8,128)S(1)}, f32[14,256,128]{2,1,0:T(8,128)S(1)}, f32[256,256]{1,0:T(8,128)S(1)}, f32[16,128]{1,0:T(8,128)S(1)}) custom-call(f32[768,128]{1,0:T(8,128)S(1)} %bitcast.34, f32[9]{0:T(128)S(1)} %copy-done.1), custom_call_target="tpu_custom_call" | custom-call | tf_op jit(solution)/shard_map/factor/pallas_call | solution.py:827
  80.3 3.6 %start.1 = (f32[8,16,256]{2,1,0:T(8,128)S(1)}, f32[8,16,256]{2,1,0:T(8,128)S(1)}, f32[10,24,256]{2,1,0:T(8,128)S(1)}, f32[256,128]{1,0:T(8,128)S(1)}) custom-call(f32[4,3,24,256]{3,2,1,0:T(8,128)S(1)} %collective-permute-done.2.low_ref, f32[4,8,24,256]{3,2,1,0:T(8,128)S(1)} %pad_maximum_fusion.mid_ref, ...), custom_call_target="tpu_custom_call" | custom-call | tf_op jit(solution)/shard_map/start/pallas_call | solution.py:845
  83.9 17.8 %all_to_all.20 = f32[256,1,128]{2,1,0:T(1,128)S(1)} all-to-all(f32[256,1,128]{2,1,0:T(1,128)S(1)} %bitcast.39), channel_id=1, replica_groups=mesh['axial_0'=8,'axial_1'=2,'circ_0'=4,'circ_1'=4] {'axial_0','axial_1'..., dimensions={0} | all-to-all | bytes 262144 | tf_op jit(solution)/shard_map/all_to_all | solution.py:785
  101.7 5.1 %first.1 = (f32[8,16,256]{2,1,0:T(8,128)S(1)}, f32[8,16,256]{2,1,0:T(8,128)S(1)}, f32[8,16,256]{2,1,0:T(8,128)S(1)}, f32[256,128]{1,0:T(8,128)S(1)}) custom-call(f32[256,128]{1,0:T(8,128)S(1)} %bitcast.36, f32[14,128,384]{2,1,0:T(8,128)S(1)} %get-tuple-element.28.right_ref, f32[14,256,128]{2,1,0:T(8,128)S(1)} %get-tuple-element.29.left_ref, ...), custom_call_target="tpu_custom_call" | custom-call | tf_op jit(solution)/shard_map/first/pallas_call | solution.py:854
  106.9 18.4 %all_to_all.21 = f32[256,1,128]{2,1,0:T(1,128)S(1)} all-to-all(f32[256,1,128]{2,1,0:T(1,128)S(1)} %bitcast.38), channel_id=1, replica_groups=mesh['axial_0'=8,'axial_1'=2,'circ_0'=4,'circ_1'=4] {'axial_0','axial_1'..., dimensions={0} | all-to-all | bytes 262144 | tf_op jit(solution)/shard_map/all_to_all | solution.py:785
  125.3 4.4 %last.1 = (f32[8,16,256]{2,1,0:T(8,128)}, f32[8,16,256]{2,1,0:T(8,128)}) custom-call(f32[256,128]{1,0:T(8,128)S(1)} %bitcast.35, f32[14,128,384]{2,1,0:T(8,128)S(1)} %get-tuple-element.28.right_ref, f32[14,256,128]{2,1,0:T(8,128)S(1)} %get-tuple-element.29.left_ref, f32[256,256]{1,0:T(8,128)S(1)} %get-tuple-element.30.last_ref, ...), custom_call_target="tpu_custom_call" | custom-call | tf_op jit(solution)/shard_map/last/pallas_call | solution.py:863
  (5 shorter events, 0.1 us)
Async XLA Ops:
  0.6 15.0 %copy-start = (f32[16,128]{1,0:T(8,128)S(1)}, f32[16,128]{1,0:T(8,128)}, u32[]{:S(2)}) copy-start(f32[16,128]{1,0:T(8,128)} %constant.27.clone.table_ref) | copy-start | bytes 24580
  2.6 8.2 %collective-permute-start.1 = (f32[4,8,4,256]{3,2,1,0:T(4,128)S(1)}, f32[4,8,4,256]{3,2,1,0:T(4,128)S(1)}, u32[]{:S(2)}, u32[]{:S(2)}) collective-permute-start(f32[4,8,4,256]{3,2,1,0:T(4,128)S(1)} %pad_maximum_fusion.2), channel_id=1, source_target_pairs={{0,1},{1,2},{2,3},{3,4},{4,5},{5,6},{6,7},{7,8},{8,9},{9,10},{10,1... | collective-permute-start | bytes 393224 | tf_op jit(solution)/shard_map/ppermute | solution.py:798
  4.8 6.0 %collective-permute-start = (f32[4,8,4,256]{3,2,1,0:T(4,128)S(1)}, f32[4,8,4,256]{3,2,1,0:T(4,128)S(1)}, u32[]{:S(2)}, u32[]{:S(2)}) collective-permute-start(f32[4,8,4,256]{3,2,1,0:T(4,128)S(1)} %pad_maximum_fusion.1), channel_id=1, source_target_pairs={{1,0},{2,1},{3,2},{4,3},{5,4},{6,5},{7,6},{8,7},{9,8},{10,9},{11,1... | collective-permute-start | bytes 393224 | tf_op jit(solution)/shard_map/ppermute | solution.py:799
  11.9 8.0 %collective-permute-start.3 = (f32[4,3,24,256]{3,2,1,0:T(8,128)S(1)}, f32[4,3,24,256]{3,2,1,0:T(8,128)S(1)}, u32[]{:S(2)}, u32[]{:S(2)}) collective-permute-start(f32[4,3,24,256]{3,2,1,0:T(8,128)S(1)} %get-tuple-element.38), channel_id=1, source_target_pairs={{16,0},{32,16},{48,32},{64,48},{80,64},{96,80},{112,96},{128,112},... | collective-permute-start | bytes 884744 | tf_op jit(solution)/shard_map/ppermute | solution.py:802
  15.3 4.6 %collective-permute-start.2 = (f32[4,3,24,256]{3,2,1,0:T(8,128)S(1)}, f32[4,3,24,256]{3,2,1,0:T(8,128)S(1)}, u32[]{:S(2)}, u32[]{:S(2)}) collective-permute-start(f32[4,3,24,256]{3,2,1,0:T(8,128)S(1)} %get-tuple-element.39), channel_id=1, source_target_pairs={{0,16},{16,32},{32,48},{48,64},{64,80},{80,96},{96,112},{112,128},... | collective-permute-start | bytes 884744 | tf_op jit(solution)/shard_map/ppermute | solution.py:801
  19.7 36.3 %copy-start.1 = (f32[9]{0:T(128)S(1)}, f32[9]{0:T(128)}, u32[]{:S(2)}) copy-start(f32[9]{0:T(128)} %constant.28.clone.scale_ref) | copy-start | bytes 112

commit v5 on v4

--- a/solution.py
+++ b/solution.py
@@ -458,20 +458,16 @@
             x_ref[q] = (2.0 * c) * x - (c * c) * product[size:]
         return carry
 
-    lax.fori_loop(begin + 1, len(SCALES) - 2, step, 0)
+    lax.fori_loop(begin + 1, len(SCALES) - 1, step, 0)
     values = [x_ref[q] for q in range(len(blocks))]
-    rests = [
-        eye - dot(left_stack(split2(s)), right_stack(split2(x))) for s, x in zip(blocks, values)
-    ]
-    values = [x + dot(x.astype(BF16), r.astype(BF16)) for x, r in zip(values, rests)]
     rests = [eye - dot_high(s, x) for s, x in zip(blocks, values)]
     return [x + dot(x.astype(BF16), r.astype(BF16)) for x, r in zip(values, rests)]
 
 
-def turned(values):
+def turned(values, split):
     shape = (BLOCK, BLOCK)
     eye = jnp.where(lanes(shape) == sublanes(shape), 1.0, 0.0).astype(BF16)
-    return sum(dot(eye, part, ((1,), (1,))) for part in split3(values))
+    return sum(dot(eye, part, ((1,), (1,))) for part in split(values))
 
 
 def gather_lanes(values, spot):
@@ -491,10 +487,14 @@
         for s in range(16):
             at = 48 * s + 3 * top
             rows = [slots_ref[pl.ds(at + r, 8, stride=3), :] for r in range(3)]
+            behind = pltpu.roll(slots_ref[pl.ds(48 * s, 16, stride=3), :], 1, axis=0)[top : top + 8]
             for label in range(LABELS):
                 row = 16 * label + top
                 got = gather_lanes(rows[0], home + 16 * label)
-                d_ref[s, row : row + 8, :] = jnp.where(ahead < 2, got, 0.0)
+                same = got + gather_lanes(rows[0], 16 * column + label)
+                back = gather_lanes(behind, 16 * column + 8 + label)
+                got = jnp.where(ahead == 0, same, jnp.where(ahead == 1, got, 0.0))
+                d_ref[s, row : row + 8, :] = jnp.where(ahead == 15, back, got)
                 if s < 15:
                     got = jnp.where(
                         side < 2,
@@ -526,8 +526,6 @@
 ):
     unpack_coarse(slots_ref, d_ref, b_ref, f_ref, n_ref)
     b_ref[15] = jnp.zeros((BLOCK, BLOCK), F32)
-    for i in range(16):
-        d_ref[i] = d_ref[i] + turned(d_ref[i])
     first = first_step(d_ref, n_ref)
     begin = 0
     stride = 1
@@ -545,8 +543,8 @@
             right_ref[begin + q, :, BLOCK:] = products[q]
         grams = [dot_high(b_ref[i - stride], product) for i, product in zip(odd, products)]
         for q in range(count):
-            left_ref[begin + q, :BLOCK, :] = turned(ups[q])
-            left_ref[begin + q, BLOCK:, :] = turned(downs[q])
+            left_ref[begin + q, :BLOCK, :] = turned(ups[q], split2)
+            left_ref[begin + q, BLOCK:, :] = turned(downs[q], split2)
         afters = [
             dot_high(left_ref[begin + q, BLOCK:, :], b_ref[i])
             for q, i in enumerate(odd)
@@ -563,7 +561,7 @@
     pair = jnp.concatenate(
         [
             jnp.concatenate([d_ref[0], b_ref[0]], axis=1),
-            jnp.concatenate([turned(b_ref[0]), d_ref[8]], axis=1),
+            jnp.concatenate([turned(b_ref[0], split3), d_ref[8]], axis=1),
         ],
         axis=0,
     )

time: 130 us -> 131 us (level)
  no operation moved by 1% of the time
where the time goes in v5:
time: 131 us
  blocking collectives  69.6 us (53%)
  Pallas kernels  45.2 us (35%)
  starting transfers between devices  9.58 us (7%)
  other arithmetic  3.15 us (2%)
  waiting for transfers between devices  1.48 us (1%)
    all_to_all x2, blocking collectives, exchange(): lax.all_to_all(slots.reshape(256, count, 128), AXIAL_CIRC, 0, 0, tiled=True)  36.3 us
    all_to_all x1, blocking collectives, exchange_all(): lax.all_to_all(slots.reshape(256, width * 128), AXIAL_CIRC, 0, 0, tiled=T...  33.4 us
    pallas_call x1, Pallas kernels, shards(): call(factor_kernel, 'factor', (shape_of(14, BLOCK, 3 * BLOCK), shape_of(1...  25.3 us
    pallas_call x1, Pallas kernels, shards(): call(first_kernel, 'first', (shape_of(*own), shape_of(*own), shape_of(*ow...  5.14 us
    pallas_call x1, Pallas kernels, shards(): call(last_kernel, 'last', (shape_of(*own), shape_of(*own)), [pltpu.VMEM((...  4.38 us
    pallas_call x1, Pallas kernels, shards(): call(inner_kernel, 'inner', (shape_of(8, 13, *ext), shape_of(64, 80), sha...  4.04 us
    ppermute x1, starting transfers between devices, shards(): after = lax.ppermute(fields(slice(0, EDGE)), CIRC, down)  3.73 us
    pallas_call x1, Pallas kernels, shards(): call(start_kernel, 'start', (shape_of(*own), shape_of(*own), shape_of(10,...  3.64 us
  transfers between devices with their start and end apart: 4, of which 2 were waited for; matrix products, arithmetic and copies ran while one was open for 1% of the time, Pallas kernels for 3%

profile of v5, /device:TPU:1, one launch (start us, length us, event | category | flops | bytes accessed | tf_op | source)
XLA Modules:
  0.0 130.8 jit_solution(4623165819440944068)
XLA Ops:
  0.6 0.0 copy-start
  0.6 1.0 slice_bitcast_fusion.2
  1.6 1.0 convert_bitcast_fusion.4
  2.6 2.2 %collective-permute-start.1 = (f32[4,8,4,256]{3,2,1,0:T(4,128)S(1)}, f32[4,8,4,256]{3,2,1,0:T(4,128)S(1)}, u32[]{:S(2)}, u32[]{:S(2)}) collective-permute-start(f32[4,8,4,256]{3,2,1,0:T(4,128)S(1)} %pad_maximum_fusion.2), channel_id=1, source_target_pairs={{0,1},{1,2},{2,3},{3,4},{4,5},{5,6},{6,7},{7,8},{8,9},{9,10},{10,1... | collective-permute-start | bytes 393224 | tf_op jit(solution)/shard_map/ppermute | solution.py:796
  4.8 3.7 %collective-permute-start = (f32[4,8,4,256]{3,2,1,0:T(4,128)S(1)}, f32[4,8,4,256]{3,2,1,0:T(4,128)S(1)}, u32[]{:S(2)}, u32[]{:S(2)}) collective-permute-start(f32[4,8,4,256]{3,2,1,0:T(4,128)S(1)} %pad_maximum_fusion.1), channel_id=1, source_target_pairs={{1,0},{2,1},{3,2},{4,3},{5,4},{6,5},{7,6},{8,7},{9,8},{10,9},{11,1... | collective-permute-start | bytes 393224 | tf_op jit(solution)/shard_map/ppermute | solution.py:797
  8.6 1.0 convert_bitcast_fusion
  9.6 1.2 collective-permute-done.1
  10.8 0.0 collective-permute-done
  10.8 1.1 pad_maximum_fusion.mid_ref
  11.9 0.1 fusion
  11.9 3.4 %collective-permute-start.3 = (f32[4,3,24,256]{3,2,1,0:T(8,128)S(1)}, f32[4,3,24,256]{3,2,1,0:T(8,128)S(1)}, u32[]{:S(2)}, u32[]{:S(2)}) collective-permute-start(f32[4,3,24,256]{3,2,1,0:T(8,128)S(1)} %get-tuple-element.38), channel_id=1, source_target_pairs={{16,0},{32,16},{48,32},{64,48},{80,64},{96,80},{112,96},{128,112},... | collective-permute-start | bytes 884744 | tf_op jit(solution)/shard_map/ppermute | solution.py:800
  15.3 0.3 collective-permute-start.2
  15.6 0.1 pad_add_fusion.place_ref
  15.7 4.0 %inner.1 = (f32[8,13,24,256]{3,2,1,0:T(8,128)S(1)}, f32[64,80]{1,0:T(8,128)S(1)}, f32[64,144]{1,0:T(8,128)S(1)}) custom-call(f32[4,8,24,256]{3,2,1,0:T(8,128)S(1)} %pad_maximum_fusion.mid_ref, f32[16,128]{1,0:T(8,128)S(1)} %copy-done), custom_call_target="tpu_custom_call" | custom-call | flops 40000000 | bytes 4000000 | tf_op jit(solution)/shard_map/inner/pallas_call | solution.py:805
  19.7 0.0 copy-start.1
  19.7 0.2 collective-permute-done.3.high_ref
  20.0 2.7 %setup.1 = (f32[6,13,24,256]{3,2,1,0:T(8,128)S(1)}, f32[12,24,256]{2,1,0:T(8,128)S(1)}, f32[768,128]{1,0:T(8,128)S(1)}) custom-call(f32[4,3,24,256]{3,2,1,0:T(8,128)S(1)} %collective-permute-done.2.low_ref, f32[4,8,24,256]{3,2,1,0:T(8,128)S(1)} %pad_maximum_fusion.mid_ref, f32[4,3,24,256]{3,2,1,0:T(8,128)S(1)} %collective-permute-done.3.high_ref, ...), custom_call_target="tpu_custom_call" | custom-call | tf_op jit(solution)/shard_map/setup/pallas_call | solution.py:814
  22.7 33.4 %all_to_all.19 = f32[256,1,384]{2,1,0:T(1,128)S(1)} all-to-all(f32[256,1,384]{2,1,0:T(1,128)S(1)} %bitcast.37), channel_id=1, replica_groups=mesh['axial_0'=8,'axial_1'=2,'circ_0'=4,'circ_1'=4] {'axial_0','axial_1'..., dimensions={0} | all-to-all | bytes 786432 | tf_op jit(solution)/shard_map/all_to_all | solution.py:777
  56.0 25.3 %factor.1 = (f32[14,128,384]{2,1,0:T(8,128)S(1)}, f32[14,256,128]{2,1,0:T(8,128)S(1)}, f32[256,256]{1,0:T(8,128)S(1)}, f32[16,128]{1,0:T(8,128)S(1)}) custom-call(f32[768,128]{1,0:T(8,128)S(1)} %bitcast.34, f32[9]{0:T(128)S(1)} %copy-done.1), custom_call_target="tpu_custom_call" | custom-call | tf_op jit(solution)/shard_map/factor/pallas_call | solution.py:825
  81.4 3.6 %start.1 = (f32[8,16,256]{2,1,0:T(8,128)S(1)}, f32[8,16,256]{2,1,0:T(8,128)S(1)}, f32[10,24,256]{2,1,0:T(8,128)S(1)}, f32[256,128]{1,0:T(8,128)S(1)}) custom-call(f32[4,3,24,256]{3,2,1,0:T(8,128)S(1)} %collective-permute-done.2.low_ref, f32[4,8,24,256]{3,2,1,0:T(8,128)S(1)} %pad_maximum_fusion.mid_ref, ...), custom_call_target="tpu_custom_call" | custom-call | tf_op jit(solution)/shard_map/start/pallas_call | solution.py:843
  85.0 17.8 %all_to_all.20 = f32[256,1,128]{2,1,0:T(1,128)S(1)} all-to-all(f32[256,1,128]{2,1,0:T(1,128)S(1)} %bitcast.39), channel_id=1, replica_groups=mesh['axial_0'=8,'axial_1'=2,'circ_0'=4,'circ_1'=4] {'axial_0','axial_1'..., dimensions={0} | all-to-all | bytes 262144 | tf_op jit(solution)/shard_map/all_to_all | solution.py:783
  102.9 5.1 %first.1 = (f32[8,16,256]{2,1,0:T(8,128)S(1)}, f32[8,16,256]{2,1,0:T(8,128)S(1)}, f32[8,16,256]{2,1,0:T(8,128)S(1)}, f32[256,128]{1,0:T(8,128)S(1)}) custom-call(f32[256,128]{1,0:T(8,128)S(1)} %bitcast.36, f32[14,128,384]{2,1,0:T(8,128)S(1)} %get-tuple-element.28.right_ref, f32[14,256,128]{2,1,0:T(8,128)S(1)} %get-tuple-element.29.left_ref, ...), custom_call_target="tpu_custom_call" | custom-call | tf_op jit(solution)/shard_map/first/pallas_call | solution.py:852
  108.0 18.4 %all_to_all.21 = f32[256,1,128]{2,1,0:T(1,128)S(1)} all-to-all(f32[256,1,128]{2,1,0:T(1,128)S(1)} %bitcast.38), channel_id=1, replica_groups=mesh['axial_0'=8,'axial_1'=2,'circ_0'=4,'circ_1'=4] {'axial_0','axial_1'..., dimensions={0} | all-to-all | bytes 262144 | tf_op jit(solution)/shard_map/all_to_all | solution.py:783
  126.4 4.4 %last.1 = (f32[8,16,256]{2,1,0:T(8,128)}, f32[8,16,256]{2,1,0:T(8,128)}) custom-call(f32[256,128]{1,0:T(8,128)S(1)} %bitcast.35, f32[14,128,384]{2,1,0:T(8,128)S(1)} %get-tuple-element.28.right_ref, f32[14,256,128]{2,1,0:T(8,128)S(1)} %get-tuple-element.29.left_ref, f32[256,256]{1,0:T(8,128)S(1)} %get-tuple-element.30.last_ref, ...), custom_call_target="tpu_custom_call" | custom-call | tf_op jit(solution)/shard_map/last/pallas_call | solution.py:861
  (5 shorter events, 0.1 us)
Async XLA Ops:
  0.6 15.0 %copy-start = (f32[16,128]{1,0:T(8,128)S(1)}, f32[16,128]{1,0:T(8,128)}, u32[]{:S(2)}) copy-start(f32[16,128]{1,0:T(8,128)} %constant.27.clone.table_ref) | copy-start | bytes 24580
  2.6 8.2 %collective-permute-start.1 = (f32[4,8,4,256]{3,2,1,0:T(4,128)S(1)}, f32[4,8,4,256]{3,2,1,0:T(4,128)S(1)}, u32[]{:S(2)}, u32[]{:S(2)}) collective-permute-start(f32[4,8,4,256]{3,2,1,0:T(4,128)S(1)} %pad_maximum_fusion.2), channel_id=1, source_target_pairs={{0,1},{1,2},{2,3},{3,4},{4,5},{5,6},{6,7},{7,8},{8,9},{9,10},{10,1... | collective-permute-start | bytes 393224 | tf_op jit(solution)/shard_map/ppermute | solution.py:796
  4.8 6.0 %collective-permute-start = (f32[4,8,4,256]{3,2,1,0:T(4,128)S(1)}, f32[4,8,4,256]{3,2,1,0:T(4,128)S(1)}, u32[]{:S(2)}, u32[]{:S(2)}) collective-permute-start(f32[4,8,4,256]{3,2,1,0:T(4,128)S(1)} %pad_maximum_fusion.1), channel_id=1, source_target_pairs={{1,0},{2,1},{3,2},{4,3},{5,4},{6,5},{7,6},{8,7},{9,8},{10,9},{11,1... | collective-permute-start | bytes 393224 | tf_op jit(solution)/shard_map/ppermute | solution.py:797
  11.9 8.0 %collective-permute-start.3 = (f32[4,3,24,256]{3,2,1,0:T(8,128)S(1)}, f32[4,3,24,256]{3,2,1,0:T(8,128)S(1)}, u32[]{:S(2)}, u32[]{:S(2)}) collective-permute-start(f32[4,3,24,256]{3,2,1,0:T(8,128)S(1)} %get-tuple-element.38), channel_id=1, source_target_pairs={{16,0},{32,16},{48,32},{64,48},{80,64},{96,80},{112,96},{128,112},... | collective-permute-start | bytes 884744 | tf_op jit(solution)/shard_map/ppermute | solution.py:800
  15.3 4.6 %collective-permute-start.2 = (f32[4,3,24,256]{3,2,1,0:T(8,128)S(1)}, f32[4,3,24,256]{3,2,1,0:T(8,128)S(1)}, u32[]{:S(2)}, u32[]{:S(2)}) collective-permute-start(f32[4,3,24,256]{3,2,1,0:T(8,128)S(1)} %get-tuple-element.39), channel_id=1, source_target_pairs={{0,16},{16,32},{32,48},{48,64},{64,80},{80,96},{96,112},{112,128},... | collective-permute-start | bytes 884744 | tf_op jit(solution)/shard_map/ppermute | solution.py:799
  19.7 36.3 %copy-start.1 = (f32[9]{0:T(128)S(1)}, f32[9]{0:T(128)}, u32[]{:S(2)}) copy-start(f32[9]{0:T(128)} %constant.28.clone.scale_ref) | copy-start | bytes 112

commit v6 on v4

--- a/solution.py
+++ b/solution.py
@@ -545,8 +545,8 @@
             right_ref[begin + q, :, BLOCK:] = products[q]
         grams = [dot_high(b_ref[i - stride], product) for i, product in zip(odd, products)]
         for q in range(count):
-            left_ref[begin + q, :BLOCK, :] = turned(ups[q])
-            left_ref[begin + q, BLOCK:, :] = turned(downs[q])
+            left_ref[begin + q, :BLOCK, :] = ups[q].T
+            left_ref[begin + q, BLOCK:, :] = downs[q].T
         afters = [
             dot_high(left_ref[begin + q, BLOCK:, :], b_ref[i])
             for q, i in enumerate(odd)

time: 130 us -> 128 us (0.985)
  Pallas kernels: 44.1 us -> 42.4 us
    pallas_call x1, Pallas kernels: 24.2 us -> 22.5 us  [shards(): call(factor_kernel, 'factor', (shape_of(14, BLOCK, 3 * BLOCK), shape_of(1...]
where the time goes in v6:
time: 128 us
  blocking collectives  69.6 us (54%)
  Pallas kernels  42.4 us (33%)
  starting transfers between devices  9.58 us (7%)
  other arithmetic  3.15 us (2%)
  waiting for transfers between devices  1.48 us (1%)
    all_to_all x2, blocking collectives, exchange(): lax.all_to_all(slots.reshape(256, count, 128), AXIAL_CIRC, 0, 0, tiled=True)  36.3 us
    all_to_all x1, blocking collectives, exchange_all(): lax.all_to_all(slots.reshape(256, width * 128), AXIAL_CIRC, 0, 0, tiled=T...  33.4 us
    pallas_call x1, Pallas kernels, shards(): call(factor_kernel, 'factor', (shape_of(14, BLOCK, 3 * BLOCK), shape_of(1...  22.5 us
    pallas_call x1, Pallas kernels, shards(): call(first_kernel, 'first', (shape_of(*own), shape_of(*own), shape_of(*ow...  5.14 us
    pallas_call x1, Pallas kernels, shards(): call(last_kernel, 'last', (shape_of(*own), shape_of(*own)), [pltpu.VMEM((...  4.38 us
    pallas_call x1, Pallas kernels, shards(): call(inner_kernel, 'inner', (shape_of(8, 13, *ext), shape_of(64, 80), sha...  4.04 us
    ppermute x1, starting transfers between devices, shards(): after = lax.ppermute(fields(slice(0, EDGE)), CIRC, down)  3.73 us
    pallas_call x1, Pallas kernels, shards(): call(start_kernel, 'start', (shape_of(*own), shape_of(*own), shape_of(10,...  3.64 us
  transfers between devices with their start and end apart: 4, of which 2 were waited for; matrix products, arithmetic and copies ran while one was open for 1% of the time, Pallas kernels for 3%

profile of v6, /device:TPU:1, one launch (start us, length us, event | category | flops | bytes accessed | tf_op | source)
XLA Modules:
  0.0 128.0 jit_solution(12568368037175782179)
XLA Ops:
  0.6 0.0 copy-start
  0.6 1.0 slice_bitcast_fusion.2
  1.6 1.0 convert_bitcast_fusion.4
  2.6 2.2 %collective-permute-start.1 = (f32[4,8,4,256]{3,2,1,0:T(4,128)S(1)}, f32[4,8,4,256]{3,2,1,0:T(4,128)S(1)}, u32[]{:S(2)}, u32[]{:S(2)}) collective-permute-start(f32[4,8,4,256]{3,2,1,0:T(4,128)S(1)} %pad_maximum_fusion.2), channel_id=1, source_target_pairs={{0,1},{1,2},{2,3},{3,4},{4,5},{5,6},{6,7},{7,8},{8,9},{9,10},{10,1... | collective-permute-start | bytes 393224 | tf_op jit(solution)/shard_map/ppermute | solution.py:798
  4.8 3.7 %collective-permute-start = (f32[4,8,4,256]{3,2,1,0:T(4,128)S(1)}, f32[4,8,4,256]{3,2,1,0:T(4,128)S(1)}, u32[]{:S(2)}, u32[]{:S(2)}) collective-permute-start(f32[4,8,4,256]{3,2,1,0:T(4,128)S(1)} %pad_maximum_fusion.1), channel_id=1, source_target_pairs={{1,0},{2,1},{3,2},{4,3},{5,4},{6,5},{7,6},{8,7},{9,8},{10,9},{11,1... | collective-permute-start | bytes 393224 | tf_op jit(solution)/shard_map/ppermute | solution.py:799
  8.6 1.0 convert_bitcast_fusion
  9.6 1.2 collective-permute-done.1
  10.8 0.0 collective-permute-done
  10.8 1.1 pad_maximum_fusion.mid_ref
  11.9 0.1 fusion
  11.9 3.4 %collective-permute-start.3 = (f32[4,3,24,256]{3,2,1,0:T(8,128)S(1)}, f32[4,3,24,256]{3,2,1,0:T(8,128)S(1)}, u32[]{:S(2)}, u32[]{:S(2)}) collective-permute-start(f32[4,3,24,256]{3,2,1,0:T(8,128)S(1)} %get-tuple-element.38), channel_id=1, source_target_pairs={{16,0},{32,16},{48,32},{64,48},{80,64},{96,80},{112,96},{128,112},... | collective-permute-start | bytes 884744 | tf_op jit(solution)/shard_map/ppermute | solution.py:802
  15.3 0.3 collective-permute-start.2
  15.6 0.1 pad_add_fusion.place_ref
  15.7 4.0 %inner.1 = (f32[8,13,24,256]{3,2,1,0:T(8,128)S(1)}, f32[64,80]{1,0:T(8,128)S(1)}, f32[64,144]{1,0:T(8,128)S(1)}) custom-call(f32[4,8,24,256]{3,2,1,0:T(8,128)S(1)} %pad_maximum_fusion.mid_ref, f32[16,128]{1,0:T(8,128)S(1)} %copy-done), custom_call_target="tpu_custom_call" | custom-call | flops 40000000 | bytes 4000000 | tf_op jit(solution)/shard_map/inner/pallas_call | solution.py:807
  19.7 0.0 copy-start.1
  19.7 0.2 collective-permute-done.3.high_ref
  20.0 2.7 %setup.1 = (f32[6,13,24,256]{3,2,1,0:T(8,128)S(1)}, f32[12,24,256]{2,1,0:T(8,128)S(1)}, f32[768,128]{1,0:T(8,128)S(1)}) custom-call(f32[4,3,24,256]{3,2,1,0:T(8,128)S(1)} %collective-permute-done.2.low_ref, f32[4,8,24,256]{3,2,1,0:T(8,128)S(1)} %pad_maximum_fusion.mid_ref, f32[4,3,24,256]{3,2,1,0:T(8,128)S(1)} %collective-permute-done.3.high_ref, ...), custom_call_target="tpu_custom_call" | custom-call | tf_op jit(solution)/shard_map/setup/pallas_call | solution.py:816
  22.7 33.4 %all_to_all.19 = f32[256,1,384]{2,1,0:T(1,128)S(1)} all-to-all(f32[256,1,384]{2,1,0:T(1,128)S(1)} %bitcast.37), channel_id=1, replica_groups=mesh['axial_0'=8,'axial_1'=2,'circ_0'=4,'circ_1'=4] {'axial_0','axial_1'..., dimensions={0} | all-to-all | bytes 786432 | tf_op jit(solution)/shard_map/all_to_all | solution.py:779
  56.0 22.5 %factor.1 = (f32[14,128,384]{2,1,0:T(8,128)S(1)}, f32[14,256,128]{2,1,0:T(8,128)S(1)}, f32[256,256]{1,0:T(8,128)S(1)}, f32[16,128]{1,0:T(8,128)S(1)}) custom-call(f32[768,128]{1,0:T(8,128)S(1)} %bitcast.34, f32[9]{0:T(128)S(1)} %copy-done.1), custom_call_target="tpu_custom_call" | custom-call | tf_op jit(solution)/shard_map/factor/pallas_call | solution.py:827
  78.5 3.6 %start.1 = (f32[8,16,256]{2,1,0:T(8,128)S(1)}, f32[8,16,256]{2,1,0:T(8,128)S(1)}, f32[10,24,256]{2,1,0:T(8,128)S(1)}, f32[256,128]{1,0:T(8,128)S(1)}) custom-call(f32[4,3,24,256]{3,2,1,0:T(8,128)S(1)} %collective-permute-done.2.low_ref, f32[4,8,24,256]{3,2,1,0:T(8,128)S(1)} %pad_maximum_fusion.mid_ref, ...), custom_call_target="tpu_custom_call" | custom-call | tf_op jit(solution)/shard_map/start/pallas_call | solution.py:845
  82.2 17.8 %all_to_all.20 = f32[256,1,128]{2,1,0:T(1,128)S(1)} all-to-all(f32[256,1,128]{2,1,0:T(1,128)S(1)} %bitcast.39), channel_id=1, replica_groups=mesh['axial_0'=8,'axial_1'=2,'circ_0'=4,'circ_1'=4] {'axial_0','axial_1'..., dimensions={0} | all-to-all | bytes 262144 | tf_op jit(solution)/shard_map/all_to_all | solution.py:785
  100.0 5.1 %first.1 = (f32[8,16,256]{2,1,0:T(8,128)S(1)}, f32[8,16,256]{2,1,0:T(8,128)S(1)}, f32[8,16,256]{2,1,0:T(8,128)S(1)}, f32[256,128]{1,0:T(8,128)S(1)}) custom-call(f32[256,128]{1,0:T(8,128)S(1)} %bitcast.36, f32[14,128,384]{2,1,0:T(8,128)S(1)} %get-tuple-element.28.right_ref, f32[14,256,128]{2,1,0:T(8,128)S(1)} %get-tuple-element.29.left_ref, ...), custom_call_target="tpu_custom_call" | custom-call | tf_op jit(solution)/shard_map/first/pallas_call | solution.py:854
  105.2 18.4 %all_to_all.21 = f32[256,1,128]{2,1,0:T(1,128)S(1)} all-to-all(f32[256,1,128]{2,1,0:T(1,128)S(1)} %bitcast.38), channel_id=1, replica_groups=mesh['axial_0'=8,'axial_1'=2,'circ_0'=4,'circ_1'=4] {'axial_0','axial_1'..., dimensions={0} | all-to-all | bytes 262144 | tf_op jit(solution)/shard_map/all_to_all | solution.py:785
  123.6 4.4 %last.1 = (f32[8,16,256]{2,1,0:T(8,128)}, f32[8,16,256]{2,1,0:T(8,128)}) custom-call(f32[256,128]{1,0:T(8,128)S(1)} %bitcast.35, f32[14,128,384]{2,1,0:T(8,128)S(1)} %get-tuple-element.28.right_ref, f32[14,256,128]{2,1,0:T(8,128)S(1)} %get-tuple-element.29.left_ref, f32[256,256]{1,0:T(8,128)S(1)} %get-tuple-element.30.last_ref, ...), custom_call_target="tpu_custom_call" | custom-call | tf_op jit(solution)/shard_map/last/pallas_call | solution.py:863
  (5 shorter events, 0.1 us)
Async XLA Ops:
  0.6 15.0 %copy-start = (f32[16,128]{1,0:T(8,128)S(1)}, f32[16,128]{1,0:T(8,128)}, u32[]{:S(2)}) copy-start(f32[16,128]{1,0:T(8,128)} %constant.27.clone.table_ref) | copy-start | bytes 24580
  2.6 8.2 %collective-permute-start.1 = (f32[4,8,4,256]{3,2,1,0:T(4,128)S(1)}, f32[4,8,4,256]{3,2,1,0:T(4,128)S(1)}, u32[]{:S(2)}, u32[]{:S(2)}) collective-permute-start(f32[4,8,4,256]{3,2,1,0:T(4,128)S(1)} %pad_maximum_fusion.2), channel_id=1, source_target_pairs={{0,1},{1,2},{2,3},{3,4},{4,5},{5,6},{6,7},{7,8},{8,9},{9,10},{10,1... | collective-permute-start | bytes 393224 | tf_op jit(solution)/shard_map/ppermute | solution.py:798
  4.8 6.0 %collective-permute-start = (f32[4,8,4,256]{3,2,1,0:T(4,128)S(1)}, f32[4,8,4,256]{3,2,1,0:T(4,128)S(1)}, u32[]{:S(2)}, u32[]{:S(2)}) collective-permute-start(f32[4,8,4,256]{3,2,1,0:T(4,128)S(1)} %pad_maximum_fusion.1), channel_id=1, source_target_pairs={{1,0},{2,1},{3,2},{4,3},{5,4},{6,5},{7,6},{8,7},{9,8},{10,9},{11,1... | collective-permute-start | bytes 393224 | tf_op jit(solution)/shard_map/ppermute | solution.py:799
  11.9 8.0 %collective-permute-start.3 = (f32[4,3,24,256]{3,2,1,0:T(8,128)S(1)}, f32[4,3,24,256]{3,2,1,0:T(8,128)S(1)}, u32[]{:S(2)}, u32[]{:S(2)}) collective-permute-start(f32[4,3,24,256]{3,2,1,0:T(8,128)S(1)} %get-tuple-element.38), channel_id=1, source_target_pairs={{16,0},{32,16},{48,32},{64,48},{80,64},{96,80},{112,96},{128,112},... | collective-permute-start | bytes 884744 | tf_op jit(solution)/shard_map/ppermute | solution.py:802
  15.3 4.6 %collective-permute-start.2 = (f32[4,3,24,256]{3,2,1,0:T(8,128)S(1)}, f32[4,3,24,256]{3,2,1,0:T(8,128)S(1)}, u32[]{:S(2)}, u32[]{:S(2)}) collective-permute-start(f32[4,3,24,256]{3,2,1,0:T(8,128)S(1)} %get-tuple-element.39), channel_id=1, source_target_pairs={{0,16},{16,32},{32,48},{48,64},{64,80},{80,96},{96,112},{112,128},... | collective-permute-start | bytes 884744 | tf_op jit(solution)/shard_map/ppermute | solution.py:801
  19.7 36.3 %copy-start.1 = (f32[9]{0:T(128)S(1)}, f32[9]{0:T(128)}, u32[]{:S(2)}) copy-start(f32[9]{0:T(128)} %constant.28.clone.scale_ref) | copy-start | bytes 112

commit v7 on v6

--- a/solution.py
+++ b/solution.py
@@ -536,7 +536,7 @@
         odd = [(2 * q + 1) * stride for q in range(count)]
         inverses = invert([d_ref[i] for i in odd], first, scale_ref, x_ref, p_ref)
         ups = [
-            dot_high(inverse, b_ref[i - stride], ((1,), (1,))) for i, inverse in zip(odd, inverses)
+            dot_high(inverse, b_ref[i - stride].T) for i, inverse in zip(odd, inverses)
         ]
         downs = [dot_high(inverse, b_ref[i]) for i, inverse in zip(odd, inverses)]
         products = [jnp.concatenate(pair, axis=1) for pair in zip(ups, downs)]
@@ -563,7 +563,7 @@
     pair = jnp.concatenate(
         [
             jnp.concatenate([d_ref[0], b_ref[0]], axis=1),
-            jnp.concatenate([turned(b_ref[0]), d_ref[8]], axis=1),
+            jnp.concatenate([b_ref[0].T, d_ref[8]], axis=1),
         ],
         axis=0,
     )

time: 128 us -> 128 us (level)
  no operation moved by 1% of the time
where the time goes in v7:
time: 128 us
  blocking collectives  69.6 us (54%)
  Pallas kernels  42.3 us (33%)
  starting transfers between devices  9.58 us (7%)
  other arithmetic  3.15 us (2%)
  waiting for transfers between devices  1.48 us (1%)
    all_to_all x2, blocking collectives, exchange(): lax.all_to_all(slots.reshape(256, count, 128), AXIAL_CIRC, 0, 0, tiled=True)  36.3 us
    all_to_all x1, blocking collectives, exchange_all(): lax.all_to_all(slots.reshape(256, width * 128), AXIAL_CIRC, 0, 0, tiled=T...  33.4 us
    pallas_call x1, Pallas kernels, shards(): call(factor_kernel, 'factor', (shape_of(14, BLOCK, 3 * BLOCK), shape_of(1...  22.4 us
    pallas_call x1, Pallas kernels, shards(): call(first_kernel, 'first', (shape_of(*own), shape_of(*own), shape_of(*ow...  5.14 us
    pallas_call x1, Pallas kernels, shards(): call(last_kernel, 'last', (shape_of(*own), shape_of(*own)), [pltpu.VMEM((...  4.38 us
    pallas_call x1, Pallas kernels, shards(): call(inner_kernel, 'inner', (shape_of(8, 13, *ext), shape_of(64, 80), sha...  4.04 us
    ppermute x1, starting transfers between devices, shards(): after = lax.ppermute(fields(slice(0, EDGE)), CIRC, down)  3.73 us
    pallas_call x1, Pallas kernels, shards(): call(start_kernel, 'start', (shape_of(*own), shape_of(*own), shape_of(10,...  3.64 us
  transfers between devices with their start and end apart: 4, of which 2 were waited for; matrix products, arithmetic and copies ran while one was open for 1% of the time, Pallas kernels for 3%

profile of v7, /device:TPU:1, one launch (start us, length us, event | category | flops | bytes accessed | tf_op | source)
XLA Modules:
  0.0 127.9 jit_solution(11224107655100335977)
XLA Ops:
  0.6 0.0 copy-start
  0.6 1.0 slice_bitcast_fusion.2
  1.6 1.0 convert_bitcast_fusion.4
  2.6 2.2 %collective-permute-start.1 = (f32[4,8,4,256]{3,2,1,0:T(4,128)S(1)}, f32[4,8,4,256]{3,2,1,0:T(4,128)S(1)}, u32[]{:S(2)}, u32[]{:S(2)}) collective-permute-start(f32[4,8,4,256]{3,2,1,0:T(4,128)S(1)} %pad_maximum_fusion.2), channel_id=1, source_target_pairs={{0,1},{1,2},{2,3},{3,4},{4,5},{5,6},{6,7},{7,8},{8,9},{9,10},{10,1... | collective-permute-start | bytes 393224 | tf_op jit(solution)/shard_map/ppermute | solution.py:798
  4.8 3.7 %collective-permute-start = (f32[4,8,4,256]{3,2,1,0:T(4,128)S(1)}, f32[4,8,4,256]{3,2,1,0:T(4,128)S(1)}, u32[]{:S(2)}, u32[]{:S(2)}) collective-permute-start(f32[4,8,4,256]{3,2,1,0:T(4,128)S(1)} %pad_maximum_fusion.1), channel_id=1, source_target_pairs={{1,0},{2,1},{3,2},{4,3},{5,4},{6,5},{7,6},{8,7},{9,8},{10,9},{11,1... | collective-permute-start | bytes 393224 | tf_op jit(solution)/shard_map/ppermute | solution.py:799
  8.6 1.0 convert_bitcast_fusion
  9.6 1.2 collective-permute-done.1
  10.8 0.0 collective-permute-done
  10.8 1.1 pad_maximum_fusion.mid_ref
  11.9 0.1 fusion
  11.9 3.4 %collective-permute-start.3 = (f32[4,3,24,256]{3,2,1,0:T(8,128)S(1)}, f32[4,3,24,256]{3,2,1,0:T(8,128)S(1)}, u32[]{:S(2)}, u32[]{:S(2)}) collective-permute-start(f32[4,3,24,256]{3,2,1,0:T(8,128)S(1)} %get-tuple-element.38), channel_id=1, source_target_pairs={{16,0},{32,16},{48,32},{64,48},{80,64},{96,80},{112,96},{128,112},... | collective-permute-start | bytes 884744 | tf_op jit(solution)/shard_map/ppermute | solution.py:802
  15.3 0.3 collective-permute-start.2
  15.6 0.1 pad_add_fusion.place_ref
  15.7 4.0 %inner.1 = (f32[8,13,24,256]{3,2,1,0:T(8,128)S(1)}, f32[64,80]{1,0:T(8,128)S(1)}, f32[64,144]{1,0:T(8,128)S(1)}) custom-call(f32[4,8,24,256]{3,2,1,0:T(8,128)S(1)} %pad_maximum_fusion.mid_ref, f32[16,128]{1,0:T(8,128)S(1)} %copy-done), custom_call_target="tpu_custom_call" | custom-call | flops 40000000 | bytes 4000000 | tf_op jit(solution)/shard_map/inner/pallas_call | solution.py:807
  19.7 0.0 copy-start.1
  19.7 0.2 collective-permute-done.3.high_ref
  20.0 2.7 %setup.1 = (f32[6,13,24,256]{3,2,1,0:T(8,128)S(1)}, f32[12,24,256]{2,1,0:T(8,128)S(1)}, f32[768,128]{1,0:T(8,128)S(1)}) custom-call(f32[4,3,24,256]{3,2,1,0:T(8,128)S(1)} %collective-permute-done.2.low_ref, f32[4,8,24,256]{3,2,1,0:T(8,128)S(1)} %pad_maximum_fusion.mid_ref, f32[4,3,24,256]{3,2,1,0:T(8,128)S(1)} %collective-permute-done.3.high_ref, ...), custom_call_target="tpu_custom_call" | custom-call | tf_op jit(solution)/shard_map/setup/pallas_call | solution.py:816
  22.7 33.4 %all_to_all.19 = f32[256,1,384]{2,1,0:T(1,128)S(1)} all-to-all(f32[256,1,384]{2,1,0:T(1,128)S(1)} %bitcast.37), channel_id=1, replica_groups=mesh['axial_0'=8,'axial_1'=2,'circ_0'=4,'circ_1'=4] {'axial_0','axial_1'..., dimensions={0} | all-to-all | bytes 786432 | tf_op jit(solution)/shard_map/all_to_all | solution.py:779
  56.0 22.4 %factor.1 = (f32[14,128,384]{2,1,0:T(8,128)S(1)}, f32[14,256,128]{2,1,0:T(8,128)S(1)}, f32[256,256]{1,0:T(8,128)S(1)}, f32[16,128]{1,0:T(8,128)S(1)}) custom-call(f32[768,128]{1,0:T(8,128)S(1)} %bitcast.34, f32[9]{0:T(128)S(1)} %copy-done.1), custom_call_target="tpu_custom_call" | custom-call | tf_op jit(solution)/shard_map/factor/pallas_call | solution.py:827
  78.5 3.6 %start.1 = (f32[8,16,256]{2,1,0:T(8,128)S(1)}, f32[8,16,256]{2,1,0:T(8,128)S(1)}, f32[10,24,256]{2,1,0:T(8,128)S(1)}, f32[256,128]{1,0:T(8,128)S(1)}) custom-call(f32[4,3,24,256]{3,2,1,0:T(8,128)S(1)} %collective-permute-done.2.low_ref, f32[4,8,24,256]{3,2,1,0:T(8,128)S(1)} %pad_maximum_fusion.mid_ref, ...), custom_call_target="tpu_custom_call" | custom-call | tf_op jit(solution)/shard_map/start/pallas_call | solution.py:845
  82.1 17.8 %all_to_all.20 = f32[256,1,128]{2,1,0:T(1,128)S(1)} all-to-all(f32[256,1,128]{2,1,0:T(1,128)S(1)} %bitcast.39), channel_id=1, replica_groups=mesh['axial_0'=8,'axial_1'=2,'circ_0'=4,'circ_1'=4] {'axial_0','axial_1'..., dimensions={0} | all-to-all | bytes 262144 | tf_op jit(solution)/shard_map/all_to_all | solution.py:785
  99.9 5.1 %first.1 = (f32[8,16,256]{2,1,0:T(8,128)S(1)}, f32[8,16,256]{2,1,0:T(8,128)S(1)}, f32[8,16,256]{2,1,0:T(8,128)S(1)}, f32[256,128]{1,0:T(8,128)S(1)}) custom-call(f32[256,128]{1,0:T(8,128)S(1)} %bitcast.36, f32[14,128,384]{2,1,0:T(8,128)S(1)} %get-tuple-element.28.right_ref, f32[14,256,128]{2,1,0:T(8,128)S(1)} %get-tuple-element.29.left_ref, ...), custom_call_target="tpu_custom_call" | custom-call | tf_op jit(solution)/shard_map/first/pallas_call | solution.py:854
  105.1 18.4 %all_to_all.21 = f32[256,1,128]{2,1,0:T(1,128)S(1)} all-to-all(f32[256,1,128]{2,1,0:T(1,128)S(1)} %bitcast.38), channel_id=1, replica_groups=mesh['axial_0'=8,'axial_1'=2,'circ_0'=4,'circ_1'=4] {'axial_0','axial_1'..., dimensions={0} | all-to-all | bytes 262144 | tf_op jit(solution)/shard_map/all_to_all | solution.py:785
  123.5 4.4 %last.1 = (f32[8,16,256]{2,1,0:T(8,128)}, f32[8,16,256]{2,1,0:T(8,128)}) custom-call(f32[256,128]{1,0:T(8,128)S(1)} %bitcast.35, f32[14,128,384]{2,1,0:T(8,128)S(1)} %get-tuple-element.28.right_ref, f32[14,256,128]{2,1,0:T(8,128)S(1)} %get-tuple-element.29.left_ref, f32[256,256]{1,0:T(8,128)S(1)} %get-tuple-element.30.last_ref, ...), custom_call_target="tpu_custom_call" | custom-call | tf_op jit(solution)/shard_map/last/pallas_call | solution.py:863
  (5 shorter events, 0.1 us)
Async XLA Ops:
  0.6 15.0 %copy-start = (f32[16,128]{1,0:T(8,128)S(1)}, f32[16,128]{1,0:T(8,128)}, u32[]{:S(2)}) copy-start(f32[16,128]{1,0:T(8,128)} %constant.27.clone.table_ref) | copy-start | bytes 24580
  2.6 8.2 %collective-permute-start.1 = (f32[4,8,4,256]{3,2,1,0:T(4,128)S(1)}, f32[4,8,4,256]{3,2,1,0:T(4,128)S(1)}, u32[]{:S(2)}, u32[]{:S(2)}) collective-permute-start(f32[4,8,4,256]{3,2,1,0:T(4,128)S(1)} %pad_maximum_fusion.2), channel_id=1, source_target_pairs={{0,1},{1,2},{2,3},{3,4},{4,5},{5,6},{6,7},{7,8},{8,9},{9,10},{10,1... | collective-permute-start | bytes 393224 | tf_op jit(solution)/shard_map/ppermute | solution.py:798
  4.8 6.0 %collective-permute-start = (f32[4,8,4,256]{3,2,1,0:T(4,128)S(1)}, f32[4,8,4,256]{3,2,1,0:T(4,128)S(1)}, u32[]{:S(2)}, u32[]{:S(2)}) collective-permute-start(f32[4,8,4,256]{3,2,1,0:T(4,128)S(1)} %pad_maximum_fusion.1), channel_id=1, source_target_pairs={{1,0},{2,1},{3,2},{4,3},{5,4},{6,5},{7,6},{8,7},{9,8},{10,9},{11,1... | collective-permute-start | bytes 393224 | tf_op jit(solution)/shard_map/ppermute | solution.py:799
  11.9 8.0 %collective-permute-start.3 = (f32[4,3,24,256]{3,2,1,0:T(8,128)S(1)}, f32[4,3,24,256]{3,2,1,0:T(8,128)S(1)}, u32[]{:S(2)}, u32[]{:S(2)}) collective-permute-start(f32[4,3,24,256]{3,2,1,0:T(8,128)S(1)} %get-tuple-element.38), channel_id=1, source_target_pairs={{16,0},{32,16},{48,32},{64,48},{80,64},{96,80},{112,96},{128,112},... | collective-permute-start | bytes 884744 | tf_op jit(solution)/shard_map/ppermute | solution.py:802
  15.3 4.6 %collective-permute-start.2 = (f32[4,3,24,256]{3,2,1,0:T(8,128)S(1)}, f32[4,3,24,256]{3,2,1,0:T(8,128)S(1)}, u32[]{:S(2)}, u32[]{:S(2)}) collective-permute-start(f32[4,3,24,256]{3,2,1,0:T(8,128)S(1)} %get-tuple-element.39), channel_id=1, source_target_pairs={{0,16},{16,32},{32,48},{48,64},{64,80},{80,96},{96,112},{112,128},... | collective-permute-start | bytes 884744 | tf_op jit(solution)/shard_map/ppermute | solution.py:801
  19.7 36.3 %copy-start.1 = (f32[9]{0:T(128)S(1)}, f32[9]{0:T(128)}, u32[]{:S(2)}) copy-start(f32[9]{0:T(128)} %constant.28.clone.scale_ref) | copy-start | bytes 112
